TPU v7x, 512 devices: a whole 4x8x8 slice. The times are simulated.
512 devices in a mesh: ctx: 32 (over x, y), head: 16 (over z, core).
Axes of the slice: x: 4, y: 8, z: 8, core: 2. Of those that a mesh axis runs over, the one named last changes fastest.
Arguments:
- queries: bfloat16 [8192, 4096], P('ctx', 'head'), may hold values from -6 to 6
- keys_values: bfloat16 [8192, 1024], P('ctx'), may hold values from -6 to 6
- grad_rows: bfloat16 [8192, 2880], P('ctx', 'head'), may hold values from -6 to 6
- doc_ids: int32 [8192], replicated, may hold values from 0 to 7, never falling along the last dimension, each value on 1 to 2048 neighbouring positions
- tile_list: int32 [64], replicated, may hold values from 0 to 63, each once
Outputs:
- attended: float32 [8192, 4096], P('ctx', 'head')
- weight_grad: float32 [2880, 4096], P('ctx', 'head')
Inputs may be any that keep to these rules, and one draw needn't show every extreme that they name: `tile_list`: every slot index names a different tile. `doc_ids`: never falling along the window; each document holds 1 to 2048 positions.
All inputs are finite; a program needn't handle non-finite values.
Results may differ from a plain program's by a relative error of at most 0.0018.
Values may be sent and summed in bfloat16 or wider, within the bound.
No kernel may reach another device: no remote copies, remote signals or barrier semaphores. Data moves between devices by JAX's collectives and lax.ppermute only.
A program may use at most 128 MiB of HBM per device.

v0:
```python
import jax
import jax.numpy as jnp
from jax import lax
from jax.sharding import PartitionSpec as P

H = 64
KVH = 8
DH = 64
TILE = 128


NEG_FILL = -1e30


def on_device(queries, keys_values, grad_rows, doc_ids, tile_list):
    tokens_local = queries.shape[0]
    heads_local = queries.shape[1] // DH
    group = H // KVH
    kv_local = max(1, heads_local // group)
    per_kv = heads_local // kv_local
    scale = DH ** (-0.5)
    head_index = lax.axis_index("head")
    kv_start = head_index * heads_local // group
    own_kv = lax.dynamic_slice_in_dim(keys_values, kv_start * 2 * DH, kv_local * 2 * DH, 1)
    tile_count = tile_list.shape[0]
    offsets = jnp.arange(TILE, dtype=jnp.int32)
    slot_pos = (tile_list[:, None] * TILE + offsets[None, :]).reshape(-1)
    slot_doc = doc_ids.reshape(tile_count, TILE)[tile_list].reshape(-1)
    row_start = lax.axis_index("ctx") * tokens_local
    query_pos = lax.dynamic_slice_in_dim(slot_pos, row_start, tokens_local)
    query_doc = lax.dynamic_slice_in_dim(slot_doc, row_start, tokens_local)
    grouped = queries.reshape(tokens_local, kv_local, per_kv, DH)
    piece = lax.all_gather(own_kv, "ctx", axis=0, tiled=True)
    count = piece.shape[0]
    allowed = (query_doc[:, None] == slot_doc[None, :]) & (slot_pos[None, :] <= query_pos[:, None])
    run_max = jnp.full((kv_local, per_kv, tokens_local), NEG_FILL, jnp.float32)
    parts = piece.reshape(count, kv_local, 2, DH)
    keys = parts[:, :, 0]
    values = parts[:, :, 1]
    scores = jnp.einsum("tgqd,ngd->gqtn", grouped, keys, preferred_element_type=jnp.float32) * scale
    masked = jnp.where(allowed, scores, NEG_FILL)
    new_max = jnp.maximum(run_max, jnp.max(masked, axis=-1))
    weights = jnp.where(allowed, jnp.exp(masked - new_max[..., None]), 0.0)
    new_sum = jnp.sum(weights, axis=-1)
    added = jnp.einsum(
        "gqtn,ngd->gqtd", weights.astype(jnp.bfloat16), values, preferred_element_type=jnp.float32
    )
    normed = added / new_sum[..., None]
    attended = jnp.transpose(normed, (2, 0, 1, 3)).reshape(tokens_local, heads_local * DH)
    term = lax.dot_general(
        lax.all_gather(grad_rows, "head", axis=1, tiled=True).astype(jnp.float32),
        attended,
        (((0,), (0,)), ((), ())),
        precision=lax.Precision.HIGHEST,
        preferred_element_type=jnp.float32,
    )
    summed = lax.psum(term, "ctx")
    share = summed.shape[0] // lax.axis_size("ctx")
    weight_grad = lax.dynamic_slice_in_dim(summed, lax.axis_index("ctx") * share, share, 0)
    return (attended, weight_grad)


def solution(mesh):
    in_specs = (P("ctx", "head"), P("ctx", None), P("ctx", "head"), P(), P())
    out_specs = (P("ctx", "head"), P("ctx", "head"))
    return jax.shard_map(
        on_device, mesh=mesh, in_specs=in_specs, out_specs=out_specs, check_vma=False
    )
```

profile of v0, /device:TPU:16, one launch (start us, length us, event | category | flops | bytes accessed | tf_op | source)
XLA Modules:
  0.0 366.6 jit_solution(1659560030699857460)
XLA Ops:
  7.2 0.0 copy-start
  7.2 0.0 all-gather.6.cloned.1.call-start
  7.2 0.7 all-gather.6.cloned.1.call-update
  7.9 0.0 all-gather.4.cloned.1.call-start
  8.0 0.2 copy-done
  8.2 0.6 constant_dynamic-slice_fusion.1
  8.9 0.0 all-gather.4.cloned.1.call-update
  8.9 0.0 all-reduce.2.cloned.1.call-start
  8.9 0.7 compare_select_fusion
  9.6 1.4 gather_fusion
  11.0 0.1 dynamic_slice.12
  11.0 0.1 add_bitcast_fusion
  11.1 0.1 dynamic_slice.13
  11.2 1.0 copy.16
  12.2 5.7 %compare_and_fusion = pred[256,8192]{0,1:T(8,128)(4,1)S(1)} fusion(s32[256]{0:T(256)S(1)} %dynamic_slice.13, s32[256]{0:T(256)S(1)} %dynamic_slice.12, s32[8192]{0:T(1024)S(1)} %add_bitcast_fusion, s32[8192]{0:T(1024)S(1)} %bitcast.59), kind=kLoop, calls=%fused_computation.9 | loop fusion | flops 6291456 | bytes 2164736 | tf_op jit(solution)/shard_map/and | solution.py:35
  17.9 39.0 %all-gather.6.cloned.1.call-done = bf16[16,180,256]{2,1,0:T(8,128)(2,1)} async-done(((bf16[1,180,256]{2,1,0:T(8,128)(2,1)}), bf16[16,180,256]{2,1,0:T(8,128)(2,1)}) %all-gather.6.cloned.1.call-update) | async-done | bytes 1474576 | tf_op jit(solution)/shard_map/all_gather | solution.py:51
  56.9 3.3 reshape.91
  60.2 81.3 %all-gather.4.cloned.1.call-done = bf16[8192,128]{1,0:T(8,128)(2,1)} async-done(((bf16[256,128]{1,0:T(8,128)(2,1)}), bf16[8192,128]{1,0:T(8,128)(2,1)}) %all-gather.4.cloned.1.call-update) | async-done | bytes 2097168 | tf_op jit(solution)/shard_map/all_gather | solution.py:33
  141.4 4.1 %copy.15 = bf16[8192,128]{0,1:T(8,128)(2,1)} copy(bf16[8192,128]{1,0:T(8,128)(2,1)} %all-gather.4.cloned.1.call-done) | data formatting | bytes 4194304 | tf_op jit(solution)/shard_map/all_gather | solution.py:33
  145.5 14.5 %fusion = (f32[4,256]{1,0:T(4,128)S(1)}, f32[8192,256,4]{1,0,2:T(8,128)}) fusion(pred[256,8192]{0,1:T(8,128)(4,1)S(1)} %compare_and_fusion, bf16[256,4,64]{0,2,1:T(8,128)(2,1)S(1)} %bitcast.60, bf16[8192,1,2,64]{0,3,2,1:T(8,128)(2,1)} %bitcast.54), kind=kOutput, calls=%fused_computation.3 | convolution fusion | flops 1098906624 | bytes 36835328 | tf_op jit(solution)/shard_map/tgqd,ngd->gqtn/dot_general | solution.py:40
  160.0 15.0 %fusion.1 = f32[4,256]{1,0:T(4,128)S(1)} fusion(f32[8192,256,4]{1,0,2:T(8,128)} %get-tuple-element.11, f32[4,256]{1,0:T(4,128)S(1)} %broadcast_maximum_fusion, pred[256,8192]{0,1:T(8,128)(4,1)S(1)} %compare_and_fusion), kind=kLoop, calls=%fused_computation.4 | loop fusion | flops 41942016 | bytes 35659776 | tf_op jit(solution)/shard_map/reduce_sum | solution.py:44
  175.0 0.0 copy-start.1
  175.0 14.5 %fusion.7 = f32[4,256,64]{1,2,0:T(8,128)S(1)} fusion(f32[8192,256,4]{1,0,2:T(8,128)} %get-tuple-element.11, f32[4,256]{1,0:T(4,128)S(1)} %broadcast_maximum_fusion, pred[256,8192]{0,1:T(8,128)(4,1)S(1)} %compare_and_fusion, bf16[8192,1,2,64]{0,3,2,1:T(8,128)(2,1)} %bitcast.55, f32[4,256]{1,0:T(4,128)S(1)} %fusion.1), kind=kOutput, calls=%fused_computation.11 | convolution fusion | flops 1115750400 | bytes 36970496 | tf_op jit(solution)/shard_map/gqtn,ngd->gqtd/dot_general | solution.py:45
  189.5 0.0 copy-done.1
  189.5 3.0 convolution_bitcast_fusion
  192.5 0.0 all-reduce.2.cloned.1.call-update
  192.6 0.8 copy.18
  193.4 165.1 %all-reduce.2.cloned.1.call-done = f32[2880,256]{1,0:T(8,128)} async-done(((f32[2880,256]{1,0:T(8,128)}), f32[2880,256]{1,0:T(8,128)}) %all-reduce.2.cloned.1.call-update) | async-done | bytes 2949136 | tf_op jit(solution)/shard_map/psum | solution.py:57
  358.5 1.5 constant_dynamic-slice_fusion
  (2 shorter events, 0.0 us)
Async XLA Ops:
  7.2 1.0 copy-start
  7.2 49.7 %all-gather.6.cloned.1.call-start = ((), (), s32[]{:S(2)}) async-start(), calls=%async_computation.2 | async-start | bytes 1601536 | tf_op jit(solution)/shard_map/all_gather | solution.py:51
  7.9 133.5 %all-gather.4.cloned.1.call-start = ((), (), s32[]{:S(2)}) async-start(), calls=%async_computation | async-start | bytes 2162688 | tf_op jit(solution)/shard_map/all_gather | solution.py:33
  8.9 349.6 %all-reduce.2.cloned.1.call-start = ((), (), s32[]{:S(2)}) async-start(), calls=%async_computation.1 | async-start | bytes 5898240 | tf_op jit(solution)/shard_map/psum | solution.py:57
  175.0 14.5 %copy-start.1 = (bf16[2880,256]{1,0:T(8,128)(2,1)S(1)}, bf16[2880,256]{1,0:T(8,128)(2,1)}, u32[]{:S(2)}) copy-start(bf16[2880,256]{1,0:T(8,128)(2,1)} %reshape.91) | copy-start | bytes 4423684
Sparse Core Ops, SparseCore 0:
  10.1 46.7 all-gather.5
  60.6 80.7 all-gather.3
  192.7 165.7 all-reduce.1
where the time goes:
time: 367 us
  waiting for transfers between devices  286 us (78%)
  matrix products  32 us (9%)
  other arithmetic  21.4 us (6%)
  between operations  13.8 us (4%)
  local copies, waits for them, and re-layouts  13.2 us (4%)
    psum x1, waiting for transfers between devices, on_device(): summed = lax.psum(term, 'ctx')  165 us
    all_gather x1, waiting for transfers between devices, on_device(): piece = lax.all_gather(own_kv, 'ctx', axis=0, tiled=True)  81.3 us
    all_gather x1, waiting for transfers between devices, on_device(): lax.all_gather(grad_rows, 'head', axis=1, tiled=True).astype(jnp.float32)  39 us
    reduce_sum x1, other arithmetic, on_device(): new_sum = jnp.sum(weights, axis=-1)  15 us
    dot_general x1, matrix products, on_device(): jnp.einsum('gqtn,ngd->gqtd', weights.astype(jnp.bfloat16), values, prefer...  14.5 us
    dot_general x1, matrix products, on_device(): jnp.einsum('tgqd,ngd->gqtn', grouped, keys, preferred_element_type=jnp.fl...  14.5 us
  transfers between devices with their start and end apart: 3, of which 3 were waited for; matrix products, arithmetic and copies ran while one was open for 4% of the time, Pallas kernels for 0%

commit v1 on v0

v1 whole, which is shorter than its diff:
```python
import jax
import jax.numpy as jnp
from jax import lax
from jax.experimental import pallas as pl
from jax.experimental.pallas import tpu as pltpu
from jax.sharding import Mesh, PartitionSpec as P

H = 64
KVH = 8
DH = 64
TILE = 128
DOCS = 8
HEADS = 4
SPAN = 18
BLOCK = 90
PADDED = 96
NEG_FILL = -1e30


def attention_kernel(core_ref, tiles_ref, docs_ref, q_ref, own_ref, other_ref, out_ref, slot_ref, s_ref):
    count = tiles_ref.shape[0]
    tokens = docs_ref.shape[0]
    core = core_ref[0]
    first_slot = core_ref[1]
    width = HEADS * TILE

    def invert(slot, carry):
        slot_ref[tiles_ref[slot]] = slot
        return carry

    lax.fori_loop(0, count, invert, 0)

    def bisect(step, lows):
        size = lax.shift_right_logical(tokens, step + 1)
        return tuple(
            jnp.where(docs_ref[low + size - 1] < doc + 1, low + size, low) for doc, low in enumerate(lows)
        )

    steps = tokens.bit_length() - 1
    bounds = lax.fori_loop(0, steps, bisect, (jnp.int32(0),) * (DOCS - 1))
    bounds = tuple(
        jnp.where(docs_ref[jnp.minimum(low, tokens - 1)] < doc + 1, low + 1, low) for doc, low in enumerate(bounds)
    )

    lane = lax.broadcasted_iota(jnp.int32, (1, TILE), 1)
    sub = lax.broadcasted_iota(jnp.int32, (2 * TILE, TILE), 0)

    def pick(tile):
        slot = slot_ref[tile]
        at = lax.shift_right_logical(slot, 1)
        return jnp.where((slot & 1) == core, own_ref[at], other_ref[at])

    for part in range(2):
        tile = tiles_ref[first_slot + part]
        base = tile * TILE
        begin = jnp.int32(0)
        row_pos = base + lane
        row_begin = jnp.zeros((1, TILE), jnp.int32)
        for bound in bounds:
            begin = jnp.where(bound <= base, jnp.maximum(begin, bound), begin)
            row_begin = jnp.where(bound <= row_pos, jnp.maximum(row_begin, bound), row_begin)
        low = lax.div(begin, TILE)
        pairs = lax.div(tile - low + 2, 2)

        q = q_ref[part * TILE:(part + 1) * TILE, :]
        q_t = jnp.transpose(q.astype(jnp.float32) * (DH ** -0.5)).astype(jnp.bfloat16)
        q_t = jnp.concatenate([q_t[h * DH:(h + 1) * DH] for h in range(HEADS)], axis=1)
        q_t = jnp.concatenate([q_t, jnp.zeros_like(q_t)], axis=0)

        def score(pair, top):
            at = low + 2 * pair
            kv = jnp.concatenate([pick(at), pick(jnp.minimum(at + 1, tile))], axis=0)
            scores = jnp.dot(kv, q_t, preferred_element_type=jnp.float32)
            key_pos = at * TILE + sub
            allowed = (key_pos >= row_begin) & (key_pos <= row_pos)
            start = pl.multiple_of(pair * (2 * TILE), 2 * TILE)
            tops = []
            for h in range(HEADS):
                masked = jnp.where(allowed, scores[:, h * TILE:(h + 1) * TILE], NEG_FILL)
                s_ref[pl.ds(start, 2 * TILE), h * TILE:(h + 1) * TILE] = masked
                tops.append(jnp.max(masked.reshape(2 * TILE // 8, 8, TILE), axis=0))
            return jnp.maximum(top, jnp.concatenate(tops, axis=1))

        top = lax.fori_loop(0, pairs, score, jnp.full((8, width), NEG_FILL, jnp.float32))
        top = jnp.max(top, axis=0, keepdims=True)

        def add(pair, carry):
            total, summed = carry
            at = low + 2 * pair
            kv = jnp.concatenate([pick(at), pick(jnp.minimum(at + 1, tile))], axis=0)
            start = pl.multiple_of(pair * (2 * TILE), 2 * TILE)
            weights = jnp.exp(s_ref[pl.ds(start, 2 * TILE), :] - top)
            total = total + jnp.sum(weights.reshape(2 * TILE // 8, 8, width), axis=0)
            summed = summed + lax.dot_general(
                kv, weights.astype(jnp.bfloat16), (((0,), (0,)), ((), ())), preferred_element_type=jnp.float32
            )
            return total, summed

        total, summed = lax.fori_loop(
            0, pairs, add, (jnp.zeros((8, width), jnp.float32), jnp.zeros((2 * DH, width), jnp.float32))
        )
        total = jnp.sum(total, axis=0, keepdims=True)
        normed = summed[DH:] / total
        for h in range(0, HEADS, 2):
            both = jnp.concatenate(
                [normed[:, h * TILE:(h + 1) * TILE], normed[:, (h + 1) * TILE:(h + 2) * TILE]], axis=0
            )
            out_ref[part * TILE:(part + 1) * TILE, h * DH:(h + 2) * DH] = jnp.transpose(both)


def attention(core, tiles, docs, queries, own, other):
    smem = pl.BlockSpec(memory_space=pltpu.SMEM)
    vmem = pl.BlockSpec(memory_space=pltpu.VMEM)
    return pl.pallas_call(
        attention_kernel,
        out_shape=jax.ShapeDtypeStruct(queries.shape, jnp.float32),
        in_specs=[smem, smem, smem, vmem, vmem, vmem],
        out_specs=vmem,
        scratch_shapes=[
            pltpu.SMEM((tiles.shape[0],), jnp.int32),
            pltpu.VMEM((SPAN * TILE, HEADS * TILE), jnp.float32),
        ],
        cost_estimate=pl.CostEstimate(flops=1_200_000_000, bytes_accessed=4_000_000, transcendentals=2_200_000),
        compiler_params=pltpu.CompilerParams(vmem_limit_bytes=32 << 20),
    )(core, tiles, docs, queries, own, other)


def term_kernel(g_ref, a_ref, out_ref):
    a = a_ref[...]
    high = a.astype(jnp.bfloat16)
    low = (a - high.astype(jnp.float32)).astype(jnp.bfloat16)

    def step(i, carry):
        rows = pl.ds(pl.multiple_of(i * (4 * PADDED), 4 * PADDED), 4 * PADDED)
        g = g_ref[rows, :]
        term = jnp.dot(g, high, preferred_element_type=jnp.float32)
        term = term + jnp.dot(g, low, preferred_element_type=jnp.float32)
        out_ref[rows, :] = term.astype(out_ref.dtype)
        return carry

    lax.fori_loop(0, g_ref.shape[0] // (4 * PADDED), step, 0)


def term_of(grads, attended):
    vmem = pl.BlockSpec(memory_space=pltpu.VMEM)
    return pl.pallas_call(
        term_kernel,
        out_shape=jax.ShapeDtypeStruct((grads.shape[0], attended.shape[1]), jnp.bfloat16),
        in_specs=[vmem, vmem],
        out_specs=vmem,
        cost_estimate=pl.CostEstimate(flops=800_000_000, bytes_accessed=4_000_000, transcendentals=0),
        compiler_params=pltpu.CompilerParams(vmem_limit_bytes=32 << 20),
    )(grads, attended)


def everyone(x, axes, size):
    return lax.all_to_all(jnp.broadcast_to(x[None], (size,) + x.shape), axes, 0, 0)


def on_device(queries, keys_values, grad_rows, doc_ids, tile_list):
    nx, ny, nz, nc = (lax.axis_size(a) for a in ("x", "y", "z", "core"))
    core = lax.axis_index("core")
    ctx = lax.axis_index("x") * ny + lax.axis_index("y")
    tokens = queries.shape[0]

    mine = lax.dynamic_slice(keys_values, (core * TILE, lax.axis_index("z") * (2 * DH)), (TILE, 2 * DH))
    grads = jnp.pad(jnp.transpose(grad_rows).reshape(2, BLOCK, tokens), ((0, 0), (0, PADDED - BLOCK), (0, 0)))
    grads = everyone(grads, ("z", "core"), nz * nc).reshape(nz * nc * 2 * PADDED, tokens)

    own = everyone(mine, "y", ny)
    own = everyone(own, "x", nx).reshape(nx * ny, TILE, 2 * DH)
    other = lax.ppermute(own, "core", [(0, 1), (1, 0)])

    attended = attention(jnp.stack([core, 2 * ctx]), tile_list, doc_ids, queries, own, other)
    term = term_of(grads, attended).reshape(nx * ny, PADDED, attended.shape[1])
    parts = lax.all_to_all(term, ("x", "y"), 0, 0)
    weight_grad = jnp.sum(parts.astype(jnp.float32), axis=0)[:BLOCK]
    return attended, weight_grad


def solution(mesh):
    fine = Mesh(mesh.devices.reshape(4, 8, 8, 2), ("x", "y", "z", "core"))
    ctx, head = ("x", "y"), ("z", "core")
    in_specs = (P(ctx, head), P(ctx, None), P(ctx, head), P(), P())
    out_specs = (P(ctx, head), P(ctx, head))
    return jax.shard_map(on_device, mesh=fine, in_specs=in_specs, out_specs=out_specs, check_vma=False)
```

time: 367 us -> 139 us (0.38)
  the two profiles are of different devices: /device:TPU:16 before, /device:TPU:8 now
where the time goes in v1:
time: 139 us; the launch traced here: 138 us
  blocking collectives  64.9 us (47%)
  waiting for transfers between devices  40.2 us (29%)
  starting transfers between devices  17.2 us (12%)
  Pallas kernels  9.86 us (7%)
  local copies, waits for them, and re-layouts  4.33 us (3%)
    all_to_all x1, blocking collectives, on_device(): parts = lax.all_to_all(term, ('x', 'y'), 0, 0)  47.1 us
    all_to_all x2, waiting for transfers between devices, everyone(): lax.all_to_all(jnp.broadcast_to(x[None], (size,) + x.shape), axes, 0, 0)  37.9 us
    all_to_all x1, blocking collectives, everyone(): lax.all_to_all(jnp.broadcast_to(x[None], (size,) + x.shape), axes, 0, 0)  17.8 us
    all_to_all x2, starting transfers between devices, everyone(): lax.all_to_all(jnp.broadcast_to(x[None], (size,) + x.shape), axes, 0, 0)  14.9 us
    pallas_call x1, Pallas kernels, attention(): pl.pallas_call(attention_kernel, out_shape=jax.ShapeDtypeStruct(queries.s...  7.74 us
  transfers between devices with their start and end apart: 3, of which 3 were waited for; matrix products, arithmetic and copies ran while one was open for 0% of the time, Pallas kernels for 6%

profile of v1, /device:TPU:8, one launch (start us, length us, event | category | flops | bytes accessed | tf_op | source)
XLA Modules:
  0.0 138.1 jit_solution(8641942897936624007)
XLA Ops:
  0.6 0.8 dynamic_slice.3
  1.4 17.8 %all_to_all.20 = bf16[8,128,128]{2,1,0:T(8,128)(2,1)S(1)} all-to-all(bf16[8,128,128]{2,1,0:T(8,128)(2,1)S(1)} %broadcast_in_dim.6), channel_id=1, replica_groups=mesh['x'=4,'y'=8,'z'=8,'core'=2] {'y'}, dimensions={0} | all-to-all | bytes 524288 | tf_op jit(solution)/shard_map/all_to_all | solution.py:157
  19.2 0.0 copy-start.4
  19.2 1.2 broadcast_in_dim.7
  20.4 4.3 %all-to-all-start.1 = ((bf16[4,8,128,128]{3,2,1,0:T(8,128)(2,1)}), bf16[4,8,128,128]{3,2,1,0:T(8,128)(2,1)S(1)}, u32[]{:S(2)}, u32[]{:S(2)}) async-start(bf16[4,8,128,128]{3,2,1,0:T(8,128)(2,1)} %broadcast_in_dim.7), calls=%async_computation.1 | async-start | bytes 2097152 | tf_op jit(solution)/shard_map/all_to_all | solution.py:157
  24.7 0.0 copy-done.4
  24.8 12.5 %all-to-all-done.1 = bf16[4,8,128,128]{3,2,1,0:T(8,128)(2,1)S(1)} async-done(((bf16[4,8,128,128]{3,2,1,0:T(8,128)(2,1)}), bf16[4,8,128,128]{3,2,1,0:T(8,128)(2,1)S(1)}, u32[]{:S(2)}, u32[]{:S(2)}) %all-to-all-start.1) | async-done | bytes 1048608 | tf_op jit(solution)/shard_map/all_to_all | solution.py:157
  37.3 1.3 broadcast_in_dim.8
  38.6 0.0 copy-start.1
  38.6 0.0 copy-start.2
  38.6 0.0 copy-start.3
  38.6 10.6 %all-to-all-start.2 = ((bf16[16,2,96,256]{3,2,1,0:T(8,128)(2,1)}), bf16[16,2,96,256]{3,2,1,0:T(8,128)(2,1)S(1)}, u32[]{:S(2)}, u32[]{:S(2)}) async-start(bf16[16,2,96,256]{3,2,1,0:T(8,128)(2,1)} %broadcast_in_dim.8), calls=%async_computation.2 | async-start | bytes 3145728 | tf_op jit(solution)/shard_map/all_to_all | solution.py:157
  49.2 2.3 %collective-permute-start = (bf16[32,128,128]{2,1,0:T(8,128)(2,1)S(1)}, bf16[32,128,128]{2,1,0:T(8,128)(2,1)}, u32[]{:S(2)}, u32[]{:S(2)}) collective-permute-start(bf16[32,128,128]{2,1,0:T(8,128)(2,1)S(1)} %bitcast.9), channel_id=1, source_target_pairs={{0,1},{1,0},{2,3},{3,2},{4,5},{5,4},{6,7},{7,6},{8,9},{9,8},{10,11... | collective-permute-start | bytes 3145736 | tf_op jit(solution)/shard_map/ppermute | solution.py:172
  51.5 0.1 pad_add_fusion.core_ref
  51.6 2.3 %collective-permute-done.other_ref = bf16[32,128,128]{2,1,0:T(8,128)(2,1)} collective-permute-done((bf16[32,128,128]{2,1,0:T(8,128)(2,1)S(1)}, bf16[32,128,128]{2,1,0:T(8,128)(2,1)}, u32[]{:S(2)}, u32[]{:S(2)}) %collective-permute-start) | collective-permute-done | bytes 1048608 | tf_op jit(solution)/shard_map/ppermute | solution.py:172
  53.9 0.0 copy-done.1
  53.9 0.0 copy-done.2
  53.9 0.0 copy-done.3
  53.9 7.7 %shard_map.68.a_ref = f32[256,256]{1,0:T(8,128)} custom-call(s32[2]{0:T(128)S(1)} %pad_add_fusion.core_ref, s32[64]{0:T(128)S(1)} %copy-done.3, s32[8192]{0:T(1024)S(1)} %copy-done.2, bf16[256,256]{1,0:T(8,128)(2,1)S(1)} %copy-done.1, bf16[32,128,128]{2,1,0:T(8,128)(2,1)S(1)} %bitcast.10, bf16[32,128,128]{2,1,0:T(8,128)(2,1)} %collective-permute-done.other_ref), custom_call_target="tpu_custom_call" | custom-call | flops 1200000000 | bytes 4000000 | tf_op jit(solution)/shard_map/pallas_call | solution.py:114
  61.6 25.4 %all-to-all-done.2 = bf16[16,2,96,256]{3,2,1,0:T(8,128)(2,1)S(1)} async-done(((bf16[16,2,96,256]{3,2,1,0:T(8,128)(2,1)}), bf16[16,2,96,256]{3,2,1,0:T(8,128)(2,1)S(1)}, u32[]{:S(2)}, u32[]{:S(2)}) %all-to-all-start.2) | async-done | bytes 1572896 | tf_op jit(solution)/shard_map/all_to_all | solution.py:157
  87.0 0.0 copy-start
  87.0 0.9 copy-done
  88.0 2.1 %shard_map.69 = bf16[3072,256]{1,0:T(8,128)(2,1)S(1)} custom-call(bf16[3072,256]{1,0:T(8,128)(2,1)S(1)} %bitcast.7, f32[256,256]{1,0:T(8,128)S(1)} %copy-done), custom_call_target="tpu_custom_call" | custom-call | flops 800000000 | bytes 4000000 | tf_op jit(solution)/shard_map/pallas_call | solution.py:146
  90.1 47.1 %all_to_all.21 = bf16[32,96,256]{2,1,0:T(8,128)(2,1)S(1)} all-to-all(bf16[32,96,256]{2,1,0:T(8,128)(2,1)S(1)} %bitcast.8), channel_id=1, replica_groups=mesh['x'=4,'y'=8,'z'=8,'core'=2] {'x','y'}, dimensions={0} | all-to-all | bytes 3145728 | tf_op jit(solution)/shard_map/all_to_all | solution.py:176
  137.2 0.9 convert_reduce_fusion
  (3 shorter events, 0.1 us)
Async XLA Ops:
  19.2 5.5 %copy-start.4 = (bf16[256,180]{0,1:T(8,128)(2,1)S(1)}, bf16[256,180]{0,1:T(8,128)(2,1)}, u32[]{:S(2)}) copy-start(bf16[256,180]{0,1:T(8,128)(2,1)} %param.7) | copy-start | bytes 276484
  20.4 16.9 %all-to-all-start.1 = ((bf16[4,8,128,128]{3,2,1,0:T(8,128)(2,1)}), bf16[4,8,128,128]{3,2,1,0:T(8,128)(2,1)S(1)}, u32[]{:S(2)}, u32[]{:S(2)}) async-start(bf16[4,8,128,128]{3,2,1,0:T(8,128)(2,1)} %broadcast_in_dim.7), calls=%async_computation.1 | async-start | bytes 2097152 | tf_op jit(solution)/shard_map/all_to_all | solution.py:157
  38.6 15.3 %copy-start.1 = (bf16[256,256]{1,0:T(8,128)(2,1)S(1)}, bf16[256,256]{1,0:T(8,128)(2,1)}, u32[]{:S(2)}) copy-start(bf16[256,256]{1,0:T(8,128)(2,1)} %q_ref.1) | copy-start | bytes 393220
  38.6 15.3 %copy-start.2 = (s32[8192]{0:T(1024)S(1)}, s32[8192]{0:T(1024)}, u32[]{:S(2)}) copy-start(s32[8192]{0:T(1024)} %docs_ref.1) | copy-start | bytes 98308
  38.6 15.3 %copy-start.3 = (s32[64]{0:T(128)S(1)}, s32[64]{0:T(128)}, u32[]{:S(2)}) copy-start(s32[64]{0:T(128)} %tiles_ref.1) | copy-start | bytes 772
  38.6 48.4 %all-to-all-start.2 = ((bf16[16,2,96,256]{3,2,1,0:T(8,128)(2,1)}), bf16[16,2,96,256]{3,2,1,0:T(8,128)(2,1)S(1)}, u32[]{:S(2)}, u32[]{:S(2)}) async-start(bf16[16,2,96,256]{3,2,1,0:T(8,128)(2,1)} %broadcast_in_dim.8), calls=%async_computation.2 | async-start | bytes 3145728 | tf_op jit(solution)/shard_map/all_to_all | solution.py:157
  49.2 4.7 %collective-permute-start = (bf16[32,128,128]{2,1,0:T(8,128)(2,1)S(1)}, bf16[32,128,128]{2,1,0:T(8,128)(2,1)}, u32[]{:S(2)}, u32[]{:S(2)}) collective-permute-start(bf16[32,128,128]{2,1,0:T(8,128)(2,1)S(1)} %bitcast.9), channel_id=1, source_target_pairs={{0,1},{1,0},{2,3},{3,2},{4,5},{5,4},{6,7},{7,6},{8,9},{9,8},{10,11... | collective-permute-start | bytes 3145736 | tf_op jit(solution)/shard_map/ppermute | solution.py:172
  87.0 1.0 copy-start

commit v2 on v1

--- a/solution.py
+++ b/solution.py
@@ -5,8 +5,7 @@
 from jax.experimental.pallas import tpu as pltpu
 from jax.sharding import Mesh, PartitionSpec as P
 
-H = 64
-KVH = 8
+
 DH = 64
 TILE = 128
 DOCS = 8
@@ -17,7 +16,7 @@
 NEG_FILL = -1e30
 
 
-def attention_kernel(core_ref, tiles_ref, docs_ref, q_ref, own_ref, other_ref, out_ref, slot_ref, s_ref):
+def attention_kernel(core_ref, tiles_ref, docs_ref, q_ref, own_ref, other_ref, out_ref, send_ref, slot_ref, s_ref):
     count = tiles_ref.shape[0]
     tokens = docs_ref.shape[0]
     core = core_ref[0]
@@ -105,17 +104,23 @@
             both = jnp.concatenate(
                 [normed[:, h * TILE:(h + 1) * TILE], normed[:, (h + 1) * TILE:(h + 2) * TILE]], axis=0
             )
-            out_ref[part * TILE:(part + 1) * TILE, h * DH:(h + 2) * DH] = jnp.transpose(both)
-
-
-def attention(core, tiles, docs, queries, own, other):
+            both = jnp.transpose(both)
+            out_ref[part * TILE:(part + 1) * TILE, h * DH:(h + 2) * DH] = both
+            for peer in range(send_ref.shape[0]):
+                send_ref[peer, part * TILE:(part + 1) * TILE, h * DH:(h + 2) * DH] = both.astype(send_ref.dtype)
+
+
+def attention(core, tiles, docs, queries, own, other, peers):
     smem = pl.BlockSpec(memory_space=pltpu.SMEM)
     vmem = pl.BlockSpec(memory_space=pltpu.VMEM)
     return pl.pallas_call(
         attention_kernel,
-        out_shape=jax.ShapeDtypeStruct(queries.shape, jnp.float32),
+        out_shape=(
+            jax.ShapeDtypeStruct(queries.shape, jnp.float32),
+            jax.ShapeDtypeStruct((peers,) + queries.shape, jnp.bfloat16),
+        ),
         in_specs=[smem, smem, smem, vmem, vmem, vmem],
-        out_specs=vmem,
+        out_specs=(vmem, vmem),
         scratch_shapes=[
             pltpu.SMEM((tiles.shape[0],), jnp.int32),
             pltpu.VMEM((SPAN * TILE, HEADS * TILE), jnp.float32),
@@ -125,32 +130,33 @@
     )(core, tiles, docs, queries, own, other)
 
 
-def term_kernel(g_ref, a_ref, out_ref):
-    a = a_ref[...]
-    high = a.astype(jnp.bfloat16)
-    low = (a - high.astype(jnp.float32)).astype(jnp.bfloat16)
-
-    def step(i, carry):
-        rows = pl.ds(pl.multiple_of(i * (4 * PADDED), 4 * PADDED), 4 * PADDED)
-        g = g_ref[rows, :]
-        term = jnp.dot(g, high, preferred_element_type=jnp.float32)
-        term = term + jnp.dot(g, low, preferred_element_type=jnp.float32)
-        out_ref[rows, :] = term.astype(out_ref.dtype)
-        return carry
-
-    lax.fori_loop(0, g_ref.shape[0] // (4 * PADDED), step, 0)
-
-
-def term_of(grads, attended):
+def term_kernel(place_ref, g_own_ref, g_other_ref, a_ref, own_ref, out_ref):
+    core, x = place_ref[0], place_ref[1]
+    pairs = out_ref.shape[0] // 2
+    a = own_ref[...]
+    low = (a - a.astype(jnp.bfloat16).astype(jnp.float32)).astype(jnp.bfloat16)
+    for pair in range(pairs):
+        for g_ref, side in ((g_own_ref, core), (g_other_ref, 1 - core)):
+            term = jnp.dot(g_ref[pairs * x + pair], low, preferred_element_type=jnp.float32)
+            for peer in range(a_ref.shape[0]):
+                term = term + jnp.dot(
+                    g_ref[pairs * peer + pair], a_ref[peer], preferred_element_type=jnp.float32
+                )
+            out_ref[2 * pair + side] = term
+
+
+def term_of(place, g_own, g_other, gathered, attended):
+    smem = pl.BlockSpec(memory_space=pltpu.SMEM)
     vmem = pl.BlockSpec(memory_space=pltpu.VMEM)
+    blocks = 2 * g_own.shape[0] // gathered.shape[0]
     return pl.pallas_call(
         term_kernel,
-        out_shape=jax.ShapeDtypeStruct((grads.shape[0], attended.shape[1]), jnp.bfloat16),
-        in_specs=[vmem, vmem],
+        out_shape=jax.ShapeDtypeStruct((blocks, g_own.shape[1], attended.shape[1]), jnp.float32),
+        in_specs=[smem, vmem, vmem, vmem, vmem],
         out_specs=vmem,
-        cost_estimate=pl.CostEstimate(flops=800_000_000, bytes_accessed=4_000_000, transcendentals=0),
+        cost_estimate=pl.CostEstimate(flops=500_000_000, bytes_accessed=3_000_000, transcendentals=0),
         compiler_params=pltpu.CompilerParams(vmem_limit_bytes=32 << 20),
-    )(grads, attended)
+    )(place, g_own, g_other, gathered, attended)
 
 
 def everyone(x, axes, size):
@@ -158,23 +164,33 @@
 
 
 def on_device(queries, keys_values, grad_rows, doc_ids, tile_list):
-    nx, ny, nz, nc = (lax.axis_size(a) for a in ("x", "y", "z", "core"))
-    core = lax.axis_index("core")
-    ctx = lax.axis_index("x") * ny + lax.axis_index("y")
+    nx, ny, nz = (lax.axis_size(a) for a in ("x", "y", "z"))
+    core, x = lax.axis_index("core"), lax.axis_index("x")
+    ctx = x * ny + lax.axis_index("y")
     tokens = queries.shape[0]
+    swap = [(0, 1), (1, 0)]
+    half = nz // nx
+
+    grads = jnp.pad(jnp.transpose(grad_rows).reshape(2, BLOCK, tokens), ((0, 0), (0, PADDED - BLOCK), (0, 0)))
+    grads = grads.reshape(2 * PADDED, tokens)
+    turn = [(a * nz + half * b + c, b * nz + half * a + c) for a in range(nx) for b in range(nx) for c in range(half)]
+    grads = lax.ppermute(grads, ("x", "z"), turn)
 
     mine = lax.dynamic_slice(keys_values, (core * TILE, lax.axis_index("z") * (2 * DH)), (TILE, 2 * DH))
-    grads = jnp.pad(jnp.transpose(grad_rows).reshape(2, BLOCK, tokens), ((0, 0), (0, PADDED - BLOCK), (0, 0)))
-    grads = everyone(grads, ("z", "core"), nz * nc).reshape(nz * nc * 2 * PADDED, tokens)
-
     own = everyone(mine, "y", ny)
     own = everyone(own, "x", nx).reshape(nx * ny, TILE, 2 * DH)
-    other = lax.ppermute(own, "core", [(0, 1), (1, 0)])
-
-    attended = attention(jnp.stack([core, 2 * ctx]), tile_list, doc_ids, queries, own, other)
-    term = term_of(grads, attended).reshape(nx * ny, PADDED, attended.shape[1])
-    parts = lax.all_to_all(term, ("x", "y"), 0, 0)
-    weight_grad = jnp.sum(parts.astype(jnp.float32), axis=0)[:BLOCK]
+    other = lax.ppermute(own, "core", swap)
+
+    g_own = everyone(grads, "z", nz)
+    g_other = lax.ppermute(g_own, "core", swap)
+
+    attended, send = attention(
+        jnp.stack([core, 2 * ctx]), tile_list, doc_ids, queries, own, other, nx
+    )
+    gathered = lax.all_to_all(send, "x", 0, 0)
+    term = term_of(jnp.stack([core, x]), g_own, g_other, gathered, attended)
+    parts = lax.all_to_all(term.reshape(ny, PADDED, attended.shape[1]), "y", 0, 0)
+    weight_grad = jnp.sum(parts, axis=0)[:BLOCK]
     return attended, weight_grad
 
 

time: 139 us -> 127 us (0.914)
  the two profiles are of different devices: /device:TPU:8 before, /device:TPU:2 now
where the time goes in v2:
time: 127 us; the launch traced here: 126 us
  blocking collectives  46.3 us (36%)
  starting transfers between devices  33.9 us (27%)
  waiting for transfers between devices  33.5 us (26%)
  Pallas kernels  7.34 us (6%)
  local copies, waits for them, and re-layouts  3.62 us (3%)
    all_to_all x1, blocking collectives, on_device(): lax.all_to_all(term.reshape(ny, PADDED, attended.shape[1]), 'y', 0, 0)  27.6 us
    all_to_all x2, waiting for transfers between devices, everyone(): lax.all_to_all(jnp.broadcast_to(x[None], (size,) + x.shape), axes, 0, 0)  21.7 us
    all_to_all x2, starting transfers between devices, everyone(): lax.all_to_all(jnp.broadcast_to(x[None], (size,) + x.shape), axes, 0, 0)  19.6 us
    all_to_all x1, blocking collectives, everyone(): lax.all_to_all(jnp.broadcast_to(x[None], (size,) + x.shape), axes, 0, 0)  18.8 us
    all_to_all x1, waiting for transfers between devices, on_device(): gathered = lax.all_to_all(send, 'x', 0, 0)  8.89 us
    pallas_call x1, Pallas kernels, attention(): pl.pallas_call(attention_kernel, out_shape=(jax.ShapeDtypeStruct(queries....  6.12 us
    ppermute x1, starting transfers between devices, on_device(): grads = lax.ppermute(grads, ('x', 'z'), turn)  5.53 us
    all_to_all x1, starting transfers between devices, on_device(): gathered = lax.all_to_all(send, 'x', 0, 0)  4.96 us
  transfers between devices with their start and end apart: 6, of which 4 were waited for; matrix products, arithmetic and copies ran while one was open for 0% of the time, Pallas kernels for 5%

profile of v2, /device:TPU:2, one launch (start us, length us, event | category | flops | bytes accessed | tf_op | source)
XLA Modules:
  0.0 126.3 jit_solution(7811019321408600214)
XLA Ops:
  0.6 0.0 dynamic-slice-start
  0.7 0.7 dynamic-slice-done
  1.4 18.8 %all_to_all.25 = bf16[8,128,128]{2,1,0:T(8,128)(2,1)S(1)} all-to-all(bf16[8,128,128]{2,1,0:T(8,128)(2,1)S(1)} %broadcast_in_dim.6), channel_id=1, replica_groups=mesh['x'=4,'y'=8,'z'=8,'core'=2] {'y'}, dimensions={0} | all-to-all | bytes 524288 | tf_op jit(solution)/shard_map/all_to_all | solution.py:163
  20.2 1.2 broadcast_in_dim.7
  21.4 0.0 copy-start.4
  21.4 5.0 %all-to-all-start.1 = ((bf16[4,8,128,128]{3,2,1,0:T(8,128)(2,1)}), bf16[4,8,128,128]{3,2,1,0:T(8,128)(2,1)S(1)}, u32[]{:S(2)}, u32[]{:S(2)}) async-start(bf16[4,8,128,128]{3,2,1,0:T(8,128)(2,1)} %broadcast_in_dim.7), calls=%async_computation.1 | async-start | bytes 2097152 | tf_op jit(solution)/shard_map/all_to_all | solution.py:163
  26.4 0.0 copy-done.4
  26.4 5.5 %collective-permute-start.1 = (bf16[192,256]{1,0:T(8,128)(2,1)S(1)}, bf16[192,256]{1,0:T(8,128)(2,1)S(1)}, u32[]{:S(2)}, u32[]{:S(2)}) collective-permute-start(bf16[192,256]{1,0:T(8,128)(2,1)S(1)} %bitcast.12), channel_id=1, source_target_pairs={{0,0},{2,2},{4,128},{6,130},{8,256},{10,258},{12,384},{14,386},{12... | collective-permute-start | bytes 294920 | tf_op jit(solution)/shard_map/ppermute | solution.py:177
  32.0 2.9 %collective-permute-done.1 = bf16[192,256]{1,0:T(8,128)(2,1)S(1)} collective-permute-done((bf16[192,256]{1,0:T(8,128)(2,1)S(1)}, bf16[192,256]{1,0:T(8,128)(2,1)S(1)}, u32[]{:S(2)}, u32[]{:S(2)}) %collective-permute-start.1) | collective-permute-done | bytes 98336 | tf_op jit(solution)/shard_map/ppermute | solution.py:177
  34.9 3.5 %all-to-all-done.1 = bf16[4,8,128,128]{3,2,1,0:T(8,128)(2,1)S(1)} async-done(((bf16[4,8,128,128]{3,2,1,0:T(8,128)(2,1)}), bf16[4,8,128,128]{3,2,1,0:T(8,128)(2,1)S(1)}, u32[]{:S(2)}, u32[]{:S(2)}) %all-to-all-start.1) | async-done | bytes 1048608 | tf_op jit(solution)/shard_map/all_to_all | solution.py:163
  38.4 1.0 broadcast_in_dim.8
  39.4 0.0 copy-start.1
  39.4 0.0 copy-start.2
  39.4 14.7 %all-to-all-start.2 = ((bf16[8,192,256]{2,1,0:T(8,128)(2,1)}), bf16[8,192,256]{2,1,0:T(8,128)(2,1)S(1)}, u32[]{:S(2)}, u32[]{:S(2)}) async-start(bf16[8,192,256]{2,1,0:T(8,128)(2,1)} %broadcast_in_dim.8), calls=%async_computation.2 | async-start | bytes 1572864 | tf_op jit(solution)/shard_map/all_to_all | solution.py:163
  54.0 1.9 %collective-permute-start = (bf16[32,128,128]{2,1,0:T(8,128)(2,1)S(1)}, bf16[32,128,128]{2,1,0:T(8,128)(2,1)}, u32[]{:S(2)}, u32[]{:S(2)}) collective-permute-start(bf16[32,128,128]{2,1,0:T(8,128)(2,1)S(1)} %bitcast.9), channel_id=1, source_target_pairs={{0,1},{1,0},{2,3},{3,2},{4,5},{5,4},{6,7},{7,6},{8,9},{9,8},{10,11... | collective-permute-start | bytes 3145736 | tf_op jit(solution)/shard_map/ppermute | solution.py:182
  56.0 18.2 %all-to-all-done.2.g_own_ref = bf16[8,192,256]{2,1,0:T(8,128)(2,1)S(1)} async-done(((bf16[8,192,256]{2,1,0:T(8,128)(2,1)}), bf16[8,192,256]{2,1,0:T(8,128)(2,1)S(1)}, u32[]{:S(2)}, u32[]{:S(2)}) %all-to-all-start.2) | async-done | bytes 786464 | tf_op jit(solution)/shard_map/all_to_all | solution.py:163
  74.2 1.9 %collective-permute-start.2 = (bf16[8,192,256]{2,1,0:T(8,128)(2,1)S(1)}, bf16[8,192,256]{2,1,0:T(8,128)(2,1)S(1)}, u32[]{:S(2)}, u32[]{:S(2)}) collective-permute-start(bf16[8,192,256]{2,1,0:T(8,128)(2,1)S(1)} %all-to-all-done.2.g_own_ref), channel_id=1, source_target_pairs={{0,1},{1,0},{2,3},{3,2},{4,5},{5,4},{6,7},{7,6},{8,9},{9,8},{10,11... | collective-permute-start | bytes 2359304 | tf_op jit(solution)/shard_map/ppermute | solution.py:185
  76.1 0.0 copy-start.3
  76.1 0.1 pad_add_fusion.core_ref
  76.2 0.0 collective-permute-done.other_ref
  76.2 0.0 copy-done.1
  76.2 0.0 copy-done.2
  76.2 0.6 copy-done.3
  76.7 6.1 %shard_map.68 = (f32[256,256]{1,0:T(8,128)}, bf16[4,256,256]{2,1,0:T(8,128)(2,1)}) custom-call(s32[2]{0:T(128)S(1)} %pad_add_fusion.core_ref, s32[64]{0:T(128)S(1)} %copy-done.3, s32[8192]{0:T(1024)S(1)} %copy-done.2, bf16[256,256]{1,0:T(8,128)(2,1)S(1)} %copy-done.1, bf16[32,128,128]{2,1,0:T(8,128)(2,1)S(1)} %bitcast.10, ...), custom_call_target="tpu_custom_call" | custom-call | flops 1200000000 | bytes 4000000 | tf_op jit(solution)/shard_map/pallas_call | solution.py:116
  82.9 5.0 %all-to-all-start.3 = ((bf16[4,256,256]{2,1,0:T(8,128)(2,1)}), bf16[4,256,256]{2,1,0:T(8,128)(2,1)S(1)}, u32[]{:S(2)}, u32[]{:S(2)}) async-start(bf16[4,256,256]{2,1,0:T(8,128)(2,1)} %get-tuple-element.5), calls=%async_computation.3 | async-start | bytes 1048576 | tf_op jit(solution)/shard_map/all_to_all | solution.py:190
  87.8 0.1 pad_add_fusion.1.place_ref
  87.9 0.0 collective-permute-done.2.g_other_ref
  87.9 8.9 %all-to-all-done.3.a_ref = bf16[4,256,256]{2,1,0:T(8,128)(2,1)S(1)} async-done(((bf16[4,256,256]{2,1,0:T(8,128)(2,1)}), bf16[4,256,256]{2,1,0:T(8,128)(2,1)S(1)}, u32[]{:S(2)}, u32[]{:S(2)}) %all-to-all-start.3) | async-done | bytes 524320 | tf_op jit(solution)/shard_map/all_to_all | solution.py:190
  96.8 0.0 copy-done
  96.8 1.2 shard_map.69
  98.0 27.6 %all_to_all.26 = f32[8,96,256]{2,1,0:T(8,128)S(1)} all-to-all(f32[8,96,256]{2,1,0:T(8,128)S(1)} %bitcast.8), channel_id=1, replica_groups=mesh['x'=4,'y'=8,'z'=8,'core'=2] {'y'}, dimensions={0} | all-to-all | bytes 1572864 | tf_op jit(solution)/shard_map/all_to_all | solution.py:192
  125.6 0.7 reduce_sum.9
  (4 shorter events, 0.1 us)
Async XLA Ops:
  0.6 0.8 dynamic-slice-start
  21.4 5.0 %copy-start.4 = (bf16[256,180]{0,1:T(8,128)(2,1)S(1)}, bf16[256,180]{0,1:T(8,128)(2,1)}, u32[]{:S(2)}) copy-start(bf16[256,180]{0,1:T(8,128)(2,1)} %param.7) | copy-start | bytes 276484
  21.4 16.9 %all-to-all-start.1 = ((bf16[4,8,128,128]{3,2,1,0:T(8,128)(2,1)}), bf16[4,8,128,128]{3,2,1,0:T(8,128)(2,1)S(1)}, u32[]{:S(2)}, u32[]{:S(2)}) async-start(bf16[4,8,128,128]{3,2,1,0:T(8,128)(2,1)} %broadcast_in_dim.7), calls=%async_computation.1 | async-start | bytes 2097152 | tf_op jit(solution)/shard_map/all_to_all | solution.py:163
  26.4 8.4 %collective-permute-start.1 = (bf16[192,256]{1,0:T(8,128)(2,1)S(1)}, bf16[192,256]{1,0:T(8,128)(2,1)S(1)}, u32[]{:S(2)}, u32[]{:S(2)}) collective-permute-start(bf16[192,256]{1,0:T(8,128)(2,1)S(1)} %bitcast.12), channel_id=1, source_target_pairs={{0,0},{2,2},{4,128},{6,130},{8,256},{10,258},{12,384},{14,386},{12... | collective-permute-start | bytes 294920 | tf_op jit(solution)/shard_map/ppermute | solution.py:177
  39.4 36.8 %copy-start.1 = (bf16[256,256]{1,0:T(8,128)(2,1)S(1)}, bf16[256,256]{1,0:T(8,128)(2,1)}, u32[]{:S(2)}) copy-start(bf16[256,256]{1,0:T(8,128)(2,1)} %q_ref.1) | copy-start | bytes 393220
  39.4 36.8 %copy-start.2 = (s32[8192]{0:T(1024)S(1)}, s32[8192]{0:T(1024)}, u32[]{:S(2)}) copy-start(s32[8192]{0:T(1024)} %docs_ref.1) | copy-start | bytes 98308
  39.4 34.8 %all-to-all-start.2 = ((bf16[8,192,256]{2,1,0:T(8,128)(2,1)}), bf16[8,192,256]{2,1,0:T(8,128)(2,1)S(1)}, u32[]{:S(2)}, u32[]{:S(2)}) async-start(bf16[8,192,256]{2,1,0:T(8,128)(2,1)} %broadcast_in_dim.8), calls=%async_computation.2 | async-start | bytes 1572864 | tf_op jit(solution)/shard_map/all_to_all | solution.py:163
  54.0 22.1 %collective-permute-start = (bf16[32,128,128]{2,1,0:T(8,128)(2,1)S(1)}, bf16[32,128,128]{2,1,0:T(8,128)(2,1)}, u32[]{:S(2)}, u32[]{:S(2)}) collective-permute-start(bf16[32,128,128]{2,1,0:T(8,128)(2,1)S(1)} %bitcast.9), channel_id=1, source_target_pairs={{0,1},{1,0},{2,3},{3,2},{4,5},{5,4},{6,7},{7,6},{8,9},{9,8},{10,11... | collective-permute-start | bytes 3145736 | tf_op jit(solution)/shard_map/ppermute | solution.py:182
  74.2 13.7 %collective-permute-start.2 = (bf16[8,192,256]{2,1,0:T(8,128)(2,1)S(1)}, bf16[8,192,256]{2,1,0:T(8,128)(2,1)S(1)}, u32[]{:S(2)}, u32[]{:S(2)}) collective-permute-start(bf16[8,192,256]{2,1,0:T(8,128)(2,1)S(1)} %all-to-all-done.2.g_own_ref), channel_id=1, source_target_pairs={{0,1},{1,0},{2,3},{3,2},{4,5},{5,4},{6,7},{7,6},{8,9},{9,8},{10,11... | collective-permute-start | bytes 2359304 | tf_op jit(solution)/shard_map/ppermute | solution.py:185
  76.1 0.7 copy-start.3
  82.9 13.9 %copy-start = (f32[256,256]{1,0:T(8,128)S(1)}, f32[256,256]{1,0:T(8,128)}, u32[]{:S(2)}) copy-start(f32[256,256]{1,0:T(8,128)} %get-tuple-element.2.own_ref) | copy-start | bytes 786436
  82.9 13.9 %all-to-all-start.3 = ((bf16[4,256,256]{2,1,0:T(8,128)(2,1)}), bf16[4,256,256]{2,1,0:T(8,128)(2,1)S(1)}, u32[]{:S(2)}, u32[]{:S(2)}) async-start(bf16[4,256,256]{2,1,0:T(8,128)(2,1)} %get-tuple-element.5), calls=%async_computation.3 | async-start | bytes 1048576 | tf_op jit(solution)/shard_map/all_to_all | solution.py:190

commit v3 on v2

--- a/solution.py
+++ b/solution.py
@@ -131,16 +131,21 @@
 
 
 def term_kernel(place_ref, g_own_ref, g_other_ref, a_ref, own_ref, out_ref):
-    core, x = place_ref[0], place_ref[1]
+    core, x, z = place_ref[0], place_ref[1], place_ref[2]
     pairs = out_ref.shape[0] // 2
+
+    def slot(peer, pair):
+        apart = z ^ (pairs * peer + pair)
+        return ((apart & 1) << 2) | (apart & 2) | (apart >> 2)
+
     a = own_ref[...]
     low = (a - a.astype(jnp.bfloat16).astype(jnp.float32)).astype(jnp.bfloat16)
     for pair in range(pairs):
         for g_ref, side in ((g_own_ref, core), (g_other_ref, 1 - core)):
-            term = jnp.dot(g_ref[pairs * x + pair], low, preferred_element_type=jnp.float32)
+            term = jnp.dot(g_ref[slot(x, pair)], low, preferred_element_type=jnp.float32)
             for peer in range(a_ref.shape[0]):
                 term = term + jnp.dot(
-                    g_ref[pairs * peer + pair], a_ref[peer], preferred_element_type=jnp.float32
+                    g_ref[slot(peer, pair)], a_ref[peer], preferred_element_type=jnp.float32
                 )
             out_ref[2 * pair + side] = term
 
@@ -181,14 +186,20 @@
     own = everyone(own, "x", nx).reshape(nx * ny, TILE, 2 * DH)
     other = lax.ppermute(own, "core", swap)
 
-    g_own = everyone(grads, "z", nz)
+    g_own = grads[None]
+    bit = nz // 2
+    while bit:
+        came = lax.ppermute(g_own, "z", [(i, i ^ bit) for i in range(nz)])
+        g_own = jnp.concatenate([g_own, came], axis=0)
+        bit //= 2
     g_other = lax.ppermute(g_own, "core", swap)
 
     attended, send = attention(
         jnp.stack([core, 2 * ctx]), tile_list, doc_ids, queries, own, other, nx
     )
     gathered = lax.all_to_all(send, "x", 0, 0)
-    term = term_of(jnp.stack([core, x]), g_own, g_other, gathered, attended)
+    place = jnp.stack([core, x, lax.axis_index("z")])
+    term = term_of(place, g_own, g_other, gathered, attended)
     parts = lax.all_to_all(term.reshape(ny, PADDED, attended.shape[1]), "y", 0, 0)
     weight_grad = jnp.sum(parts, axis=0)[:BLOCK]
     return attended, weight_grad

time: 127 us -> 126 us (level)
  waiting for transfers between devices: 33.5 us -> 25.1 us
  starting transfers between devices: 33.9 us -> 41.9 us
    ppermute x0 -> x3, starting transfers between devices: none -> 22.9 us  [on_device(): came = lax.ppermute(g_own, 'z', [(i, i ^ bit) for i in range(nz)])]
    all_to_all x2 -> x1, waiting for transfers between devices: 21.7 us -> 0.01 us  [everyone(): lax.all_to_all(jnp.broadcast_to(x[None], (size,) + x.shape), axes, 0, 0)]
    all_to_all x2 -> x1, starting transfers between devices: 19.6 us -> 4.96 us  [everyone(): lax.all_to_all(jnp.broadcast_to(x[None], (size,) + x.shape), axes, 0, 0)]
    ppermute x0 -> x3, waiting for transfers between devices: none -> 13.3 us  [on_device(): came = lax.ppermute(g_own, 'z', [(i, i ^ bit) for i in range(nz)])]
  transfers between devices with their start and end apart: 6 -> 8, of which waited for: 4 -> 5; matrix products, arithmetic and copies ran while one was open for 0% -> 0% of each run, Pallas kernels for 5% -> 5%
where the time goes in v3:
time: 126 us
  blocking collectives  47.2 us (37%)
  starting transfers between devices  41.9 us (33%)
  waiting for transfers between devices  25.1 us (20%)
  Pallas kernels  7.32 us (6%)
  local copies, waits for them, and re-layouts  2.63 us (2%)
    all_to_all x1, blocking collectives, on_device(): lax.all_to_all(term.reshape(ny, PADDED, attended.shape[1]), 'y', 0, 0)  28.4 us
    ppermute x3, starting transfers between devices, on_device(): came = lax.ppermute(g_own, 'z', [(i, i ^ bit) for i in range(nz)])  22.9 us
    all_to_all x1, blocking collectives, everyone(): lax.all_to_all(jnp.broadcast_to(x[None], (size,) + x.shape), axes, 0, 0)  18.8 us
    ppermute x3, waiting for transfers between devices, on_device(): came = lax.ppermute(g_own, 'z', [(i, i ^ bit) for i in range(nz)])  13.3 us
    all_to_all x1, waiting for transfers between devices, on_device(): gathered = lax.all_to_all(send, 'x', 0, 0)  8.9 us
    pallas_call x1, Pallas kernels, attention(): pl.pallas_call(attention_kernel, out_shape=(jax.ShapeDtypeStruct(queries....  6.1 us
    ppermute x1, starting transfers between devices, on_device(): grads = lax.ppermute(grads, ('x', 'z'), turn)  5.53 us
    all_to_all x1, starting transfers between devices, everyone(): lax.all_to_all(jnp.broadcast_to(x[None], (size,) + x.shape), axes, 0, 0)  4.96 us
  transfers between devices with their start and end apart: 8, of which 5 were waited for; matrix products, arithmetic and copies ran while one was open for 0% of the time, Pallas kernels for 5%

profile of v3, /device:TPU:2, one launch (start us, length us, event | category | flops | bytes accessed | tf_op | source)
XLA Modules:
  0.0 125.9 jit_solution(5750107309438365859)
XLA Ops:
  0.6 0.0 dynamic-slice-start
  0.7 0.7 dynamic-slice-done
  1.4 18.8 %all_to_all.20 = bf16[8,128,128]{2,1,0:T(8,128)(2,1)S(1)} all-to-all(bf16[8,128,128]{2,1,0:T(8,128)(2,1)S(1)} %broadcast_in_dim.6), channel_id=1, replica_groups=mesh['x'=4,'y'=8,'z'=8,'core'=2] {'y'}, dimensions={0} | all-to-all | bytes 524288 | tf_op jit(solution)/shard_map/all_to_all | solution.py:168
  20.2 1.2 broadcast_in_dim.7
  21.4 5.0 %all-to-all-start.1 = ((bf16[4,8,128,128]{3,2,1,0:T(8,128)(2,1)}), bf16[4,8,128,128]{3,2,1,0:T(8,128)(2,1)S(1)}, u32[]{:S(2)}, u32[]{:S(2)}) async-start(bf16[4,8,128,128]{3,2,1,0:T(8,128)(2,1)} %broadcast_in_dim.7), calls=%async_computation.1 | async-start | bytes 2097152 | tf_op jit(solution)/shard_map/all_to_all | solution.py:168
  26.4 0.0 copy-done.4
  26.4 5.5 %collective-permute-start.1 = (bf16[192,256]{1,0:T(8,128)(2,1)S(1)}, bf16[192,256]{1,0:T(8,128)(2,1)S(1)}, u32[]{:S(2)}, u32[]{:S(2)}) collective-permute-start(bf16[192,256]{1,0:T(8,128)(2,1)S(1)} %bitcast.18), channel_id=1, source_target_pairs={{0,0},{2,2},{4,128},{6,130},{8,256},{10,258},{12,384},{14,386},{12... | collective-permute-start | bytes 294920 | tf_op jit(solution)/shard_map/ppermute | solution.py:182
  32.0 2.9 %collective-permute-done.1 = bf16[192,256]{1,0:T(8,128)(2,1)S(1)} collective-permute-done((bf16[192,256]{1,0:T(8,128)(2,1)S(1)}, bf16[192,256]{1,0:T(8,128)(2,1)S(1)}, u32[]{:S(2)}, u32[]{:S(2)}) %collective-permute-start.1) | collective-permute-done | bytes 98336 | tf_op jit(solution)/shard_map/ppermute | solution.py:182
  34.9 12.6 %collective-permute-start.2 = (bf16[1,192,256]{2,1,0:T(8,128)(2,1)S(1)}, bf16[1,192,256]{2,1,0:T(8,128)(2,1)S(1)}, u32[]{:S(2)}, u32[]{:S(2)}) collective-permute-start(bf16[1,192,256]{2,1,0:T(8,128)(2,1)S(1)} %bitcast.13), channel_id=1, source_target_pairs={{0,8},{2,10},{4,12},{6,14},{8,0},{10,2},{12,4},{14,6},{1,9},{3,11}... | collective-permute-start | bytes 294920 | tf_op jit(solution)/shard_map/ppermute | solution.py:192
  47.5 2.6 %collective-permute-done.2 = bf16[1,192,256]{2,1,0:T(8,128)(2,1)S(1)} collective-permute-done((bf16[1,192,256]{2,1,0:T(8,128)(2,1)S(1)}, bf16[1,192,256]{2,1,0:T(8,128)(2,1)S(1)}, u32[]{:S(2)}, u32[]{:S(2)}) %collective-permute-start.2) | collective-permute-done | bytes 98336 | tf_op jit(solution)/shard_map/ppermute | solution.py:192
  50.1 7.4 %collective-permute-start.3 = (bf16[2,192,256]{2,1,0:T(8,128)(2,1)S(1)}, bf16[2,192,256]{2,1,0:T(8,128)(2,1)S(1)}, u32[]{:S(2)}, u32[]{:S(2)}) collective-permute-start(bf16[2,192,256]{2,1,0:T(8,128)(2,1)S(1)} %pad_maximum_fusion.2), channel_id=1, source_target_pairs={{0,4},{2,6},{4,0},{6,2},{8,12},{10,14},{12,8},{14,10},{1,5},{3,7},... | collective-permute-start | bytes 589832 | tf_op jit(solution)/shard_map/ppermute | solution.py:192
  57.5 0.0 all-to-all-done.1
  57.5 1.9 %collective-permute-start = (bf16[32,128,128]{2,1,0:T(8,128)(2,1)S(1)}, bf16[32,128,128]{2,1,0:T(8,128)(2,1)}, u32[]{:S(2)}, u32[]{:S(2)}) collective-permute-start(bf16[32,128,128]{2,1,0:T(8,128)(2,1)S(1)} %bitcast.11), channel_id=1, source_target_pairs={{0,1},{1,0},{2,3},{3,2},{4,5},{5,4},{6,7},{7,6},{8,9},{9,8},{10,11... | collective-permute-start | bytes 3145736 | tf_op jit(solution)/shard_map/ppermute | solution.py:187
  59.4 3.9 %collective-permute-done.3 = bf16[2,192,256]{2,1,0:T(8,128)(2,1)S(1)} collective-permute-done((bf16[2,192,256]{2,1,0:T(8,128)(2,1)S(1)}, bf16[2,192,256]{2,1,0:T(8,128)(2,1)S(1)}, u32[]{:S(2)}, u32[]{:S(2)}) %collective-permute-start.3) | collective-permute-done | bytes 196640 | tf_op jit(solution)/shard_map/ppermute | solution.py:192
  63.4 0.0 copy-start.1
  63.4 0.0 copy-start.2
  63.4 2.9 %collective-permute-start.4 = (bf16[4,192,256]{2,1,0:T(8,128)(2,1)S(1)}, bf16[4,192,256]{2,1,0:T(8,128)(2,1)S(1)}, u32[]{:S(2)}, u32[]{:S(2)}) collective-permute-start(bf16[4,192,256]{2,1,0:T(8,128)(2,1)S(1)} %pad_maximum_fusion.1), channel_id=1, source_target_pairs={{0,2},{2,0},{4,6},{6,4},{8,10},{10,8},{12,14},{14,12},{1,3},{3,1},... | collective-permute-start | bytes 1179656 | tf_op jit(solution)/shard_map/ppermute | solution.py:192
  66.3 6.8 %collective-permute-done.4 = bf16[4,192,256]{2,1,0:T(8,128)(2,1)S(1)} collective-permute-done((bf16[4,192,256]{2,1,0:T(8,128)(2,1)S(1)}, bf16[4,192,256]{2,1,0:T(8,128)(2,1)S(1)}, u32[]{:S(2)}, u32[]{:S(2)}) %collective-permute-start.4) | collective-permute-done | bytes 393248 | tf_op jit(solution)/shard_map/ppermute | solution.py:192
  73.2 0.1 pad_maximum_fusion.g_own_ref
  73.3 1.9 %collective-permute-start.5 = (bf16[8,192,256]{2,1,0:T(8,128)(2,1)S(1)}, bf16[8,192,256]{2,1,0:T(8,128)(2,1)S(1)}, u32[]{:S(2)}, u32[]{:S(2)}) collective-permute-start(bf16[8,192,256]{2,1,0:T(8,128)(2,1)S(1)} %pad_maximum_fusion.g_own_ref), channel_id=1, source_target_pairs={{0,1},{1,0},{2,3},{3,2},{4,5},{5,4},{6,7},{7,6},{8,9},{9,8},{10,11... | collective-permute-start | bytes 2359304 | tf_op jit(solution)/shard_map/ppermute | solution.py:195
  75.2 0.0 copy-start.3
  75.2 0.1 pad_add_fusion.core_ref
  75.3 0.0 collective-permute-done.other_ref
  75.3 0.6 copy-done.3
  75.9 6.1 %shard_map.68 = (f32[256,256]{1,0:T(8,128)}, bf16[4,256,256]{2,1,0:T(8,128)(2,1)}) custom-call(s32[2]{0:T(128)S(1)} %pad_add_fusion.core_ref, s32[64]{0:T(128)S(1)} %copy-done.3, s32[8192]{0:T(1024)S(1)} %copy-done.2, bf16[256,256]{1,0:T(8,128)(2,1)S(1)} %copy-done.1, bf16[32,128,128]{2,1,0:T(8,128)(2,1)S(1)} %bitcast.12, ...), custom_call_target="tpu_custom_call" | custom-call | flops 1200000000 | bytes 4000000 | tf_op jit(solution)/shard_map/pallas_call | solution.py:116
  82.0 4.6 %all-to-all-start.2 = ((bf16[4,256,256]{2,1,0:T(8,128)(2,1)}), bf16[4,256,256]{2,1,0:T(8,128)(2,1)S(1)}, u32[]{:S(2)}, u32[]{:S(2)}) async-start(bf16[4,256,256]{2,1,0:T(8,128)(2,1)} %get-tuple-element.5), calls=%async_computation.2 | async-start | bytes 1048576 | tf_op jit(solution)/shard_map/all_to_all | solution.py:200
  86.6 0.1 pad_add_fusion.1.place_ref
  86.7 0.0 collective-permute-done.5.g_other_ref
  86.7 8.9 %all-to-all-done.2.a_ref = bf16[4,256,256]{2,1,0:T(8,128)(2,1)S(1)} async-done(((bf16[4,256,256]{2,1,0:T(8,128)(2,1)}), bf16[4,256,256]{2,1,0:T(8,128)(2,1)S(1)}, u32[]{:S(2)}, u32[]{:S(2)}) %all-to-all-start.2) | async-done | bytes 524320 | tf_op jit(solution)/shard_map/all_to_all | solution.py:200
  95.6 1.2 shard_map.69
  96.8 28.4 %all_to_all.21 = f32[8,96,256]{2,1,0:T(8,128)S(1)} all-to-all(f32[8,96,256]{2,1,0:T(8,128)S(1)} %bitcast.10), channel_id=1, replica_groups=mesh['x'=4,'y'=8,'z'=8,'core'=2] {'y'}, dimensions={0} | all-to-all | bytes 1572864 | tf_op jit(solution)/shard_map/all_to_all | solution.py:203
  125.2 0.7 reduce_sum.9
  (10 shorter events, 0.1 us)
Async XLA Ops:
  0.6 0.8 dynamic-slice-start
  21.4 5.0 %copy-start.4 = (bf16[256,180]{0,1:T(8,128)(2,1)S(1)}, bf16[256,180]{0,1:T(8,128)(2,1)}, u32[]{:S(2)}) copy-start(bf16[256,180]{0,1:T(8,128)(2,1)} %param.7) | copy-start | bytes 276484
  21.4 36.0 %all-to-all-start.1 = ((bf16[4,8,128,128]{3,2,1,0:T(8,128)(2,1)}), bf16[4,8,128,128]{3,2,1,0:T(8,128)(2,1)S(1)}, u32[]{:S(2)}, u32[]{:S(2)}) async-start(bf16[4,8,128,128]{3,2,1,0:T(8,128)(2,1)} %broadcast_in_dim.7), calls=%async_computation.1 | async-start | bytes 2097152 | tf_op jit(solution)/shard_map/all_to_all | solution.py:168
  26.4 8.4 %collective-permute-start.1 = (bf16[192,256]{1,0:T(8,128)(2,1)S(1)}, bf16[192,256]{1,0:T(8,128)(2,1)S(1)}, u32[]{:S(2)}, u32[]{:S(2)}) collective-permute-start(bf16[192,256]{1,0:T(8,128)(2,1)S(1)} %bitcast.18), channel_id=1, source_target_pairs={{0,0},{2,2},{4,128},{6,130},{8,256},{10,258},{12,384},{14,386},{12... | collective-permute-start | bytes 294920 | tf_op jit(solution)/shard_map/ppermute | solution.py:182
  34.9 15.2 %collective-permute-start.2 = (bf16[1,192,256]{2,1,0:T(8,128)(2,1)S(1)}, bf16[1,192,256]{2,1,0:T(8,128)(2,1)S(1)}, u32[]{:S(2)}, u32[]{:S(2)}) collective-permute-start(bf16[1,192,256]{2,1,0:T(8,128)(2,1)S(1)} %bitcast.13), channel_id=1, source_target_pairs={{0,8},{2,10},{4,12},{6,14},{8,0},{10,2},{12,4},{14,6},{1,9},{3,11}... | collective-permute-start | bytes 294920 | tf_op jit(solution)/shard_map/ppermute | solution.py:192
  50.1 13.2 %collective-permute-start.3 = (bf16[2,192,256]{2,1,0:T(8,128)(2,1)S(1)}, bf16[2,192,256]{2,1,0:T(8,128)(2,1)S(1)}, u32[]{:S(2)}, u32[]{:S(2)}) collective-permute-start(bf16[2,192,256]{2,1,0:T(8,128)(2,1)S(1)} %pad_maximum_fusion.2), channel_id=1, source_target_pairs={{0,4},{2,6},{4,0},{6,2},{8,12},{10,14},{12,8},{14,10},{1,5},{3,7},... | collective-permute-start | bytes 589832 | tf_op jit(solution)/shard_map/ppermute | solution.py:192
  57.5 17.8 %collective-permute-start = (bf16[32,128,128]{2,1,0:T(8,128)(2,1)S(1)}, bf16[32,128,128]{2,1,0:T(8,128)(2,1)}, u32[]{:S(2)}, u32[]{:S(2)}) collective-permute-start(bf16[32,128,128]{2,1,0:T(8,128)(2,1)S(1)} %bitcast.11), channel_id=1, source_target_pairs={{0,1},{1,0},{2,3},{3,2},{4,5},{5,4},{6,7},{7,6},{8,9},{9,8},{10,11... | collective-permute-start | bytes 3145736 | tf_op jit(solution)/shard_map/ppermute | solution.py:187
  63.4 11.9 %copy-start.1 = (bf16[256,256]{1,0:T(8,128)(2,1)S(1)}, bf16[256,256]{1,0:T(8,128)(2,1)}, u32[]{:S(2)}) copy-start(bf16[256,256]{1,0:T(8,128)(2,1)} %q_ref.1) | copy-start | bytes 393220
  63.4 11.9 %copy-start.2 = (s32[8192]{0:T(1024)S(1)}, s32[8192]{0:T(1024)}, u32[]{:S(2)}) copy-start(s32[8192]{0:T(1024)} %docs_ref.1) | copy-start | bytes 98308
  63.4 9.8 %collective-permute-start.4 = (bf16[4,192,256]{2,1,0:T(8,128)(2,1)S(1)}, bf16[4,192,256]{2,1,0:T(8,128)(2,1)S(1)}, u32[]{:S(2)}, u32[]{:S(2)}) collective-permute-start(bf16[4,192,256]{2,1,0:T(8,128)(2,1)S(1)} %pad_maximum_fusion.1), channel_id=1, source_target_pairs={{0,2},{2,0},{4,6},{6,4},{8,10},{10,8},{12,14},{14,12},{1,3},{3,1},... | collective-permute-start | bytes 1179656 | tf_op jit(solution)/shard_map/ppermute | solution.py:192
  73.3 13.4 %collective-permute-start.5 = (bf16[8,192,256]{2,1,0:T(8,128)(2,1)S(1)}, bf16[8,192,256]{2,1,0:T(8,128)(2,1)S(1)}, u32[]{:S(2)}, u32[]{:S(2)}) collective-permute-start(bf16[8,192,256]{2,1,0:T(8,128)(2,1)S(1)} %pad_maximum_fusion.g_own_ref), channel_id=1, source_target_pairs={{0,1},{1,0},{2,3},{3,2},{4,5},{5,4},{6,7},{7,6},{8,9},{9,8},{10,11... | collective-permute-start | bytes 2359304 | tf_op jit(solution)/shard_map/ppermute | solution.py:195
  75.2 0.7 copy-start.3
  82.0 13.6 %copy-start = (f32[256,256]{1,0:T(8,128)S(1)}, f32[256,256]{1,0:T(8,128)}, u32[]{:S(2)}) copy-start(f32[256,256]{1,0:T(8,128)} %get-tuple-element.2.own_ref) | copy-start | bytes 786436
  82.0 13.6 %all-to-all-start.2 = ((bf16[4,256,256]{2,1,0:T(8,128)(2,1)}), bf16[4,256,256]{2,1,0:T(8,128)(2,1)S(1)}, u32[]{:S(2)}, u32[]{:S(2)}) async-start(bf16[4,256,256]{2,1,0:T(8,128)(2,1)} %get-tuple-element.5), calls=%async_computation.2 | async-start | bytes 1048576 | tf_op jit(solution)/shard_map/all_to_all | solution.py:200

commit v4 on v2

v4 whole, which is shorter than its diff:
```python
import jax
import jax.numpy as jnp
from jax import lax
from jax.experimental import pallas as pl
from jax.experimental.pallas import tpu as pltpu
from jax.sharding import Mesh, PartitionSpec as P


DH = 64
TILE = 128
DOCS = 8
HEADS = 4
SPAN = 18
BLOCK = 90
PADDED = 96
NEG_FILL = -1e30


def tables_kernel(place_ref, tiles_ref, docs_ref, q_ref, table_ref, q_t_ref):
    count = tiles_ref.shape[0]
    tokens = docs_ref.shape[0]

    def invert(slot, carry):
        table_ref[tiles_ref[slot]] = slot
        return carry

    lax.fori_loop(0, count, invert, 0)

    def bisect(step, lows):
        size = lax.shift_right_logical(tokens, step + 1)
        return tuple(
            jnp.where(docs_ref[low + size - 1] < doc + 1, low + size, low) for doc, low in enumerate(lows)
        )

    steps = tokens.bit_length() - 1
    bounds = lax.fori_loop(0, steps, bisect, (jnp.int32(0),) * (DOCS - 1))
    for doc, low in enumerate(bounds):
        last = docs_ref[jnp.minimum(low, tokens - 1)] < doc + 1
        table_ref[count + doc] = jnp.where(last, low + 1, low)
    for part in range(2):
        table_ref[count + DOCS - 1 + part] = tiles_ref[place_ref[1] + part]
        q = q_ref[part * TILE:(part + 1) * TILE, :]
        q_t = jnp.transpose(q.astype(jnp.float32) * (DH ** -0.5)).astype(jnp.bfloat16)
        q_t = jnp.concatenate([q_t[h * DH:(h + 1) * DH] for h in range(HEADS)], axis=1)
        q_t_ref[part] = jnp.concatenate([q_t, jnp.zeros_like(q_t)], axis=0)


def tables_of(place, tiles, docs, queries):
    smem = pl.BlockSpec(memory_space=pltpu.SMEM)
    vmem = pl.BlockSpec(memory_space=pltpu.VMEM)
    return pl.pallas_call(
        tables_kernel,
        out_shape=(
            jax.ShapeDtypeStruct((tiles.shape[0] + DOCS + 1,), jnp.int32),
            jax.ShapeDtypeStruct((2, 2 * DH, HEADS * TILE), jnp.bfloat16),
        ),
        in_specs=[smem, smem, smem, vmem],
        out_specs=(smem, vmem),
        cost_estimate=pl.CostEstimate(flops=1_000_000, bytes_accessed=500_000, transcendentals=0),
        compiler_params=pltpu.CompilerParams(vmem_limit_bytes=8 << 20),
    )(place, tiles, docs, queries)


def attention_kernel(place_ref, table_ref, q_ref, own_ref, other_ref, out_ref, send_ref, s_ref):
    count = table_ref.shape[0] - DOCS - 1
    core = place_ref[0]
    width = HEADS * TILE
    bounds = [table_ref[count + doc] for doc in range(DOCS - 1)]

    lane = lax.broadcasted_iota(jnp.int32, (1, TILE), 1)
    sub = lax.broadcasted_iota(jnp.int32, (2 * TILE, TILE), 0)

    def pick(tile):
        slot = table_ref[tile]
        at = lax.shift_right_logical(slot, 1)
        return jnp.where((slot & 1) == core, own_ref[at], other_ref[at])

    for part in range(2):
        tile = table_ref[count + DOCS - 1 + part]
        base = tile * TILE
        begin = jnp.int32(0)
        row_pos = base + lane
        row_begin = jnp.zeros((1, TILE), jnp.int32)
        for bound in bounds:
            begin = jnp.where(bound <= base, jnp.maximum(begin, bound), begin)
            row_begin = jnp.where(bound <= row_pos, jnp.maximum(row_begin, bound), row_begin)
        low = lax.div(begin, TILE)
        pairs = lax.div(tile - low + 2, 2)

        q_t = q_ref[part]

        def score(pair, top):
            at = low + 2 * pair
            kv = jnp.concatenate([pick(at), pick(jnp.minimum(at + 1, tile))], axis=0)
            scores = jnp.dot(kv, q_t, preferred_element_type=jnp.float32)
            key_pos = at * TILE + sub
            allowed = (key_pos >= row_begin) & (key_pos <= row_pos)
            start = pl.multiple_of(pair * (2 * TILE), 2 * TILE)
            tops = []
            for h in range(HEADS):
                masked = jnp.where(allowed, scores[:, h * TILE:(h + 1) * TILE], NEG_FILL)
                s_ref[pl.ds(start, 2 * TILE), h * TILE:(h + 1) * TILE] = masked
                tops.append(jnp.max(masked.reshape(2 * TILE // 8, 8, TILE), axis=0))
            return jnp.maximum(top, jnp.concatenate(tops, axis=1))

        top = lax.fori_loop(0, pairs, score, jnp.full((8, width), NEG_FILL, jnp.float32))
        top = jnp.max(top, axis=0, keepdims=True)

        def add(pair, carry):
            total, summed = carry
            at = low + 2 * pair
            kv = jnp.concatenate([pick(at), pick(jnp.minimum(at + 1, tile))], axis=0)
            start = pl.multiple_of(pair * (2 * TILE), 2 * TILE)
            weights = jnp.exp(s_ref[pl.ds(start, 2 * TILE), :] - top)
            total = total + jnp.sum(weights.reshape(2 * TILE // 8, 8, width), axis=0)
            summed = summed + lax.dot_general(
                kv[:, DH:], weights.astype(jnp.bfloat16), (((0,), (0,)), ((), ())), preferred_element_type=jnp.float32
            )
            return total, summed

        total, summed = lax.fori_loop(
            0, pairs, add, (jnp.zeros((8, width), jnp.float32), jnp.zeros((DH, width), jnp.float32))
        )
        total = jnp.sum(total, axis=0, keepdims=True)
        normed = summed / total
        for h in range(0, HEADS, 2):
            both = jnp.concatenate(
                [normed[:, h * TILE:(h + 1) * TILE], normed[:, (h + 1) * TILE:(h + 2) * TILE]], axis=0
            )
            both = jnp.transpose(both)
            out_ref[part * TILE:(part + 1) * TILE, h * DH:(h + 2) * DH] = both
            for peer in range(send_ref.shape[0]):
                send_ref[peer, part * TILE:(part + 1) * TILE, h * DH:(h + 2) * DH] = both


def attention(place, table, q_t, own, other, peers):
    smem = pl.BlockSpec(memory_space=pltpu.SMEM)
    vmem = pl.BlockSpec(memory_space=pltpu.VMEM)
    rows, columns = 2 * TILE, HEADS * DH
    return pl.pallas_call(
        attention_kernel,
        out_shape=(
            jax.ShapeDtypeStruct((rows, columns), jnp.float32),
            jax.ShapeDtypeStruct((peers, rows, columns), jnp.float32),
        ),
        in_specs=[smem, smem, vmem, vmem, vmem],
        out_specs=(vmem, vmem),
        scratch_shapes=[pltpu.VMEM((SPAN * TILE, HEADS * TILE), jnp.float32)],
        cost_estimate=pl.CostEstimate(flops=1_200_000_000, bytes_accessed=4_000_000, transcendentals=2_200_000),
        compiler_params=pltpu.CompilerParams(vmem_limit_bytes=32 << 20),
    )(place, table, q_t, own, other)


def term_kernel(place_ref, g00_ref, g01_ref, g10_ref, g11_ref, a_ref, out_ref, own_ref, high_ref, low_ref, sum_ref):
    core, z, y = place_ref[0], place_ref[1], place_ref[2]
    a = a_ref[...]
    high = a.astype(jnp.bfloat16)
    high_ref[...] = high
    low_ref[...] = (a - high.astype(jnp.float32)).astype(jnp.bfloat16)
    for flip, sides in enumerate(((g00_ref, g01_ref), (g10_ref, g11_ref))):
        pair = (z & 1) ^ flip
        for side, g_ref in zip((core, 1 - core), sides, strict=True):
            term = None
            for i in range(g_ref.shape[0]):
                peer = lax.shift_right_logical(z, 1) ^ (((i & 1) << 1) | (i >> 1))
                for half_ref in (high_ref, low_ref):
                    part = jnp.dot(g_ref[i], half_ref[peer], preferred_element_type=jnp.float32)
                    term = part if term is None else term + part
            sum_ref[2 * pair + side] = term
            out_ref[2 * pair + side] = term.astype(out_ref.dtype)
    own_ref[...] = sum_ref[lax.shift_right_logical(y, 1), pl.ds(pl.multiple_of((y & 1) * PADDED, PADDED), PADDED), :]


def term_of(place, grads, gathered):
    smem = pl.BlockSpec(memory_space=pltpu.SMEM)
    vmem = pl.BlockSpec(memory_space=pltpu.VMEM)
    blocks, rows = grads[0].shape[0], grads[0].shape[1]
    columns = gathered.shape[2]
    return pl.pallas_call(
        term_kernel,
        out_shape=(
            jax.ShapeDtypeStruct((blocks, rows, columns), jnp.bfloat16),
            jax.ShapeDtypeStruct((PADDED, columns), jnp.float32),
        ),
        in_specs=[smem] + [vmem] * 5,
        out_specs=(vmem, vmem),
        scratch_shapes=[
            pltpu.VMEM(gathered.shape, jnp.bfloat16),
            pltpu.VMEM(gathered.shape, jnp.bfloat16),
            pltpu.VMEM((blocks, rows, columns), jnp.float32),
        ],
        cost_estimate=pl.CostEstimate(flops=900_000_000, bytes_accessed=3_000_000, transcendentals=0),
        compiler_params=pltpu.CompilerParams(vmem_limit_bytes=32 << 20),
    )(place, *grads, gathered)


def everyone(x, axes, size):
    return lax.all_to_all(jnp.broadcast_to(x[None], (size,) + x.shape), axes, 0, 0)


def on_device(queries, keys_values, grad_rows, doc_ids, tile_list):
    nx, ny, nz = (lax.axis_size(a) for a in ("x", "y", "z"))
    core, x = lax.axis_index("core"), lax.axis_index("x")
    ctx = x * ny + lax.axis_index("y")
    tokens = queries.shape[0]
    swap = [(0, 1), (1, 0)]
    half = nz // nx

    grads = jnp.pad(jnp.transpose(grad_rows).reshape(2, BLOCK, tokens), ((0, 0), (0, PADDED - BLOCK), (0, 0)))
    grads = grads.reshape(2 * PADDED, tokens)
    turn = [(a * nz + half * b + c, b * nz + half * a + c) for a in range(nx) for b in range(nx) for c in range(half)]
    grads = lax.ppermute(grads, ("x", "z"), turn)

    mine = lax.dynamic_slice(keys_values, (core * TILE, lax.axis_index("z") * (2 * DH)), (TILE, 2 * DH))
    own = everyone(mine, "y", ny)
    own = everyone(own, "x", nx).reshape(nx * ny, TILE, 2 * DH)
    other = lax.ppermute(own, "core", swap)

    place = jnp.stack([core, 2 * ctx])
    table, q_t = tables_of(place, tile_list, doc_ids, queries)

    g_own = grads[None]
    for bit in (4, 2):
        came = lax.ppermute(g_own, "z", [(i, i ^ bit) for i in range(nz)])
        g_own = jnp.concatenate([g_own, came], axis=0)
    g_next = lax.ppermute(g_own, "z", [(i, i ^ 1) for i in range(nz)])
    g_other = lax.ppermute(g_own, "core", swap)
    g_both = lax.ppermute(g_next, "core", swap)

    attended, send = attention(place, table, q_t, own, other, nx)
    gathered = lax.all_to_all(send, "x", 0, 0)
    y = lax.axis_index("y")
    place = jnp.stack([core, lax.axis_index("z"), y])
    term, mine = term_of(place, (g_own, g_other, g_next, g_both), gathered)
    parts = lax.all_to_all(term.reshape(ny, PADDED, -1), "y", 0, 0)
    others = lax.broadcasted_iota(jnp.int32, parts.shape, 0) != y
    weight_grad = (mine + jnp.sum(jnp.where(others, parts.astype(jnp.float32), 0.0), axis=0))[:BLOCK]
    return attended, weight_grad


def solution(mesh):
    fine = Mesh(mesh.devices.reshape(4, 8, 8, 2), ("x", "y", "z", "core"))
    ctx, head = ("x", "y"), ("z", "core")
    in_specs = (P(ctx, head), P(ctx, None), P(ctx, head), P(), P())
    out_specs = (P(ctx, head), P(ctx, head))
    return jax.shard_map(on_device, mesh=fine, in_specs=in_specs, out_specs=out_specs, check_vma=False)
```

time: 127 us -> 129 us (1.016)
  the two profiles are of different devices: /device:TPU:2 before, /device:TPU:64 now
where the time goes in v4:
time: 129 us; the launch traced here: 128 us
  starting transfers between devices  44.9 us (35%)
  blocking collectives  36.4 us (28%)
  waiting for transfers between devices  33.5 us (26%)
  Pallas kernels  9.91 us (8%)
  local copies, waits for them, and re-layouts  1.64 us (1%)
    all_to_all x2, blocking collectives, everyone(): lax.all_to_all(jnp.broadcast_to(x[None], (size,) + x.shape), axes, 0, 0)  36.4 us
    ppermute x2, starting transfers between devices, on_device(): came = lax.ppermute(g_own, 'z', [(i, i ^ bit) for i in range(nz)])  25.1 us
    all_to_all x1, waiting for transfers between devices, on_device(): parts = lax.all_to_all(term.reshape(ny, PADDED, -1), 'y', 0, 0)  13.8 us
    all_to_all x1, waiting for transfers between devices, on_device(): gathered = lax.all_to_all(send, 'x', 0, 0)  9.42 us
    ppermute x2, waiting for transfers between devices, on_device(): came = lax.ppermute(g_own, 'z', [(i, i ^ bit) for i in range(nz)])  9 us
    ppermute x1, starting transfers between devices, on_device(): g_next = lax.ppermute(g_own, 'z', [(i, i ^ 1) for i in range(nz)])  5.84 us
    pallas_call x1, Pallas kernels, attention(): pl.pallas_call(attention_kernel, out_shape=(jax.ShapeDtypeStruct((rows, c...  4.86 us
    all_to_all x1, starting transfers between devices, on_device(): gathered = lax.all_to_all(send, 'x', 0, 0)  3.51 us
  transfers between devices with their start and end apart: 9, of which 5 were waited for; matrix products, arithmetic and copies ran while one was open for 0% of the time, Pallas kernels for 6%

profile of v4, /device:TPU:64, one launch (start us, length us, event | category | flops | bytes accessed | tf_op | source)
XLA Modules:
  0.0 128.1 jit_solution(17530579759703434061)
XLA Ops:
  0.6 0.0 dynamic-slice-start
  0.7 0.7 dynamic-slice-done
  1.4 18.8 %all_to_all.20 = bf16[8,128,128]{2,1,0:T(8,128)(2,1)S(1)} all-to-all(bf16[8,128,128]{2,1,0:T(8,128)(2,1)S(1)} %broadcast_in_dim.9), channel_id=1, replica_groups=mesh['x'=4,'y'=8,'z'=8,'core'=2] {'y'}, dimensions={0} | all-to-all | bytes 524288 | tf_op jit(solution)/shard_map/all_to_all | solution.py:198
  20.2 0.2 broadcast_in_dim.20
  20.5 0.0 copy-start.3
  20.5 17.7 %all_to_all.21 = bf16[4,8,128,128]{3,2,1,0:T(8,128)(2,1)S(1)} all-to-all(bf16[4,8,128,128]{3,2,1,0:T(8,128)(2,1)S(1)} %broadcast_in_dim.20), channel_id=1, replica_groups=mesh['x'=4,'y'=8,'z'=8,'core'=2] {'x'}, dimensions={0} | all-to-all | bytes 2097152 | tf_op jit(solution)/shard_map/all_to_all | solution.py:198
  38.1 1.9 %collective-permute-start = (bf16[32,128,128]{2,1,0:T(8,128)(2,1)S(1)}, bf16[32,128,128]{2,1,0:T(8,128)(2,1)S(1)}, u32[]{:S(2)}, u32[]{:S(2)}) collective-permute-start(bf16[32,128,128]{2,1,0:T(8,128)(2,1)S(1)} %bitcast.9), channel_id=1, source_target_pairs={{0,1},{1,0},{2,3},{3,2},{4,5},{5,4},{6,7},{7,6},{8,9},{9,8},{10,11... | collective-permute-start | bytes 3145736 | tf_op jit(solution)/shard_map/ppermute | solution.py:217
  40.1 0.7 collective-permute-start.1
  40.8 0.0 collective-permute-done.1
  40.8 0.0 copy-start
  40.8 22.8 %collective-permute-start.2 = (bf16[1,192,256]{2,1,0:T(8,128)(2,1)S(1)}, bf16[1,192,256]{2,1,0:T(8,128)(2,1)S(1)}, u32[]{:S(2)}, u32[]{:S(2)}) collective-permute-start(bf16[1,192,256]{2,1,0:T(8,128)(2,1)S(1)} %bitcast.11), channel_id=1, source_target_pairs={{0,8},{2,10},{4,12},{6,14},{8,0},{10,2},{12,4},{14,6},{1,9},{3,11}... | collective-permute-start | bytes 294920 | tf_op jit(solution)/shard_map/ppermute | solution.py:224
  63.7 4.8 %collective-permute-done.2 = bf16[1,192,256]{2,1,0:T(8,128)(2,1)S(1)} collective-permute-done((bf16[1,192,256]{2,1,0:T(8,128)(2,1)S(1)}, bf16[1,192,256]{2,1,0:T(8,128)(2,1)S(1)}, u32[]{:S(2)}, u32[]{:S(2)}) %collective-permute-start.2) | collective-permute-done | bytes 98336 | tf_op jit(solution)/shard_map/ppermute | solution.py:224
  68.5 2.3 %collective-permute-start.3 = (bf16[2,192,256]{2,1,0:T(8,128)(2,1)S(1)}, bf16[2,192,256]{2,1,0:T(8,128)(2,1)S(1)}, u32[]{:S(2)}, u32[]{:S(2)}) collective-permute-start(bf16[2,192,256]{2,1,0:T(8,128)(2,1)S(1)} %pad_maximum_fusion.1), channel_id=1, source_target_pairs={{0,4},{2,6},{4,0},{6,2},{8,12},{10,14},{12,8},{14,10},{1,5},{3,7},... | collective-permute-start | bytes 589832 | tf_op jit(solution)/shard_map/ppermute | solution.py:224
  70.8 0.0 copy-start.2
  70.8 0.1 pad_add_fusion.place_ref
  70.9 0.6 copy-done.2
  71.4 2.5 %shard_map.68 = (s32[73]{0:T(128)S(1)}, bf16[2,128,512]{2,1,0:T(8,128)(2,1)S(1)}) custom-call(s32[2]{0:T(128)S(1)} %pad_add_fusion.place_ref, s32[64]{0:T(128)S(1)} %copy-done.2, s32[8192]{0:T(1024)S(1)} %copy-done.1, bf16[256,256]{1,0:T(8,128)(2,1)S(1)} %copy-done), custom_call_target="tpu_custom_call" | custom-call | flops 1000000 | bytes 500000 | tf_op jit(solution)/shard_map/pallas_call | solution.py:51
  73.9 4.2 %collective-permute-done.3 = bf16[2,192,256]{2,1,0:T(8,128)(2,1)S(1)} collective-permute-done((bf16[2,192,256]{2,1,0:T(8,128)(2,1)S(1)}, bf16[2,192,256]{2,1,0:T(8,128)(2,1)S(1)}, u32[]{:S(2)}, u32[]{:S(2)}) %collective-permute-start.3) | collective-permute-done | bytes 196640 | tf_op jit(solution)/shard_map/ppermute | solution.py:224
  78.2 5.8 %collective-permute-start.5 = (bf16[4,192,256]{2,1,0:T(8,128)(2,1)S(1)}, bf16[4,192,256]{2,1,0:T(8,128)(2,1)S(1)}, u32[]{:S(2)}, u32[]{:S(2)}) collective-permute-start(bf16[4,192,256]{2,1,0:T(8,128)(2,1)S(1)} %pad_maximum_fusion.g00_ref), channel_id=1, source_target_pairs={{0,2},{2,0},{4,6},{6,4},{8,10},{10,8},{12,14},{14,12},{1,3},{3,1},... | collective-permute-start | bytes 1179656 | tf_op jit(solution)/shard_map/ppermute | solution.py:226
  84.1 0.0 collective-permute-done.other_ref
  84.1 4.9 %shard_map.69 = (f32[256,256]{1,0:T(8,128)}, f32[4,256,256]{2,1,0:T(8,128)}) custom-call(s32[2]{0:T(128)S(1)} %pad_add_fusion.place_ref, s32[73]{0:T(128)S(1)} %get-tuple-element.8.table_ref, bf16[2,128,512]{2,1,0:T(8,128)(2,1)S(1)} %get-tuple-element.9.q_ref, bf16[32,128,128]{2,1,0:T(8,128)(2,1)S(1)} %bitcast.10, ...), custom_call_target="tpu_custom_call" | custom-call | flops 1200000000 | bytes 4000000 | tf_op jit(solution)/shard_map/pallas_call | solution.py:140
  88.9 3.5 %all-to-all-start.2 = ((f32[4,256,256]{2,1,0:T(8,128)}), f32[4,256,256]{2,1,0:T(8,128)S(1)}, u32[]{:S(2)}, u32[]{:S(2)}) async-start(f32[4,256,256]{2,1,0:T(8,128)} %get-tuple-element.11), calls=%async_computation.2 | async-start | bytes 2097152 | tf_op jit(solution)/shard_map/all_to_all | solution.py:231
  92.4 1.9 %collective-permute-start.4 = (bf16[4,192,256]{2,1,0:T(8,128)(2,1)S(1)}, bf16[4,192,256]{2,1,0:T(8,128)(2,1)S(1)}, u32[]{:S(2)}, u32[]{:S(2)}) collective-permute-start(bf16[4,192,256]{2,1,0:T(8,128)(2,1)S(1)} %pad_maximum_fusion.g00_ref), channel_id=1, source_target_pairs={{0,1},{1,0},{2,3},{3,2},{4,5},{5,4},{6,7},{7,6},{8,9},{9,8},{10,11... | collective-permute-start | bytes 1179656 | tf_op jit(solution)/shard_map/ppermute | solution.py:227
  94.4 2.4 %collective-permute-start.6 = (bf16[4,192,256]{2,1,0:T(8,128)(2,1)S(1)}, bf16[4,192,256]{2,1,0:T(8,128)(2,1)S(1)}, u32[]{:S(2)}, u32[]{:S(2)}) collective-permute-start(bf16[4,192,256]{2,1,0:T(8,128)(2,1)S(1)} %collective-permute-done.5.g10_ref), channel_id=1, source_target_pairs={{0,1},{1,0},{2,3},{3,2},{4,5},{5,4},{6,7},{7,6},{8,9},{9,8},{10,11... | collective-permute-start | bytes 1179656 | tf_op jit(solution)/shard_map/ppermute | solution.py:228
  96.8 0.1 pad_add_fusion.1.place_ref
  96.9 1.2 collective-permute-done.6.g11_ref
  98.1 9.4 %all-to-all-done.2.a_ref = f32[4,256,256]{2,1,0:T(8,128)S(1)} async-done(((f32[4,256,256]{2,1,0:T(8,128)}), f32[4,256,256]{2,1,0:T(8,128)S(1)}, u32[]{:S(2)}, u32[]{:S(2)}) %all-to-all-start.2) | async-done | bytes 1048608 | tf_op jit(solution)/shard_map/all_to_all | solution.py:231
  107.5 2.6 %shard_map.70 = (bf16[4,192,256]{2,1,0:T(8,128)(2,1)}, f32[96,256]{1,0:T(8,128)S(1)}) custom-call(s32[3]{0:T(128)S(1)} %pad_add_fusion.1.place_ref, bf16[4,192,256]{2,1,0:T(8,128)(2,1)S(1)} %pad_maximum_fusion.g00_ref, bf16[4,192,256]{2,1,0:T(8,128)(2,1)S(1)} %collective-permute-done.4.g01_ref, bf16[4,192,256]{2,1,0:T(8,128)(2,1)S(1)} %collective-permute-done.5.g10_ref, ...), custom_call_target="tpu_custom_call" | custom-call | flops 900000000 | bytes 3000000 | tf_op jit(solution)/shard_map/pallas_call | solution.py:179
  110.1 3.5 %all-to-all-start.3 = ((bf16[8,96,256]{2,1,0:T(8,128)(2,1)}), bf16[8,96,256]{2,1,0:T(8,128)(2,1)S(1)}, u32[]{:S(2)}, u32[]{:S(2)}) async-start(bf16[8,96,256]{2,1,0:T(8,128)(2,1)} %bitcast.8), calls=%async_computation.3 | async-start | bytes 786432 | tf_op jit(solution)/shard_map/all_to_all | solution.py:235
  113.6 13.8 %all-to-all-done.3 = bf16[8,96,256]{2,1,0:T(8,128)(2,1)S(1)} async-done(((bf16[8,96,256]{2,1,0:T(8,128)(2,1)}), bf16[8,96,256]{2,1,0:T(8,128)(2,1)S(1)}, u32[]{:S(2)}, u32[]{:S(2)}) %all-to-all-start.3) | async-done | bytes 393248 | tf_op jit(solution)/shard_map/all_to_all | solution.py:235
  127.3 0.1 select_reduce_fusion
  127.5 0.7 slice_add_fusion
  (12 shorter events, 0.1 us)
Async XLA Ops:
  0.6 0.8 dynamic-slice-start
  20.5 19.6 %copy-start.3 = (bf16[256,180]{0,1:T(8,128)(2,1)S(1)}, bf16[256,180]{0,1:T(8,128)(2,1)}, u32[]{:S(2)}) copy-start(bf16[256,180]{0,1:T(8,128)(2,1)} %param.7) | copy-start | bytes 276484
  38.1 45.9 %collective-permute-start = (bf16[32,128,128]{2,1,0:T(8,128)(2,1)S(1)}, bf16[32,128,128]{2,1,0:T(8,128)(2,1)S(1)}, u32[]{:S(2)}, u32[]{:S(2)}) collective-permute-start(bf16[32,128,128]{2,1,0:T(8,128)(2,1)S(1)} %bitcast.9), channel_id=1, source_target_pairs={{0,1},{1,0},{2,3},{3,2},{4,5},{5,4},{6,7},{7,6},{8,9},{9,8},{10,11... | collective-permute-start | bytes 3145736 | tf_op jit(solution)/shard_map/ppermute | solution.py:217
  40.1 0.7 collective-permute-start.1
  40.8 30.1 %copy-start = (bf16[256,256]{1,0:T(8,128)(2,1)S(1)}, bf16[256,256]{1,0:T(8,128)(2,1)}, u32[]{:S(2)}) copy-start(bf16[256,256]{1,0:T(8,128)(2,1)} %q_ref.1) | copy-start | bytes 393220
  40.8 27.6 %collective-permute-start.2 = (bf16[1,192,256]{2,1,0:T(8,128)(2,1)S(1)}, bf16[1,192,256]{2,1,0:T(8,128)(2,1)S(1)}, u32[]{:S(2)}, u32[]{:S(2)}) collective-permute-start(bf16[1,192,256]{2,1,0:T(8,128)(2,1)S(1)} %bitcast.11), channel_id=1, source_target_pairs={{0,8},{2,10},{4,12},{6,14},{8,0},{10,2},{12,4},{14,6},{1,9},{3,11}... | collective-permute-start | bytes 294920 | tf_op jit(solution)/shard_map/ppermute | solution.py:224
  68.4 2.4 %copy-start.1 = (s32[8192]{0:T(1024)S(1)}, s32[8192]{0:T(1024)}, u32[]{:S(2)}) copy-start(s32[8192]{0:T(1024)} %docs_ref.1) | copy-start | bytes 98308
  68.5 9.7 %collective-permute-start.3 = (bf16[2,192,256]{2,1,0:T(8,128)(2,1)S(1)}, bf16[2,192,256]{2,1,0:T(8,128)(2,1)S(1)}, u32[]{:S(2)}, u32[]{:S(2)}) collective-permute-start(bf16[2,192,256]{2,1,0:T(8,128)(2,1)S(1)} %pad_maximum_fusion.1), channel_id=1, source_target_pairs={{0,4},{2,6},{4,0},{6,2},{8,12},{10,14},{12,8},{14,10},{1,5},{3,7},... | collective-permute-start | bytes 589832 | tf_op jit(solution)/shard_map/ppermute | solution.py:224
  70.8 0.7 copy-start.2
  78.2 16.2 %collective-permute-start.5 = (bf16[4,192,256]{2,1,0:T(8,128)(2,1)S(1)}, bf16[4,192,256]{2,1,0:T(8,128)(2,1)S(1)}, u32[]{:S(2)}, u32[]{:S(2)}) collective-permute-start(bf16[4,192,256]{2,1,0:T(8,128)(2,1)S(1)} %pad_maximum_fusion.g00_ref), channel_id=1, source_target_pairs={{0,2},{2,0},{4,6},{6,4},{8,10},{10,8},{12,14},{14,12},{1,3},{3,1},... | collective-permute-start | bytes 1179656 | tf_op jit(solution)/shard_map/ppermute | solution.py:226
  88.9 18.6 %all-to-all-start.2 = ((f32[4,256,256]{2,1,0:T(8,128)}), f32[4,256,256]{2,1,0:T(8,128)S(1)}, u32[]{:S(2)}, u32[]{:S(2)}) async-start(f32[4,256,256]{2,1,0:T(8,128)} %get-tuple-element.11), calls=%async_computation.2 | async-start | bytes 2097152 | tf_op jit(solution)/shard_map/all_to_all | solution.py:231
  92.4 4.4 %collective-permute-start.4 = (bf16[4,192,256]{2,1,0:T(8,128)(2,1)S(1)}, bf16[4,192,256]{2,1,0:T(8,128)(2,1)S(1)}, u32[]{:S(2)}, u32[]{:S(2)}) collective-permute-start(bf16[4,192,256]{2,1,0:T(8,128)(2,1)S(1)} %pad_maximum_fusion.g00_ref), channel_id=1, source_target_pairs={{0,1},{1,0},{2,3},{3,2},{4,5},{5,4},{6,7},{7,6},{8,9},{9,8},{10,11... | collective-permute-start | bytes 1179656 | tf_op jit(solution)/shard_map/ppermute | solution.py:227
  94.4 3.7 %collective-permute-start.6 = (bf16[4,192,256]{2,1,0:T(8,128)(2,1)S(1)}, bf16[4,192,256]{2,1,0:T(8,128)(2,1)S(1)}, u32[]{:S(2)}, u32[]{:S(2)}) collective-permute-start(bf16[4,192,256]{2,1,0:T(8,128)(2,1)S(1)} %collective-permute-done.5.g10_ref), channel_id=1, source_target_pairs={{0,1},{1,0},{2,3},{3,2},{4,5},{5,4},{6,7},{7,6},{8,9},{9,8},{10,11... | collective-permute-start | bytes 1179656 | tf_op jit(solution)/shard_map/ppermute | solution.py:228
  110.1 17.2 %all-to-all-start.3 = ((bf16[8,96,256]{2,1,0:T(8,128)(2,1)}), bf16[8,96,256]{2,1,0:T(8,128)(2,1)S(1)}, u32[]{:S(2)}, u32[]{:S(2)}) async-start(bf16[8,96,256]{2,1,0:T(8,128)(2,1)} %bitcast.8), calls=%async_computation.3 | async-start | bytes 786432 | tf_op jit(solution)/shard_map/all_to_all | solution.py:235

commit v5 on v4

--- a/solution.py
+++ b/solution.py
@@ -61,7 +61,7 @@
     )(place, tiles, docs, queries)
 
 
-def attention_kernel(place_ref, table_ref, q_ref, own_ref, other_ref, out_ref, send_ref, s_ref):
+def attention_kernel(place_ref, table_ref, q_ref, own_ref, other_ref, out_ref, send_ref, s_ref, o_ref, b_ref, sems):
     count = table_ref.shape[0] - DOCS - 1
     core = place_ref[0]
     width = HEADS * TILE
@@ -75,6 +75,7 @@
         at = lax.shift_right_logical(slot, 1)
         return jnp.where((slot & 1) == core, own_ref[at], other_ref[at])
 
+    copies = []
     for part in range(2):
         tile = table_ref[count + DOCS - 1 + part]
         base = tile * TILE
@@ -128,9 +129,16 @@
                 [normed[:, h * TILE:(h + 1) * TILE], normed[:, (h + 1) * TILE:(h + 2) * TILE]], axis=0
             )
             both = jnp.transpose(both)
-            out_ref[part * TILE:(part + 1) * TILE, h * DH:(h + 2) * DH] = both
-            for peer in range(send_ref.shape[0]):
-                send_ref[peer, part * TILE:(part + 1) * TILE, h * DH:(h + 2) * DH] = both
+            o_ref[part, :, h * DH:(h + 2) * DH] = both
+            b_ref[part, :, h * DH:(h + 2) * DH] = both.astype(b_ref.dtype)
+        rows = pl.ds(part * TILE, TILE)
+        copies.append(pltpu.make_async_copy(o_ref.at[part], out_ref.at[rows], sems.at[part, 0]))
+        for peer in range(send_ref.shape[0]):
+            copies.append(pltpu.make_async_copy(b_ref.at[part], send_ref.at[peer, rows], sems.at[part, 1 + peer]))
+        for copy in copies[-1 - send_ref.shape[0]:]:
+            copy.start()
+    for copy in copies:
+        copy.wait()
 
 
 def attention(place, table, q_t, own, other, peers):
@@ -141,57 +149,50 @@
         attention_kernel,
         out_shape=(
             jax.ShapeDtypeStruct((rows, columns), jnp.float32),
-            jax.ShapeDtypeStruct((peers, rows, columns), jnp.float32),
+            jax.ShapeDtypeStruct((peers, rows, columns), jnp.bfloat16),
         ),
         in_specs=[smem, smem, vmem, vmem, vmem],
-        out_specs=(vmem, vmem),
-        scratch_shapes=[pltpu.VMEM((SPAN * TILE, HEADS * TILE), jnp.float32)],
+        out_specs=(pl.BlockSpec(memory_space=pl.ANY), pl.BlockSpec(memory_space=pl.ANY)),
+        scratch_shapes=[
+            pltpu.VMEM((SPAN * TILE, HEADS * TILE), jnp.float32),
+            pltpu.VMEM((2, TILE, columns), jnp.float32),
+            pltpu.VMEM((2, TILE, columns), jnp.bfloat16),
+            pltpu.SemaphoreType.DMA((2, 1 + peers)),
+        ],
         cost_estimate=pl.CostEstimate(flops=1_200_000_000, bytes_accessed=4_000_000, transcendentals=2_200_000),
         compiler_params=pltpu.CompilerParams(vmem_limit_bytes=32 << 20),
     )(place, table, q_t, own, other)
 
 
-def term_kernel(place_ref, g00_ref, g01_ref, g10_ref, g11_ref, a_ref, out_ref, own_ref, high_ref, low_ref, sum_ref):
-    core, z, y = place_ref[0], place_ref[1], place_ref[2]
-    a = a_ref[...]
-    high = a.astype(jnp.bfloat16)
-    high_ref[...] = high
-    low_ref[...] = (a - high.astype(jnp.float32)).astype(jnp.bfloat16)
+def term_kernel(place_ref, g00_ref, g01_ref, g10_ref, g11_ref, a_ref, own_ref, out_ref):
+    core, z, x = place_ref[0], place_ref[1], place_ref[2]
+    zx = lax.shift_right_logical(z, 1)
+    apart = zx ^ x
+    at = ((apart & 1) << 1) | lax.shift_right_logical(apart, 1)
+    a = own_ref[...]
+    low = (a - a.astype(jnp.bfloat16).astype(jnp.float32)).astype(jnp.bfloat16)
     for flip, sides in enumerate(((g00_ref, g01_ref), (g10_ref, g11_ref))):
         pair = (z & 1) ^ flip
         for side, g_ref in zip((core, 1 - core), sides, strict=True):
-            term = None
+            term = jnp.dot(g_ref[at], low, preferred_element_type=jnp.float32)
             for i in range(g_ref.shape[0]):
-                peer = lax.shift_right_logical(z, 1) ^ (((i & 1) << 1) | (i >> 1))
-                for half_ref in (high_ref, low_ref):
-                    part = jnp.dot(g_ref[i], half_ref[peer], preferred_element_type=jnp.float32)
-                    term = part if term is None else term + part
-            sum_ref[2 * pair + side] = term
-            out_ref[2 * pair + side] = term.astype(out_ref.dtype)
-    own_ref[...] = sum_ref[lax.shift_right_logical(y, 1), pl.ds(pl.multiple_of((y & 1) * PADDED, PADDED), PADDED), :]
-
-
-def term_of(place, grads, gathered):
+                peer = zx ^ (((i & 1) << 1) | (i >> 1))
+                term = term + jnp.dot(g_ref[i], a_ref[peer], preferred_element_type=jnp.float32)
+            out_ref[2 * pair + side] = term
+
+
+def term_of(place, grads, gathered, attended):
     smem = pl.BlockSpec(memory_space=pltpu.SMEM)
     vmem = pl.BlockSpec(memory_space=pltpu.VMEM)
     blocks, rows = grads[0].shape[0], grads[0].shape[1]
-    columns = gathered.shape[2]
     return pl.pallas_call(
         term_kernel,
-        out_shape=(
-            jax.ShapeDtypeStruct((blocks, rows, columns), jnp.bfloat16),
-            jax.ShapeDtypeStruct((PADDED, columns), jnp.float32),
-        ),
-        in_specs=[smem] + [vmem] * 5,
-        out_specs=(vmem, vmem),
-        scratch_shapes=[
-            pltpu.VMEM(gathered.shape, jnp.bfloat16),
-            pltpu.VMEM(gathered.shape, jnp.bfloat16),
-            pltpu.VMEM((blocks, rows, columns), jnp.float32),
-        ],
-        cost_estimate=pl.CostEstimate(flops=900_000_000, bytes_accessed=3_000_000, transcendentals=0),
+        out_shape=jax.ShapeDtypeStruct((blocks, rows, attended.shape[1]), jnp.float32),
+        in_specs=[smem] + [vmem] * 6,
+        out_specs=vmem,
+        cost_estimate=pl.CostEstimate(flops=500_000_000, bytes_accessed=3_000_000, transcendentals=0),
         compiler_params=pltpu.CompilerParams(vmem_limit_bytes=32 << 20),
-    )(place, *grads, gathered)
+    )(place, *grads, gathered, attended)
 
 
 def everyone(x, axes, size):
@@ -229,12 +230,10 @@
 
     attended, send = attention(place, table, q_t, own, other, nx)
     gathered = lax.all_to_all(send, "x", 0, 0)
-    y = lax.axis_index("y")
-    place = jnp.stack([core, lax.axis_index("z"), y])
-    term, mine = term_of(place, (g_own, g_other, g_next, g_both), gathered)
+    place = jnp.stack([core, lax.axis_index("z"), x])
+    term = term_of(place, (g_own, g_other, g_next, g_both), gathered, attended)
     parts = lax.all_to_all(term.reshape(ny, PADDED, -1), "y", 0, 0)
-    others = lax.broadcasted_iota(jnp.int32, parts.shape, 0) != y
-    weight_grad = (mine + jnp.sum(jnp.where(others, parts.astype(jnp.float32), 0.0), axis=0))[:BLOCK]
+    weight_grad = jnp.sum(parts, axis=0)[:BLOCK]
     return attended, weight_grad
 
 

time: 129 us -> 144 us (1.12)
  the two profiles are of different devices: /device:TPU:64 before, /device:TPU:2 now
where the time goes in v5:
time: 144 us
  blocking collectives  61.7 us (43%)
  starting transfers between devices  44.9 us (31%)
  waiting for transfers between devices  24.8 us (17%)
  Pallas kernels  9 us (6%)
  local copies, waits for them, and re-layouts  1.64 us (1%)
    all_to_all x2, blocking collectives, everyone(): lax.all_to_all(jnp.broadcast_to(x[None], (size,) + x.shape), axes, 0, 0)  35.5 us
    all_to_all x1, blocking collectives, on_device(): parts = lax.all_to_all(term.reshape(ny, PADDED, -1), 'y', 0, 0)  26.2 us
    ppermute x2, starting transfers between devices, on_device(): came = lax.ppermute(g_own, 'z', [(i, i ^ bit) for i in range(nz)])  16.2 us
    all_to_all x1, starting transfers between devices, on_device(): gathered = lax.all_to_all(send, 'x', 0, 0)  8.94 us
    all_to_all x1, waiting for transfers between devices, on_device(): gathered = lax.all_to_all(send, 'x', 0, 0)  8.89 us
    ppermute x2, waiting for transfers between devices, on_device(): came = lax.ppermute(g_own, 'z', [(i, i ^ bit) for i in range(nz)])  7.23 us
    ppermute x1, starting transfers between devices, on_device(): g_next = lax.ppermute(g_own, 'z', [(i, i ^ 1) for i in range(nz)])  7.01 us
    ppermute x1, starting transfers between devices, on_device(): grads = lax.ppermute(grads, ('x', 'z'), turn)  6.99 us
  transfers between devices with their start and end apart: 8, of which 5 were waited for; matrix products, arithmetic and copies ran while one was open for 0% of the time, Pallas kernels for 5%

profile of v5, /device:TPU:2, one launch (start us, length us, event | category | flops | bytes accessed | tf_op | source)
XLA Modules:
  0.0 143.7 jit_solution(14838250059581805612)
XLA Ops:
  0.6 0.0 dynamic-slice-start
  0.7 0.7 dynamic-slice-done
  1.4 18.8 %all_to_all.20 = bf16[8,128,128]{2,1,0:T(8,128)(2,1)S(1)} all-to-all(bf16[8,128,128]{2,1,0:T(8,128)(2,1)S(1)} %broadcast_in_dim.6), channel_id=1, replica_groups=mesh['x'=4,'y'=8,'z'=8,'core'=2] {'y'}, dimensions={0} | all-to-all | bytes 524288 | tf_op jit(solution)/shard_map/all_to_all | solution.py:199
  20.2 0.2 broadcast_in_dim.7
  20.5 0.0 copy-start.4
  20.5 16.7 %all_to_all.21 = bf16[4,8,128,128]{3,2,1,0:T(8,128)(2,1)S(1)} all-to-all(bf16[4,8,128,128]{3,2,1,0:T(8,128)(2,1)S(1)} %broadcast_in_dim.7), channel_id=1, replica_groups=mesh['x'=4,'y'=8,'z'=8,'core'=2] {'x'}, dimensions={0} | all-to-all | bytes 2097152 | tf_op jit(solution)/shard_map/all_to_all | solution.py:199
  37.2 1.9 %collective-permute-start = (bf16[32,128,128]{2,1,0:T(8,128)(2,1)S(1)}, bf16[32,128,128]{2,1,0:T(8,128)(2,1)}, u32[]{:S(2)}, u32[]{:S(2)}) collective-permute-start(bf16[32,128,128]{2,1,0:T(8,128)(2,1)S(1)} %bitcast.11), channel_id=1, source_target_pairs={{0,1},{1,0},{2,3},{3,2},{4,5},{5,4},{6,7},{7,6},{8,9},{9,8},{10,11... | collective-permute-start | bytes 3145736 | tf_op jit(solution)/shard_map/ppermute | solution.py:218
  39.2 7.0 %collective-permute-start.1 = (bf16[192,256]{1,0:T(8,128)(2,1)S(1)}, bf16[192,256]{1,0:T(8,128)(2,1)S(1)}, u32[]{:S(2)}, u32[]{:S(2)}) collective-permute-start(bf16[192,256]{1,0:T(8,128)(2,1)S(1)} %bitcast.17), channel_id=1, source_target_pairs={{0,0},{2,2},{4,128},{6,130},{8,256},{10,258},{12,384},{14,386},{12... | collective-permute-start | bytes 294920 | tf_op jit(solution)/shard_map/ppermute | solution.py:213
  46.2 5.5 %collective-permute-done.1 = bf16[192,256]{1,0:T(8,128)(2,1)S(1)} collective-permute-done((bf16[192,256]{1,0:T(8,128)(2,1)S(1)}, bf16[192,256]{1,0:T(8,128)(2,1)S(1)}, u32[]{:S(2)}, u32[]{:S(2)}) %collective-permute-start.1) | collective-permute-done | bytes 98336 | tf_op jit(solution)/shard_map/ppermute | solution.py:213
  51.7 8.6 %collective-permute-start.2 = (bf16[1,192,256]{2,1,0:T(8,128)(2,1)S(1)}, bf16[1,192,256]{2,1,0:T(8,128)(2,1)S(1)}, u32[]{:S(2)}, u32[]{:S(2)}) collective-permute-start(bf16[1,192,256]{2,1,0:T(8,128)(2,1)S(1)} %bitcast.13), channel_id=1, source_target_pairs={{0,8},{2,10},{4,12},{6,14},{8,0},{10,2},{12,4},{14,6},{1,9},{3,11}... | collective-permute-start | bytes 294920 | tf_op jit(solution)/shard_map/ppermute | solution.py:225
  60.3 2.6 %collective-permute-done.2 = bf16[1,192,256]{2,1,0:T(8,128)(2,1)S(1)} collective-permute-done((bf16[1,192,256]{2,1,0:T(8,128)(2,1)S(1)}, bf16[1,192,256]{2,1,0:T(8,128)(2,1)S(1)}, u32[]{:S(2)}, u32[]{:S(2)}) %collective-permute-start.2) | collective-permute-done | bytes 98336 | tf_op jit(solution)/shard_map/ppermute | solution.py:225
  62.9 0.0 copy-start.1
  62.9 7.6 %collective-permute-start.3 = (bf16[2,192,256]{2,1,0:T(8,128)(2,1)S(1)}, bf16[2,192,256]{2,1,0:T(8,128)(2,1)S(1)}, u32[]{:S(2)}, u32[]{:S(2)}) collective-permute-start(bf16[2,192,256]{2,1,0:T(8,128)(2,1)S(1)} %pad_maximum_fusion.1), channel_id=1, source_target_pairs={{0,4},{2,6},{4,0},{6,2},{8,12},{10,14},{12,8},{14,10},{1,5},{3,7},... | collective-permute-start | bytes 589832 | tf_op jit(solution)/shard_map/ppermute | solution.py:225
  70.5 4.6 %collective-permute-done.3 = bf16[2,192,256]{2,1,0:T(8,128)(2,1)S(1)} collective-permute-done((bf16[2,192,256]{2,1,0:T(8,128)(2,1)S(1)}, bf16[2,192,256]{2,1,0:T(8,128)(2,1)S(1)}, u32[]{:S(2)}, u32[]{:S(2)}) %collective-permute-start.3) | collective-permute-done | bytes 196640 | tf_op jit(solution)/shard_map/ppermute | solution.py:225
  75.2 7.0 %collective-permute-start.5 = (bf16[4,192,256]{2,1,0:T(8,128)(2,1)S(1)}, bf16[4,192,256]{2,1,0:T(8,128)(2,1)S(1)}, u32[]{:S(2)}, u32[]{:S(2)}) collective-permute-start(bf16[4,192,256]{2,1,0:T(8,128)(2,1)S(1)} %pad_maximum_fusion.g00_ref), channel_id=1, source_target_pairs={{0,2},{2,0},{4,6},{6,4},{8,10},{10,8},{12,14},{14,12},{1,3},{3,1},... | collective-permute-start | bytes 1179656 | tf_op jit(solution)/shard_map/ppermute | solution.py:227
  82.3 0.0 copy-start.3
  82.3 0.1 pad_add_fusion.place_ref
  82.3 0.6 copy-done.3
  82.9 2.5 %shard_map.68 = (s32[73]{0:T(128)S(1)}, bf16[2,128,512]{2,1,0:T(8,128)(2,1)S(1)}) custom-call(s32[2]{0:T(128)S(1)} %pad_add_fusion.place_ref, s32[64]{0:T(128)S(1)} %copy-done.3, s32[8192]{0:T(1024)S(1)} %copy-done.2, bf16[256,256]{1,0:T(8,128)(2,1)S(1)} %copy-done.1), custom_call_target="tpu_custom_call" | custom-call | flops 1000000 | bytes 500000 | tf_op jit(solution)/shard_map/pallas_call | solution.py:51
  85.4 1.9 %collective-permute-start.4 = (bf16[4,192,256]{2,1,0:T(8,128)(2,1)S(1)}, bf16[4,192,256]{2,1,0:T(8,128)(2,1)S(1)}, u32[]{:S(2)}, u32[]{:S(2)}) collective-permute-start(bf16[4,192,256]{2,1,0:T(8,128)(2,1)S(1)} %pad_maximum_fusion.g00_ref), channel_id=1, source_target_pairs={{0,1},{1,0},{2,3},{3,2},{4,5},{5,4},{6,7},{7,6},{8,9},{9,8},{10,11... | collective-permute-start | bytes 1179656 | tf_op jit(solution)/shard_map/ppermute | solution.py:228
  87.3 3.1 %collective-permute-done.5.g10_ref = bf16[4,192,256]{2,1,0:T(8,128)(2,1)S(1)} collective-permute-done((bf16[4,192,256]{2,1,0:T(8,128)(2,1)S(1)}, bf16[4,192,256]{2,1,0:T(8,128)(2,1)S(1)}, u32[]{:S(2)}, u32[]{:S(2)}) %collective-permute-start.5) | collective-permute-done | bytes 393248 | tf_op jit(solution)/shard_map/ppermute | solution.py:227
  90.5 1.9 %collective-permute-start.6 = (bf16[4,192,256]{2,1,0:T(8,128)(2,1)S(1)}, bf16[4,192,256]{2,1,0:T(8,128)(2,1)S(1)}, u32[]{:S(2)}, u32[]{:S(2)}) collective-permute-start(bf16[4,192,256]{2,1,0:T(8,128)(2,1)S(1)} %collective-permute-done.5.g10_ref), channel_id=1, source_target_pairs={{0,1},{1,0},{2,3},{3,2},{4,5},{5,4},{6,7},{7,6},{8,9},{9,8},{10,11... | collective-permute-start | bytes 1179656 | tf_op jit(solution)/shard_map/ppermute | solution.py:229
  92.4 0.0 collective-permute-done.other_ref
  92.4 5.3 %shard_map.69 = (f32[256,256]{1,0:T(8,128)}, bf16[4,256,256]{2,1,0:T(8,128)(2,1)}) custom-call(s32[2]{0:T(128)S(1)} %pad_add_fusion.place_ref, s32[73]{0:T(128)S(1)} %get-tuple-element.6.table_ref, bf16[2,128,512]{2,1,0:T(8,128)(2,1)S(1)} %get-tuple-element.7.q_ref, bf16[32,128,128]{2,1,0:T(8,128)(2,1)S(1)} %bitcast.12, ...), custom_call_target="tpu_custom_call" | custom-call | flops 1200000000 | bytes 4000000 | tf_op jit(solution)/shard_map/pallas_call | solution.py:148
  97.7 0.0 copy-start
  97.7 8.9 %all-to-all-start.2 = ((bf16[4,256,256]{2,1,0:T(8,128)(2,1)}), bf16[4,256,256]{2,1,0:T(8,128)(2,1)S(1)}, u32[]{:S(2)}, u32[]{:S(2)}) async-start(bf16[4,256,256]{2,1,0:T(8,128)(2,1)} %get-tuple-element.9), calls=%async_computation.2 | async-start | bytes 1048576 | tf_op jit(solution)/shard_map/all_to_all | solution.py:232
  106.6 0.1 pad_add_fusion.1.place_ref
  106.7 0.0 collective-permute-done.4.g01_ref
  106.7 8.9 %all-to-all-done.2.a_ref = bf16[4,256,256]{2,1,0:T(8,128)(2,1)S(1)} async-done(((bf16[4,256,256]{2,1,0:T(8,128)(2,1)}), bf16[4,256,256]{2,1,0:T(8,128)(2,1)S(1)}, u32[]{:S(2)}, u32[]{:S(2)}) %all-to-all-start.2) | async-done | bytes 524320 | tf_op jit(solution)/shard_map/all_to_all | solution.py:232
  115.6 1.2 shard_map.70
  116.8 26.2 %all_to_all.22 = f32[8,96,256]{2,1,0:T(8,128)S(1)} all-to-all(f32[8,96,256]{2,1,0:T(8,128)S(1)} %bitcast.10), channel_id=1, replica_groups=mesh['x'=4,'y'=8,'z'=8,'core'=2] {'y'}, dimensions={0} | all-to-all | bytes 1572864 | tf_op jit(solution)/shard_map/all_to_all | solution.py:235
  143.0 0.7 reduce_sum.9
  (11 shorter events, 0.1 us)
Async XLA Ops:
  0.6 0.8 dynamic-slice-start
  20.5 18.7 %copy-start.4 = (bf16[256,180]{0,1:T(8,128)(2,1)S(1)}, bf16[256,180]{0,1:T(8,128)(2,1)}, u32[]{:S(2)}) copy-start(bf16[256,180]{0,1:T(8,128)(2,1)} %param.7) | copy-start | bytes 276484
  37.2 55.2 %collective-permute-start = (bf16[32,128,128]{2,1,0:T(8,128)(2,1)S(1)}, bf16[32,128,128]{2,1,0:T(8,128)(2,1)}, u32[]{:S(2)}, u32[]{:S(2)}) collective-permute-start(bf16[32,128,128]{2,1,0:T(8,128)(2,1)S(1)} %bitcast.11), channel_id=1, source_target_pairs={{0,1},{1,0},{2,3},{3,2},{4,5},{5,4},{6,7},{7,6},{8,9},{9,8},{10,11... | collective-permute-start | bytes 3145736 | tf_op jit(solution)/shard_map/ppermute | solution.py:218
  39.2 12.5 %collective-permute-start.1 = (bf16[192,256]{1,0:T(8,128)(2,1)S(1)}, bf16[192,256]{1,0:T(8,128)(2,1)S(1)}, u32[]{:S(2)}, u32[]{:S(2)}) collective-permute-start(bf16[192,256]{1,0:T(8,128)(2,1)S(1)} %bitcast.17), channel_id=1, source_target_pairs={{0,0},{2,2},{4,128},{6,130},{8,256},{10,258},{12,384},{14,386},{12... | collective-permute-start | bytes 294920 | tf_op jit(solution)/shard_map/ppermute | solution.py:213
  51.7 11.1 %collective-permute-start.2 = (bf16[1,192,256]{2,1,0:T(8,128)(2,1)S(1)}, bf16[1,192,256]{2,1,0:T(8,128)(2,1)S(1)}, u32[]{:S(2)}, u32[]{:S(2)}) collective-permute-start(bf16[1,192,256]{2,1,0:T(8,128)(2,1)S(1)} %bitcast.13), channel_id=1, source_target_pairs={{0,8},{2,10},{4,12},{6,14},{8,0},{10,2},{12,4},{14,6},{1,9},{3,11}... | collective-permute-start | bytes 294920 | tf_op jit(solution)/shard_map/ppermute | solution.py:225
  62.9 19.5 %copy-start.1 = (bf16[256,256]{1,0:T(8,128)(2,1)S(1)}, bf16[256,256]{1,0:T(8,128)(2,1)}, u32[]{:S(2)}) copy-start(bf16[256,256]{1,0:T(8,128)(2,1)} %q_ref.1) | copy-start | bytes 393220
  62.9 12.3 %collective-permute-start.3 = (bf16[2,192,256]{2,1,0:T(8,128)(2,1)S(1)}, bf16[2,192,256]{2,1,0:T(8,128)(2,1)S(1)}, u32[]{:S(2)}, u32[]{:S(2)}) collective-permute-start(bf16[2,192,256]{2,1,0:T(8,128)(2,1)S(1)} %pad_maximum_fusion.1), channel_id=1, source_target_pairs={{0,4},{2,6},{4,0},{6,2},{8,12},{10,14},{12,8},{14,10},{1,5},{3,7},... | collective-permute-start | bytes 589832 | tf_op jit(solution)/shard_map/ppermute | solution.py:225
  75.2 7.2 %copy-start.2 = (s32[8192]{0:T(1024)S(1)}, s32[8192]{0:T(1024)}, u32[]{:S(2)}) copy-start(s32[8192]{0:T(1024)} %docs_ref.1) | copy-start | bytes 98308
  75.2 15.2 %collective-permute-start.5 = (bf16[4,192,256]{2,1,0:T(8,128)(2,1)S(1)}, bf16[4,192,256]{2,1,0:T(8,128)(2,1)S(1)}, u32[]{:S(2)}, u32[]{:S(2)}) collective-permute-start(bf16[4,192,256]{2,1,0:T(8,128)(2,1)S(1)} %pad_maximum_fusion.g00_ref), channel_id=1, source_target_pairs={{0,2},{2,0},{4,6},{6,4},{8,10},{10,8},{12,14},{14,12},{1,3},{3,1},... | collective-permute-start | bytes 1179656 | tf_op jit(solution)/shard_map/ppermute | solution.py:227
  82.3 0.7 copy-start.3
  85.4 21.3 %collective-permute-start.4 = (bf16[4,192,256]{2,1,0:T(8,128)(2,1)S(1)}, bf16[4,192,256]{2,1,0:T(8,128)(2,1)S(1)}, u32[]{:S(2)}, u32[]{:S(2)}) collective-permute-start(bf16[4,192,256]{2,1,0:T(8,128)(2,1)S(1)} %pad_maximum_fusion.g00_ref), channel_id=1, source_target_pairs={{0,1},{1,0},{2,3},{3,2},{4,5},{5,4},{6,7},{7,6},{8,9},{9,8},{10,11... | collective-permute-start | bytes 1179656 | tf_op jit(solution)/shard_map/ppermute | solution.py:228
  90.5 16.2 %collective-permute-start.6 = (bf16[4,192,256]{2,1,0:T(8,128)(2,1)S(1)}, bf16[4,192,256]{2,1,0:T(8,128)(2,1)S(1)}, u32[]{:S(2)}, u32[]{:S(2)}) collective-permute-start(bf16[4,192,256]{2,1,0:T(8,128)(2,1)S(1)} %collective-permute-done.5.g10_ref), channel_id=1, source_target_pairs={{0,1},{1,0},{2,3},{3,2},{4,5},{5,4},{6,7},{7,6},{8,9},{9,8},{10,11... | collective-permute-start | bytes 1179656 | tf_op jit(solution)/shard_map/ppermute | solution.py:229
  97.7 17.9 %copy-start = (f32[256,256]{1,0:T(8,128)S(1)}, f32[256,256]{1,0:T(8,128)}, u32[]{:S(2)}) copy-start(f32[256,256]{1,0:T(8,128)} %get-tuple-element.4.own_ref) | copy-start | bytes 786436
  97.7 17.9 %all-to-all-start.2 = ((bf16[4,256,256]{2,1,0:T(8,128)(2,1)}), bf16[4,256,256]{2,1,0:T(8,128)(2,1)S(1)}, u32[]{:S(2)}, u32[]{:S(2)}) async-start(bf16[4,256,256]{2,1,0:T(8,128)(2,1)} %get-tuple-element.9), calls=%async_computation.2 | async-start | bytes 1048576 | tf_op jit(solution)/shard_map/all_to_all | solution.py:232

commit v6 on v5

--- a/solution.py
+++ b/solution.py
@@ -72,8 +72,9 @@
 
     def pick(tile):
         slot = table_ref[tile]
-        at = lax.shift_right_logical(slot, 1)
-        return jnp.where((slot & 1) == core, own_ref[at], other_ref[at])
+        ctx = lax.shift_right_logical(slot, 1)
+        y, x = lax.rem(ctx, own_ref.shape[0]), lax.div(ctx, own_ref.shape[0])
+        return jnp.where((slot & 1) == core, own_ref[y, x], other_ref[y, x])
 
     copies = []
     for part in range(2):
@@ -213,8 +214,8 @@
     grads = lax.ppermute(grads, ("x", "z"), turn)
 
     mine = lax.dynamic_slice(keys_values, (core * TILE, lax.axis_index("z") * (2 * DH)), (TILE, 2 * DH))
-    own = everyone(mine, "y", ny)
-    own = everyone(own, "x", nx).reshape(nx * ny, TILE, 2 * DH)
+    own = everyone(mine, "x", nx)
+    own = everyone(own, "y", ny)
     other = lax.ppermute(own, "core", swap)
 
     place = jnp.stack([core, 2 * ctx])

time: 144 us -> 153 us (1.062)
  blocking collectives: 61.7 us -> 70.4 us
    all_to_all x2, blocking collectives: 35.5 us -> 43.5 us  [everyone(): lax.all_to_all(jnp.broadcast_to(x[None], (size,) + x.shape), axes, 0, 0)]
where the time goes in v6:
time: 153 us; the launch traced here: 152 us
  blocking collectives  70.4 us (46%)
  starting transfers between devices  44.9 us (29%)
  waiting for transfers between devices  24.8 us (16%)
  Pallas kernels  8.97 us (6%)
  local copies, waits for them, and re-layouts  1.63 us (1%)
    all_to_all x2, blocking collectives, everyone(): lax.all_to_all(jnp.broadcast_to(x[None], (size,) + x.shape), axes, 0, 0)  43.5 us
    all_to_all x1, blocking collectives, on_device(): parts = lax.all_to_all(term.reshape(ny, PADDED, -1), 'y', 0, 0)  26.9 us
    ppermute x2, starting transfers between devices, on_device(): came = lax.ppermute(g_own, 'z', [(i, i ^ bit) for i in range(nz)])  16.2 us
    all_to_all x1, starting transfers between devices, on_device(): gathered = lax.all_to_all(send, 'x', 0, 0)  8.97 us
    all_to_all x1, waiting for transfers between devices, on_device(): gathered = lax.all_to_all(send, 'x', 0, 0)  8.89 us
    ppermute x2, waiting for transfers between devices, on_device(): came = lax.ppermute(g_own, 'z', [(i, i ^ bit) for i in range(nz)])  7.23 us
    ppermute x1, starting transfers between devices, on_device(): g_next = lax.ppermute(g_own, 'z', [(i, i ^ 1) for i in range(nz)])  7.01 us
    ppermute x1, starting transfers between devices, on_device(): grads = lax.ppermute(grads, ('x', 'z'), turn)  6.99 us
  transfers between devices with their start and end apart: 8, of which 5 were waited for; matrix products, arithmetic and copies ran while one was open for 0% of the time, Pallas kernels for 5%

profile of v6, /device:TPU:2, one launch (start us, length us, event | category | flops | bytes accessed | tf_op | source)
XLA Modules:
  0.0 152.4 jit_solution(12162218658730524271)
XLA Ops:
  0.6 0.0 dynamic-slice-start
  0.7 0.7 dynamic-slice-done
  1.4 12.8 %all_to_all.20 = bf16[4,128,128]{2,1,0:T(8,128)(2,1)S(1)} all-to-all(bf16[4,128,128]{2,1,0:T(8,128)(2,1)S(1)} %broadcast_in_dim.6), channel_id=1, replica_groups=mesh['x'=4,'y'=8,'z'=8,'core'=2] {'x'}, dimensions={0} | all-to-all | bytes 262144 | tf_op jit(solution)/shard_map/all_to_all | solution.py:200
  14.2 0.2 broadcast_in_dim.7
  14.4 0.0 copy-start.4
  14.5 30.7 %all_to_all.21.own_ref = bf16[8,4,128,128]{3,2,1,0:T(8,128)(2,1)S(1)} all-to-all(bf16[8,4,128,128]{3,2,1,0:T(8,128)(2,1)S(1)} %broadcast_in_dim.7), channel_id=1, replica_groups=mesh['x'=4,'y'=8,'z'=8,'core'=2] {'y'}, dimensions={0} | all-to-all | bytes 2097152 | tf_op jit(solution)/shard_map/all_to_all | solution.py:200
  45.1 1.9 %collective-permute-start = (bf16[8,4,128,128]{3,2,1,0:T(8,128)(2,1)S(1)}, bf16[8,4,128,128]{3,2,1,0:T(8,128)(2,1)}, u32[]{:S(2)}, u32[]{:S(2)}) collective-permute-start(bf16[8,4,128,128]{3,2,1,0:T(8,128)(2,1)S(1)} %all_to_all.21.own_ref), channel_id=1, source_target_pairs={{0,1},{1,0},{2,3},{3,2},{4,5},{5,4},{6,7},{7,6},{8,9},{9,8},{10,11... | collective-permute-start | bytes 3145736 | tf_op jit(solution)/shard_map/ppermute | solution.py:219
  47.1 7.0 %collective-permute-start.1 = (bf16[192,256]{1,0:T(8,128)(2,1)S(1)}, bf16[192,256]{1,0:T(8,128)(2,1)S(1)}, u32[]{:S(2)}, u32[]{:S(2)}) collective-permute-start(bf16[192,256]{1,0:T(8,128)(2,1)S(1)} %bitcast.14), channel_id=1, source_target_pairs={{0,0},{2,2},{4,128},{6,130},{8,256},{10,258},{12,384},{14,386},{12... | collective-permute-start | bytes 294920 | tf_op jit(solution)/shard_map/ppermute | solution.py:214
  54.1 5.5 %collective-permute-done.1 = bf16[192,256]{1,0:T(8,128)(2,1)S(1)} collective-permute-done((bf16[192,256]{1,0:T(8,128)(2,1)S(1)}, bf16[192,256]{1,0:T(8,128)(2,1)S(1)}, u32[]{:S(2)}, u32[]{:S(2)}) %collective-permute-start.1) | collective-permute-done | bytes 98336 | tf_op jit(solution)/shard_map/ppermute | solution.py:214
  59.7 8.6 %collective-permute-start.2 = (bf16[1,192,256]{2,1,0:T(8,128)(2,1)S(1)}, bf16[1,192,256]{2,1,0:T(8,128)(2,1)S(1)}, u32[]{:S(2)}, u32[]{:S(2)}) collective-permute-start(bf16[1,192,256]{2,1,0:T(8,128)(2,1)S(1)} %bitcast.10), channel_id=1, source_target_pairs={{0,8},{2,10},{4,12},{6,14},{8,0},{10,2},{12,4},{14,6},{1,9},{3,11}... | collective-permute-start | bytes 294920 | tf_op jit(solution)/shard_map/ppermute | solution.py:226
  68.2 2.6 %collective-permute-done.2 = bf16[1,192,256]{2,1,0:T(8,128)(2,1)S(1)} collective-permute-done((bf16[1,192,256]{2,1,0:T(8,128)(2,1)S(1)}, bf16[1,192,256]{2,1,0:T(8,128)(2,1)S(1)}, u32[]{:S(2)}, u32[]{:S(2)}) %collective-permute-start.2) | collective-permute-done | bytes 98336 | tf_op jit(solution)/shard_map/ppermute | solution.py:226
  70.8 0.0 copy-start.1
  70.9 7.6 %collective-permute-start.3 = (bf16[2,192,256]{2,1,0:T(8,128)(2,1)S(1)}, bf16[2,192,256]{2,1,0:T(8,128)(2,1)S(1)}, u32[]{:S(2)}, u32[]{:S(2)}) collective-permute-start(bf16[2,192,256]{2,1,0:T(8,128)(2,1)S(1)} %pad_maximum_fusion.1), channel_id=1, source_target_pairs={{0,4},{2,6},{4,0},{6,2},{8,12},{10,14},{12,8},{14,10},{1,5},{3,7},... | collective-permute-start | bytes 589832 | tf_op jit(solution)/shard_map/ppermute | solution.py:226
  78.5 4.6 %collective-permute-done.3 = bf16[2,192,256]{2,1,0:T(8,128)(2,1)S(1)} collective-permute-done((bf16[2,192,256]{2,1,0:T(8,128)(2,1)S(1)}, bf16[2,192,256]{2,1,0:T(8,128)(2,1)S(1)}, u32[]{:S(2)}, u32[]{:S(2)}) %collective-permute-start.3) | collective-permute-done | bytes 196640 | tf_op jit(solution)/shard_map/ppermute | solution.py:226
  83.2 7.0 %collective-permute-start.5 = (bf16[4,192,256]{2,1,0:T(8,128)(2,1)S(1)}, bf16[4,192,256]{2,1,0:T(8,128)(2,1)S(1)}, u32[]{:S(2)}, u32[]{:S(2)}) collective-permute-start(bf16[4,192,256]{2,1,0:T(8,128)(2,1)S(1)} %pad_maximum_fusion.g00_ref), channel_id=1, source_target_pairs={{0,2},{2,0},{4,6},{6,4},{8,10},{10,8},{12,14},{14,12},{1,3},{3,1},... | collective-permute-start | bytes 1179656 | tf_op jit(solution)/shard_map/ppermute | solution.py:228
  90.2 0.0 copy-start.3
  90.2 0.1 pad_add_fusion.place_ref
  90.3 0.6 copy-done.3
  90.9 2.5 %shard_map.68 = (s32[73]{0:T(128)S(1)}, bf16[2,128,512]{2,1,0:T(8,128)(2,1)S(1)}) custom-call(s32[2]{0:T(128)S(1)} %pad_add_fusion.place_ref, s32[64]{0:T(128)S(1)} %copy-done.3, s32[8192]{0:T(1024)S(1)} %copy-done.2, bf16[256,256]{1,0:T(8,128)(2,1)S(1)} %copy-done.1), custom_call_target="tpu_custom_call" | custom-call | flops 1000000 | bytes 500000 | tf_op jit(solution)/shard_map/pallas_call | solution.py:51
  93.4 1.9 %collective-permute-start.4 = (bf16[4,192,256]{2,1,0:T(8,128)(2,1)S(1)}, bf16[4,192,256]{2,1,0:T(8,128)(2,1)S(1)}, u32[]{:S(2)}, u32[]{:S(2)}) collective-permute-start(bf16[4,192,256]{2,1,0:T(8,128)(2,1)S(1)} %pad_maximum_fusion.g00_ref), channel_id=1, source_target_pairs={{0,1},{1,0},{2,3},{3,2},{4,5},{5,4},{6,7},{7,6},{8,9},{9,8},{10,11... | collective-permute-start | bytes 1179656 | tf_op jit(solution)/shard_map/ppermute | solution.py:229
  95.3 3.1 %collective-permute-done.5.g10_ref = bf16[4,192,256]{2,1,0:T(8,128)(2,1)S(1)} collective-permute-done((bf16[4,192,256]{2,1,0:T(8,128)(2,1)S(1)}, bf16[4,192,256]{2,1,0:T(8,128)(2,1)S(1)}, u32[]{:S(2)}, u32[]{:S(2)}) %collective-permute-start.5) | collective-permute-done | bytes 393248 | tf_op jit(solution)/shard_map/ppermute | solution.py:228
  98.4 1.9 %collective-permute-start.6 = (bf16[4,192,256]{2,1,0:T(8,128)(2,1)S(1)}, bf16[4,192,256]{2,1,0:T(8,128)(2,1)S(1)}, u32[]{:S(2)}, u32[]{:S(2)}) collective-permute-start(bf16[4,192,256]{2,1,0:T(8,128)(2,1)S(1)} %collective-permute-done.5.g10_ref), channel_id=1, source_target_pairs={{0,1},{1,0},{2,3},{3,2},{4,5},{5,4},{6,7},{7,6},{8,9},{9,8},{10,11... | collective-permute-start | bytes 1179656 | tf_op jit(solution)/shard_map/ppermute | solution.py:230
  100.3 0.0 collective-permute-done.other_ref
  100.3 5.2 %shard_map.69 = (f32[256,256]{1,0:T(8,128)}, bf16[4,256,256]{2,1,0:T(8,128)(2,1)}) custom-call(s32[2]{0:T(128)S(1)} %pad_add_fusion.place_ref, s32[73]{0:T(128)S(1)} %get-tuple-element.6.table_ref, bf16[2,128,512]{2,1,0:T(8,128)(2,1)S(1)} %get-tuple-element.7.q_ref, bf16[8,4,128,128]{3,2,1,0:T(8,128)(2,1)S(1)} %all_to_all.21.own_ref, ...), custom_call_target="tpu_custom_call" | custom-call | flops 1200000000 | bytes 4000000 | tf_op jit(solution)/shard_map/pallas_call | solution.py:149
  105.6 0.0 copy-start
  105.6 9.0 %all-to-all-start.2 = ((bf16[4,256,256]{2,1,0:T(8,128)(2,1)}), bf16[4,256,256]{2,1,0:T(8,128)(2,1)S(1)}, u32[]{:S(2)}, u32[]{:S(2)}) async-start(bf16[4,256,256]{2,1,0:T(8,128)(2,1)} %get-tuple-element.9), calls=%async_computation.2 | async-start | bytes 1048576 | tf_op jit(solution)/shard_map/all_to_all | solution.py:233
  114.6 0.1 pad_add_fusion.1.place_ref
  114.6 0.0 collective-permute-done.4.g01_ref
  114.7 8.9 %all-to-all-done.2.a_ref = bf16[4,256,256]{2,1,0:T(8,128)(2,1)S(1)} async-done(((bf16[4,256,256]{2,1,0:T(8,128)(2,1)}), bf16[4,256,256]{2,1,0:T(8,128)(2,1)S(1)}, u32[]{:S(2)}, u32[]{:S(2)}) %all-to-all-start.2) | async-done | bytes 524320 | tf_op jit(solution)/shard_map/all_to_all | solution.py:233
  123.5 1.2 shard_map.70
  124.8 26.9 %all_to_all.22 = f32[8,96,256]{2,1,0:T(8,128)S(1)} all-to-all(f32[8,96,256]{2,1,0:T(8,128)S(1)} %bitcast.9), channel_id=1, replica_groups=mesh['x'=4,'y'=8,'z'=8,'core'=2] {'y'}, dimensions={0} | all-to-all | bytes 1572864 | tf_op jit(solution)/shard_map/all_to_all | solution.py:236
  151.7 0.7 reduce_sum.9
  (11 shorter events, 0.1 us)
Async XLA Ops:
  0.6 0.8 dynamic-slice-start
  14.4 32.6 %copy-start.4 = (bf16[256,180]{0,1:T(8,128)(2,1)S(1)}, bf16[256,180]{0,1:T(8,128)(2,1)}, u32[]{:S(2)}) copy-start(bf16[256,180]{0,1:T(8,128)(2,1)} %param.7) | copy-start | bytes 276484
  45.1 55.2 %collective-permute-start = (bf16[8,4,128,128]{3,2,1,0:T(8,128)(2,1)S(1)}, bf16[8,4,128,128]{3,2,1,0:T(8,128)(2,1)}, u32[]{:S(2)}, u32[]{:S(2)}) collective-permute-start(bf16[8,4,128,128]{3,2,1,0:T(8,128)(2,1)S(1)} %all_to_all.21.own_ref), channel_id=1, source_target_pairs={{0,1},{1,0},{2,3},{3,2},{4,5},{5,4},{6,7},{7,6},{8,9},{9,8},{10,11... | collective-permute-start | bytes 3145736 | tf_op jit(solution)/shard_map/ppermute | solution.py:219
  47.1 12.5 %collective-permute-start.1 = (bf16[192,256]{1,0:T(8,128)(2,1)S(1)}, bf16[192,256]{1,0:T(8,128)(2,1)S(1)}, u32[]{:S(2)}, u32[]{:S(2)}) collective-permute-start(bf16[192,256]{1,0:T(8,128)(2,1)S(1)} %bitcast.14), channel_id=1, source_target_pairs={{0,0},{2,2},{4,128},{6,130},{8,256},{10,258},{12,384},{14,386},{12... | collective-permute-start | bytes 294920 | tf_op jit(solution)/shard_map/ppermute | solution.py:214
  59.7 11.1 %collective-permute-start.2 = (bf16[1,192,256]{2,1,0:T(8,128)(2,1)S(1)}, bf16[1,192,256]{2,1,0:T(8,128)(2,1)S(1)}, u32[]{:S(2)}, u32[]{:S(2)}) collective-permute-start(bf16[1,192,256]{2,1,0:T(8,128)(2,1)S(1)} %bitcast.10), channel_id=1, source_target_pairs={{0,8},{2,10},{4,12},{6,14},{8,0},{10,2},{12,4},{14,6},{1,9},{3,11}... | collective-permute-start | bytes 294920 | tf_op jit(solution)/shard_map/ppermute | solution.py:226
  70.8 19.5 %copy-start.1 = (bf16[256,256]{1,0:T(8,128)(2,1)S(1)}, bf16[256,256]{1,0:T(8,128)(2,1)}, u32[]{:S(2)}) copy-start(bf16[256,256]{1,0:T(8,128)(2,1)} %q_ref.1) | copy-start | bytes 393220
  70.9 12.3 %collective-permute-start.3 = (bf16[2,192,256]{2,1,0:T(8,128)(2,1)S(1)}, bf16[2,192,256]{2,1,0:T(8,128)(2,1)S(1)}, u32[]{:S(2)}, u32[]{:S(2)}) collective-permute-start(bf16[2,192,256]{2,1,0:T(8,128)(2,1)S(1)} %pad_maximum_fusion.1), channel_id=1, source_target_pairs={{0,4},{2,6},{4,0},{6,2},{8,12},{10,14},{12,8},{14,10},{1,5},{3,7},... | collective-permute-start | bytes 589832 | tf_op jit(solution)/shard_map/ppermute | solution.py:226
  83.1 7.2 %copy-start.2 = (s32[8192]{0:T(1024)S(1)}, s32[8192]{0:T(1024)}, u32[]{:S(2)}) copy-start(s32[8192]{0:T(1024)} %docs_ref.1) | copy-start | bytes 98308
  83.2 15.2 %collective-permute-start.5 = (bf16[4,192,256]{2,1,0:T(8,128)(2,1)S(1)}, bf16[4,192,256]{2,1,0:T(8,128)(2,1)S(1)}, u32[]{:S(2)}, u32[]{:S(2)}) collective-permute-start(bf16[4,192,256]{2,1,0:T(8,128)(2,1)S(1)} %pad_maximum_fusion.g00_ref), channel_id=1, source_target_pairs={{0,2},{2,0},{4,6},{6,4},{8,10},{10,8},{12,14},{14,12},{1,3},{3,1},... | collective-permute-start | bytes 1179656 | tf_op jit(solution)/shard_map/ppermute | solution.py:228
  90.2 0.7 copy-start.3
  93.4 21.3 %collective-permute-start.4 = (bf16[4,192,256]{2,1,0:T(8,128)(2,1)S(1)}, bf16[4,192,256]{2,1,0:T(8,128)(2,1)S(1)}, u32[]{:S(2)}, u32[]{:S(2)}) collective-permute-start(bf16[4,192,256]{2,1,0:T(8,128)(2,1)S(1)} %pad_maximum_fusion.g00_ref), channel_id=1, source_target_pairs={{0,1},{1,0},{2,3},{3,2},{4,5},{5,4},{6,7},{7,6},{8,9},{9,8},{10,11... | collective-permute-start | bytes 1179656 | tf_op jit(solution)/shard_map/ppermute | solution.py:229
  98.4 16.2 %collective-permute-start.6 = (bf16[4,192,256]{2,1,0:T(8,128)(2,1)S(1)}, bf16[4,192,256]{2,1,0:T(8,128)(2,1)S(1)}, u32[]{:S(2)}, u32[]{:S(2)}) collective-permute-start(bf16[4,192,256]{2,1,0:T(8,128)(2,1)S(1)} %collective-permute-done.5.g10_ref), channel_id=1, source_target_pairs={{0,1},{1,0},{2,3},{3,2},{4,5},{5,4},{6,7},{7,6},{8,9},{9,8},{10,11... | collective-permute-start | bytes 1179656 | tf_op jit(solution)/shard_map/ppermute | solution.py:230
  105.6 18.0 %copy-start = (f32[256,256]{1,0:T(8,128)S(1)}, f32[256,256]{1,0:T(8,128)}, u32[]{:S(2)}) copy-start(f32[256,256]{1,0:T(8,128)} %get-tuple-element.4.own_ref) | copy-start | bytes 786436
  105.6 17.9 %all-to-all-start.2 = ((bf16[4,256,256]{2,1,0:T(8,128)(2,1)}), bf16[4,256,256]{2,1,0:T(8,128)(2,1)S(1)}, u32[]{:S(2)}, u32[]{:S(2)}) async-start(bf16[4,256,256]{2,1,0:T(8,128)(2,1)} %get-tuple-element.9), calls=%async_computation.2 | async-start | bytes 1048576 | tf_op jit(solution)/shard_map/all_to_all | solution.py:233

commit v7 on v4

--- a/solution.py
+++ b/solution.py
@@ -18,7 +18,6 @@
 
 def tables_kernel(place_ref, tiles_ref, docs_ref, q_ref, table_ref, q_t_ref):
     count = tiles_ref.shape[0]
-    tokens = docs_ref.shape[0]
 
     def invert(slot, carry):
         table_ref[tiles_ref[slot]] = slot
@@ -26,17 +25,10 @@
 
     lax.fori_loop(0, count, invert, 0)
 
-    def bisect(step, lows):
-        size = lax.shift_right_logical(tokens, step + 1)
-        return tuple(
-            jnp.where(docs_ref[low + size - 1] < doc + 1, low + size, low) for doc, low in enumerate(lows)
-        )
-
-    steps = tokens.bit_length() - 1
-    bounds = lax.fori_loop(0, steps, bisect, (jnp.int32(0),) * (DOCS - 1))
-    for doc, low in enumerate(bounds):
-        last = docs_ref[jnp.minimum(low, tokens - 1)] < doc + 1
-        table_ref[count + doc] = jnp.where(last, low + 1, low)
+    docs = docs_ref[...]
+    for doc in range(1, DOCS):
+        before = jnp.sum(jnp.where(docs < doc, 1.0, 0.0))
+        table_ref[count + doc - 1] = before.astype(jnp.int32)
     for part in range(2):
         table_ref[count + DOCS - 1 + part] = tiles_ref[place_ref[1] + part]
         q = q_ref[part * TILE:(part + 1) * TILE, :]
@@ -54,14 +46,14 @@
             jax.ShapeDtypeStruct((tiles.shape[0] + DOCS + 1,), jnp.int32),
             jax.ShapeDtypeStruct((2, 2 * DH, HEADS * TILE), jnp.bfloat16),
         ),
-        in_specs=[smem, smem, smem, vmem],
+        in_specs=[smem, smem, vmem, vmem],
         out_specs=(smem, vmem),
         cost_estimate=pl.CostEstimate(flops=1_000_000, bytes_accessed=500_000, transcendentals=0),
         compiler_params=pltpu.CompilerParams(vmem_limit_bytes=8 << 20),
-    )(place, tiles, docs, queries)
-
-
-def attention_kernel(place_ref, table_ref, q_ref, own_ref, other_ref, out_ref, send_ref, s_ref):
+    )(place, tiles, docs.reshape(-1, TILE), queries)
+
+
+def attention_kernel(place_ref, table_ref, q_ref, own_ref, other_ref, out_ref, send_ref, s_ref, o_ref, sems):
     count = table_ref.shape[0] - DOCS - 1
     core = place_ref[0]
     width = HEADS * TILE
@@ -75,6 +67,7 @@
         at = lax.shift_right_logical(slot, 1)
         return jnp.where((slot & 1) == core, own_ref[at], other_ref[at])
 
+    copies = []
     for part in range(2):
         tile = table_ref[count + DOCS - 1 + part]
         base = tile * TILE
@@ -128,9 +121,15 @@
                 [normed[:, h * TILE:(h + 1) * TILE], normed[:, (h + 1) * TILE:(h + 2) * TILE]], axis=0
             )
             both = jnp.transpose(both)
-            out_ref[part * TILE:(part + 1) * TILE, h * DH:(h + 2) * DH] = both
-            for peer in range(send_ref.shape[0]):
-                send_ref[peer, part * TILE:(part + 1) * TILE, h * DH:(h + 2) * DH] = both
+            o_ref[part, :, h * DH:(h + 2) * DH] = both
+        rows = pl.ds(part * TILE, TILE)
+        copies.append(pltpu.make_async_copy(o_ref.at[part], out_ref.at[rows], sems.at[part, 0]))
+        for peer in range(send_ref.shape[0]):
+            copies.append(pltpu.make_async_copy(o_ref.at[part], send_ref.at[peer, rows], sems.at[part, 1 + peer]))
+        for copy in copies[-1 - send_ref.shape[0]:]:
+            copy.start()
+    for copy in copies:
+        copy.wait()
 
 
 def attention(place, table, q_t, own, other, peers):
@@ -144,8 +143,12 @@
             jax.ShapeDtypeStruct((peers, rows, columns), jnp.float32),
         ),
         in_specs=[smem, smem, vmem, vmem, vmem],
-        out_specs=(vmem, vmem),
-        scratch_shapes=[pltpu.VMEM((SPAN * TILE, HEADS * TILE), jnp.float32)],
+        out_specs=(pl.BlockSpec(memory_space=pl.ANY), pl.BlockSpec(memory_space=pl.ANY)),
+        scratch_shapes=[
+            pltpu.VMEM((SPAN * TILE, HEADS * TILE), jnp.float32),
+            pltpu.VMEM((2, TILE, columns), jnp.float32),
+            pltpu.SemaphoreType.DMA((2, 1 + peers)),
+        ],
         cost_estimate=pl.CostEstimate(flops=1_200_000_000, bytes_accessed=4_000_000, transcendentals=2_200_000),
         compiler_params=pltpu.CompilerParams(vmem_limit_bytes=32 << 20),
     )(place, table, q_t, own, other)
@@ -157,12 +160,13 @@
     high = a.astype(jnp.bfloat16)
     high_ref[...] = high
     low_ref[...] = (a - high.astype(jnp.float32)).astype(jnp.bfloat16)
+    places = ([z ^ k for k in (0, 4, 2, 6)], [(z + k) & 7 for k in (1, 5, 7, 3)])
     for flip, sides in enumerate(((g00_ref, g01_ref), (g10_ref, g11_ref))):
         pair = (z & 1) ^ flip
         for side, g_ref in zip((core, 1 - core), sides, strict=True):
             term = None
-            for i in range(g_ref.shape[0]):
-                peer = lax.shift_right_logical(z, 1) ^ (((i & 1) << 1) | (i >> 1))
+            for i, place in enumerate(places[flip]):
+                peer = lax.shift_right_logical(place, 1)
                 for half_ref in (high_ref, low_ref):
                     part = jnp.dot(g_ref[i], half_ref[peer], preferred_element_type=jnp.float32)
                     term = part if term is None else term + part
@@ -219,11 +223,13 @@
     place = jnp.stack([core, 2 * ctx])
     table, q_t = tables_of(place, tile_list, doc_ids, queries)
 
-    g_own = grads[None]
-    for bit in (4, 2):
-        came = lax.ppermute(g_own, "z", [(i, i ^ bit) for i in range(nz)])
-        g_own = jnp.concatenate([g_own, came], axis=0)
-    g_next = lax.ppermute(g_own, "z", [(i, i ^ 1) for i in range(nz)])
+    came = lax.ppermute(grads[None], "z", [(i, i ^ 4) for i in range(nz)])
+    g_pair = jnp.concatenate([grads[None], came], axis=0)
+    g_even = lax.ppermute(g_pair, "z", [(i, i ^ 2) for i in range(nz)])
+    g_up = lax.ppermute(g_pair, "z", [((i + 1) % nz, i) for i in range(nz)])
+    g_down = lax.ppermute(g_pair, "z", [(i, (i + 1) % nz) for i in range(nz)])
+    g_own = jnp.concatenate([g_pair, g_even], axis=0)
+    g_next = jnp.concatenate([g_up, g_down], axis=0)
     g_other = lax.ppermute(g_own, "core", swap)
     g_both = lax.ppermute(g_next, "core", swap)
 

time: 129 us -> 128 us (level)
  the two profiles are of different devices: /device:TPU:64 before, /device:TPU:1 now
where the time goes in v7:
time: 128 us
  starting transfers between devices  56.8 us (44%)
  blocking collectives  34.5 us (27%)
  waiting for transfers between devices  23.6 us (18%)
  Pallas kernels  9.08 us (7%)
  local copies, waits for them, and re-layouts  1.75 us (1%)
    all_to_all x2, blocking collectives, everyone(): lax.all_to_all(jnp.broadcast_to(x[None], (size,) + x.shape), axes, 0, 0)  34.5 us
    ppermute x1, starting transfers between devices, on_device(): came = lax.ppermute(grads[None], 'z', [(i, i ^ 4) for i in range(nz)])  22.5 us
    all_to_all x1, waiting for transfers between devices, on_device(): parts = lax.all_to_all(term.reshape(ny, PADDED, -1), 'y', 0, 0)  15.1 us
    ppermute x1, starting transfers between devices, on_device(): g_up = lax.ppermute(g_pair, 'z', [((i + 1) % nz, i) for i in range(nz)])  5.78 us
    all_to_all x1, starting transfers between devices, on_device(): gathered = lax.all_to_all(send, 'x', 0, 0)  5.6 us
    ppermute x1, starting transfers between devices, on_device(): other = lax.ppermute(own, 'core', swap)  5.37 us
    ppermute x1, waiting for transfers between devices, on_device(): g_even = lax.ppermute(g_pair, 'z', [(i, i ^ 2) for i in range(nz)])  5.27 us
    all_to_all x1, starting transfers between devices, on_device(): parts = lax.all_to_all(term.reshape(ny, PADDED, -1), 'y', 0, 0)  4.94 us
  transfers between devices with their start and end apart: 10, of which 4 were waited for; matrix products, arithmetic and copies ran while one was open for 0% of the time, Pallas kernels for 5%

profile of v7, /device:TPU:1, one launch (start us, length us, event | category | flops | bytes accessed | tf_op | source)
XLA Modules:
  0.0 127.6 jit_solution(14790878166531380744)
XLA Ops:
  0.6 0.0 dynamic-slice-start
  0.7 0.7 dynamic-slice-done
  1.4 17.0 %all_to_all.20 = bf16[8,128,128]{2,1,0:T(8,128)(2,1)S(1)} all-to-all(bf16[8,128,128]{2,1,0:T(8,128)(2,1)S(1)} %broadcast_in_dim.9), channel_id=1, replica_groups=mesh['x'=4,'y'=8,'z'=8,'core'=2] {'y'}, dimensions={0} | all-to-all | bytes 524288 | tf_op jit(solution)/shard_map/all_to_all | solution.py:202
  18.4 0.2 broadcast_in_dim.10
  18.7 0.0 copy-start.3
  18.7 17.5 %all_to_all.21 = bf16[4,8,128,128]{3,2,1,0:T(8,128)(2,1)S(1)} all-to-all(bf16[4,8,128,128]{3,2,1,0:T(8,128)(2,1)S(1)} %broadcast_in_dim.10), channel_id=1, replica_groups=mesh['x'=4,'y'=8,'z'=8,'core'=2] {'x'}, dimensions={0} | all-to-all | bytes 2097152 | tf_op jit(solution)/shard_map/all_to_all | solution.py:202
  36.1 5.4 %collective-permute-start = (bf16[32,128,128]{2,1,0:T(8,128)(2,1)S(1)}, bf16[32,128,128]{2,1,0:T(8,128)(2,1)S(1)}, u32[]{:S(2)}, u32[]{:S(2)}) collective-permute-start(bf16[32,128,128]{2,1,0:T(8,128)(2,1)S(1)} %bitcast.10), channel_id=1, source_target_pairs={{0,1},{1,0},{2,3},{3,2},{4,5},{5,4},{6,7},{7,6},{8,9},{9,8},{10,11... | collective-permute-start | bytes 3145736 | tf_op jit(solution)/shard_map/ppermute | solution.py:221
  41.6 0.7 collective-permute-start.1
  42.3 0.0 collective-permute-done.1
  42.3 22.5 %collective-permute-start.2 = (bf16[1,192,256]{2,1,0:T(8,128)(2,1)S(1)}, bf16[1,192,256]{2,1,0:T(8,128)(2,1)S(1)}, u32[]{:S(2)}, u32[]{:S(2)}) collective-permute-start(bf16[1,192,256]{2,1,0:T(8,128)(2,1)S(1)} %bitcast.13), channel_id=1, source_target_pairs={{0,8},{2,10},{4,12},{6,14},{8,0},{10,2},{12,4},{14,6},{1,9},{3,11}... | collective-permute-start | bytes 294920 | tf_op jit(solution)/shard_map/ppermute | solution.py:226
  64.8 0.0 copy-start
  64.8 0.0 copy-start.1
  64.8 2.0 %collective-permute-done.2 = bf16[1,192,256]{2,1,0:T(8,128)(2,1)S(1)} collective-permute-done((bf16[1,192,256]{2,1,0:T(8,128)(2,1)S(1)}, bf16[1,192,256]{2,1,0:T(8,128)(2,1)S(1)}, u32[]{:S(2)}, u32[]{:S(2)}) %collective-permute-start.2) | collective-permute-done | bytes 98336 | tf_op jit(solution)/shard_map/ppermute | solution.py:226
  66.8 5.8 %collective-permute-start.5 = (bf16[2,192,256]{2,1,0:T(8,128)(2,1)S(1)}, bf16[2,192,256]{2,1,0:T(8,128)(2,1)S(1)}, u32[]{:S(2)}, u32[]{:S(2)}) collective-permute-start(bf16[2,192,256]{2,1,0:T(8,128)(2,1)S(1)} %pad_maximum_fusion.1), channel_id=1, source_target_pairs={{2,0},{4,2},{6,4},{8,6},{10,8},{12,10},{14,12},{0,14},{3,1},{5,3},... | collective-permute-start | bytes 589832 | tf_op jit(solution)/shard_map/ppermute | solution.py:229
  72.6 0.1 pad_add_fusion.place_ref
  72.7 0.6 copy-done.2
  73.3 1.8 %shard_map.68 = (s32[73]{0:T(128)S(1)}, bf16[2,128,512]{2,1,0:T(8,128)(2,1)S(1)}) custom-call(s32[2]{0:T(128)S(1)} %pad_add_fusion.place_ref, s32[64]{0:T(128)S(1)} %copy-done.2, s32[64,128]{1,0:T(8,128)S(1)} %bitcast.12, bf16[256,256]{1,0:T(8,128)(2,1)S(1)} %copy-done), custom_call_target="tpu_custom_call" | custom-call | flops 1000000 | bytes 500000 | tf_op jit(solution)/shard_map/pallas_call | solution.py:43
  75.2 1.9 %collective-permute-start.6 = (bf16[2,192,256]{2,1,0:T(8,128)(2,1)S(1)}, bf16[2,192,256]{2,1,0:T(8,128)(2,1)S(1)}, u32[]{:S(2)}, u32[]{:S(2)}) collective-permute-start(bf16[2,192,256]{2,1,0:T(8,128)(2,1)S(1)} %pad_maximum_fusion.1), channel_id=1, source_target_pairs={{0,2},{2,4},{4,6},{6,8},{8,10},{10,12},{12,14},{14,0},{1,3},{3,5},... | collective-permute-start | bytes 589832 | tf_op jit(solution)/shard_map/ppermute | solution.py:230
  77.1 4.7 %shard_map.69 = (f32[256,256]{1,0:T(8,128)}, f32[4,256,256]{2,1,0:T(8,128)}) custom-call(s32[2]{0:T(128)S(1)} %pad_add_fusion.place_ref, s32[73]{0:T(128)S(1)} %get-tuple-element.8.table_ref, bf16[2,128,512]{2,1,0:T(8,128)(2,1)S(1)} %get-tuple-element.9.q_ref, bf16[32,128,128]{2,1,0:T(8,128)(2,1)S(1)} %bitcast.11, ...), custom_call_target="tpu_custom_call" | custom-call | flops 1200000000 | bytes 4000000 | tf_op jit(solution)/shard_map/pallas_call | solution.py:139
  81.8 5.6 %all-to-all-start.2 = ((f32[4,256,256]{2,1,0:T(8,128)}), f32[4,256,256]{2,1,0:T(8,128)S(1)}, u32[]{:S(2)}, u32[]{:S(2)}) async-start(f32[4,256,256]{2,1,0:T(8,128)} %get-tuple-element.11), calls=%async_computation.2 | async-start | bytes 2097152 | tf_op jit(solution)/shard_map/all_to_all | solution.py:237
  87.4 2.5 %collective-permute-start.3 = (bf16[2,192,256]{2,1,0:T(8,128)(2,1)S(1)}, bf16[2,192,256]{2,1,0:T(8,128)(2,1)S(1)}, u32[]{:S(2)}, u32[]{:S(2)}) collective-permute-start(bf16[2,192,256]{2,1,0:T(8,128)(2,1)S(1)} %pad_maximum_fusion.1), channel_id=1, source_target_pairs={{0,4},{2,6},{4,0},{6,2},{8,12},{10,14},{12,8},{14,10},{1,5},{3,7},... | collective-permute-start | bytes 589832 | tf_op jit(solution)/shard_map/ppermute | solution.py:228
  89.9 0.0 collective-permute-done.5
  89.9 4.0 %collective-permute-start.7 = (bf16[4,192,256]{2,1,0:T(8,128)(2,1)S(1)}, bf16[4,192,256]{2,1,0:T(8,128)(2,1)S(1)}, u32[]{:S(2)}, u32[]{:S(2)}) collective-permute-start(bf16[4,192,256]{2,1,0:T(8,128)(2,1)S(1)} %constant_dynamic-update-slice_fusion.g10_ref), channel_id=1, source_target_pairs={{0,1},{1,0},{2,3},{3,2},{4,5},{5,4},{6,7},{7,6},{8,9},{9,8},{10,11... | collective-permute-start | bytes 1179656 | tf_op jit(solution)/shard_map/ppermute | solution.py:234
  94.0 5.3 %collective-permute-done.3 = bf16[2,192,256]{2,1,0:T(8,128)(2,1)S(1)} collective-permute-done((bf16[2,192,256]{2,1,0:T(8,128)(2,1)S(1)}, bf16[2,192,256]{2,1,0:T(8,128)(2,1)S(1)}, u32[]{:S(2)}, u32[]{:S(2)}) %collective-permute-start.3) | collective-permute-done | bytes 196640 | tf_op jit(solution)/shard_map/ppermute | solution.py:228
  99.3 3.5 %collective-permute-start.4 = (bf16[4,192,256]{2,1,0:T(8,128)(2,1)S(1)}, bf16[4,192,256]{2,1,0:T(8,128)(2,1)S(1)}, u32[]{:S(2)}, u32[]{:S(2)}) collective-permute-start(bf16[4,192,256]{2,1,0:T(8,128)(2,1)S(1)} %pad_maximum_fusion.g00_ref), channel_id=1, source_target_pairs={{0,1},{1,0},{2,3},{3,2},{4,5},{5,4},{6,7},{7,6},{8,9},{9,8},{10,11... | collective-permute-start | bytes 1179656 | tf_op jit(solution)/shard_map/ppermute | solution.py:233
  102.8 0.1 pad_add_fusion.1.place_ref
  102.9 1.2 collective-permute-done.4.g01_ref
  104.1 2.6 %shard_map.70 = (bf16[4,192,256]{2,1,0:T(8,128)(2,1)}, f32[96,256]{1,0:T(8,128)S(1)}) custom-call(s32[3]{0:T(128)S(1)} %pad_add_fusion.1.place_ref, bf16[4,192,256]{2,1,0:T(8,128)(2,1)S(1)} %pad_maximum_fusion.g00_ref, bf16[4,192,256]{2,1,0:T(8,128)(2,1)S(1)} %collective-permute-done.4.g01_ref, ...), custom_call_target="tpu_custom_call" | custom-call | flops 900000000 | bytes 3000000 | tf_op jit(solution)/shard_map/pallas_call | solution.py:183
  106.7 4.9 %all-to-all-start.3 = ((bf16[8,96,256]{2,1,0:T(8,128)(2,1)}), bf16[8,96,256]{2,1,0:T(8,128)(2,1)S(1)}, u32[]{:S(2)}, u32[]{:S(2)}) async-start(bf16[8,96,256]{2,1,0:T(8,128)(2,1)} %bitcast.9), calls=%async_computation.3 | async-start | bytes 786432 | tf_op jit(solution)/shard_map/all_to_all | solution.py:241
  111.6 15.1 %all-to-all-done.3 = bf16[8,96,256]{2,1,0:T(8,128)(2,1)S(1)} async-done(((bf16[8,96,256]{2,1,0:T(8,128)(2,1)}), bf16[8,96,256]{2,1,0:T(8,128)(2,1)S(1)}, u32[]{:S(2)}, u32[]{:S(2)}) %all-to-all-start.3) | async-done | bytes 393248 | tf_op jit(solution)/shard_map/all_to_all | solution.py:241
  126.8 0.1 select_reduce_fusion
  126.9 0.7 slice_add_fusion
  (16 shorter events, 0.2 us)
Async XLA Ops:
  0.6 0.8 dynamic-slice-start
  18.7 22.9 %copy-start.3 = (bf16[256,180]{0,1:T(8,128)(2,1)S(1)}, bf16[256,180]{0,1:T(8,128)(2,1)}, u32[]{:S(2)}) copy-start(bf16[256,180]{0,1:T(8,128)(2,1)} %param.7) | copy-start | bytes 276484
  36.1 40.9 %collective-permute-start = (bf16[32,128,128]{2,1,0:T(8,128)(2,1)S(1)}, bf16[32,128,128]{2,1,0:T(8,128)(2,1)S(1)}, u32[]{:S(2)}, u32[]{:S(2)}) collective-permute-start(bf16[32,128,128]{2,1,0:T(8,128)(2,1)S(1)} %bitcast.10), channel_id=1, source_target_pairs={{0,1},{1,0},{2,3},{3,2},{4,5},{5,4},{6,7},{7,6},{8,9},{9,8},{10,11... | collective-permute-start | bytes 3145736 | tf_op jit(solution)/shard_map/ppermute | solution.py:221
  41.6 0.7 collective-permute-start.1
  42.3 24.5 %collective-permute-start.2 = (bf16[1,192,256]{2,1,0:T(8,128)(2,1)S(1)}, bf16[1,192,256]{2,1,0:T(8,128)(2,1)S(1)}, u32[]{:S(2)}, u32[]{:S(2)}) collective-permute-start(bf16[1,192,256]{2,1,0:T(8,128)(2,1)S(1)} %bitcast.13), channel_id=1, source_target_pairs={{0,8},{2,10},{4,12},{6,14},{8,0},{10,2},{12,4},{14,6},{1,9},{3,11}... | collective-permute-start | bytes 294920 | tf_op jit(solution)/shard_map/ppermute | solution.py:226
  64.8 7.9 %copy-start = (bf16[256,256]{1,0:T(8,128)(2,1)S(1)}, bf16[256,256]{1,0:T(8,128)(2,1)}, u32[]{:S(2)}) copy-start(bf16[256,256]{1,0:T(8,128)(2,1)} %q_ref.1) | copy-start | bytes 393220
  64.8 7.9 %copy-start.1 = (s32[8192]{0:T(1024)S(1)}, s32[8192]{0:T(1024)}, u32[]{:S(2)}) copy-start(s32[8192]{0:T(1024)} %param.8) | copy-start | bytes 98308
  66.8 23.1 %collective-permute-start.5 = (bf16[2,192,256]{2,1,0:T(8,128)(2,1)S(1)}, bf16[2,192,256]{2,1,0:T(8,128)(2,1)S(1)}, u32[]{:S(2)}, u32[]{:S(2)}) collective-permute-start(bf16[2,192,256]{2,1,0:T(8,128)(2,1)S(1)} %pad_maximum_fusion.1), channel_id=1, source_target_pairs={{2,0},{4,2},{6,4},{8,6},{10,8},{12,10},{14,12},{0,14},{3,1},{5,3},... | collective-permute-start | bytes 589832 | tf_op jit(solution)/shard_map/ppermute | solution.py:229
  72.7 0.7 copy-start.2
  75.2 14.7 %collective-permute-start.6 = (bf16[2,192,256]{2,1,0:T(8,128)(2,1)S(1)}, bf16[2,192,256]{2,1,0:T(8,128)(2,1)S(1)}, u32[]{:S(2)}, u32[]{:S(2)}) collective-permute-start(bf16[2,192,256]{2,1,0:T(8,128)(2,1)S(1)} %pad_maximum_fusion.1), channel_id=1, source_target_pairs={{0,2},{2,4},{4,6},{6,8},{8,10},{10,12},{12,14},{14,0},{1,3},{3,5},... | collective-permute-start | bytes 589832 | tf_op jit(solution)/shard_map/ppermute | solution.py:230
  81.8 22.3 %all-to-all-start.2 = ((f32[4,256,256]{2,1,0:T(8,128)}), f32[4,256,256]{2,1,0:T(8,128)S(1)}, u32[]{:S(2)}, u32[]{:S(2)}) async-start(f32[4,256,256]{2,1,0:T(8,128)} %get-tuple-element.11), calls=%async_computation.2 | async-start | bytes 2097152 | tf_op jit(solution)/shard_map/all_to_all | solution.py:237
  87.4 11.8 %collective-permute-start.3 = (bf16[2,192,256]{2,1,0:T(8,128)(2,1)S(1)}, bf16[2,192,256]{2,1,0:T(8,128)(2,1)S(1)}, u32[]{:S(2)}, u32[]{:S(2)}) collective-permute-start(bf16[2,192,256]{2,1,0:T(8,128)(2,1)S(1)} %pad_maximum_fusion.1), channel_id=1, source_target_pairs={{0,4},{2,6},{4,0},{6,2},{8,12},{10,14},{12,8},{14,10},{1,5},{3,7},... | collective-permute-start | bytes 589832 | tf_op jit(solution)/shard_map/ppermute | solution.py:228
  89.9 12.9 %collective-permute-start.7 = (bf16[4,192,256]{2,1,0:T(8,128)(2,1)S(1)}, bf16[4,192,256]{2,1,0:T(8,128)(2,1)S(1)}, u32[]{:S(2)}, u32[]{:S(2)}) collective-permute-start(bf16[4,192,256]{2,1,0:T(8,128)(2,1)S(1)} %constant_dynamic-update-slice_fusion.g10_ref), channel_id=1, source_target_pairs={{0,1},{1,0},{2,3},{3,2},{4,5},{5,4},{6,7},{7,6},{8,9},{9,8},{10,11... | collective-permute-start | bytes 1179656 | tf_op jit(solution)/shard_map/ppermute | solution.py:234
  99.3 4.8 %collective-permute-start.4 = (bf16[4,192,256]{2,1,0:T(8,128)(2,1)S(1)}, bf16[4,192,256]{2,1,0:T(8,128)(2,1)S(1)}, u32[]{:S(2)}, u32[]{:S(2)}) collective-permute-start(bf16[4,192,256]{2,1,0:T(8,128)(2,1)S(1)} %pad_maximum_fusion.g00_ref), channel_id=1, source_target_pairs={{0,1},{1,0},{2,3},{3,2},{4,5},{5,4},{6,7},{7,6},{8,9},{9,8},{10,11... | collective-permute-start | bytes 1179656 | tf_op jit(solution)/shard_map/ppermute | solution.py:233
  106.7 20.1 %all-to-all-start.3 = ((bf16[8,96,256]{2,1,0:T(8,128)(2,1)}), bf16[8,96,256]{2,1,0:T(8,128)(2,1)S(1)}, u32[]{:S(2)}, u32[]{:S(2)}) async-start(bf16[8,96,256]{2,1,0:T(8,128)(2,1)} %bitcast.9), calls=%async_computation.3 | async-start | bytes 786432 | tf_op jit(solution)/shard_map/all_to_all | solution.py:241

commit v8 on v7

--- a/solution.py
+++ b/solution.py
@@ -16,60 +16,28 @@
 NEG_FILL = -1e30
 
 
-def tables_kernel(place_ref, tiles_ref, docs_ref, q_ref, table_ref, q_t_ref):
-    count = tiles_ref.shape[0]
-
-    def invert(slot, carry):
-        table_ref[tiles_ref[slot]] = slot
-        return carry
-
-    lax.fori_loop(0, count, invert, 0)
-
-    docs = docs_ref[...]
-    for doc in range(1, DOCS):
-        before = jnp.sum(jnp.where(docs < doc, 1.0, 0.0))
-        table_ref[count + doc - 1] = before.astype(jnp.int32)
-    for part in range(2):
-        table_ref[count + DOCS - 1 + part] = tiles_ref[place_ref[1] + part]
-        q = q_ref[part * TILE:(part + 1) * TILE, :]
-        q_t = jnp.transpose(q.astype(jnp.float32) * (DH ** -0.5)).astype(jnp.bfloat16)
-        q_t = jnp.concatenate([q_t[h * DH:(h + 1) * DH] for h in range(HEADS)], axis=1)
-        q_t_ref[part] = jnp.concatenate([q_t, jnp.zeros_like(q_t)], axis=0)
-
-
-def tables_of(place, tiles, docs, queries):
-    smem = pl.BlockSpec(memory_space=pltpu.SMEM)
-    vmem = pl.BlockSpec(memory_space=pltpu.VMEM)
-    return pl.pallas_call(
-        tables_kernel,
-        out_shape=(
-            jax.ShapeDtypeStruct((tiles.shape[0] + DOCS + 1,), jnp.int32),
-            jax.ShapeDtypeStruct((2, 2 * DH, HEADS * TILE), jnp.bfloat16),
-        ),
-        in_specs=[smem, smem, vmem, vmem],
-        out_specs=(smem, vmem),
-        cost_estimate=pl.CostEstimate(flops=1_000_000, bytes_accessed=500_000, transcendentals=0),
-        compiler_params=pltpu.CompilerParams(vmem_limit_bytes=8 << 20),
-    )(place, tiles, docs.reshape(-1, TILE), queries)
-
-
-def attention_kernel(place_ref, table_ref, q_ref, own_ref, other_ref, out_ref, send_ref, s_ref, o_ref, sems):
-    count = table_ref.shape[0] - DOCS - 1
+def attention_kernel(
+    place_ref, tiles_ref, docs_ref, q_ref, own_ref, other_ref, out_ref, send_ref, slot_ref, s_ref, o_ref, sems
+):
     core = place_ref[0]
     width = HEADS * TILE
-    bounds = [table_ref[count + doc] for doc in range(DOCS - 1)]
+
+    for slot in range(tiles_ref.shape[0]):
+        slot_ref[tiles_ref[slot]] = slot
+    docs = docs_ref[...]
+    bounds = [jnp.sum(jnp.where(docs < doc, 1.0, 0.0)).astype(jnp.int32) for doc in range(1, DOCS)]
 
     lane = lax.broadcasted_iota(jnp.int32, (1, TILE), 1)
     sub = lax.broadcasted_iota(jnp.int32, (2 * TILE, TILE), 0)
 
     def pick(tile):
-        slot = table_ref[tile]
+        slot = slot_ref[tile]
         at = lax.shift_right_logical(slot, 1)
         return jnp.where((slot & 1) == core, own_ref[at], other_ref[at])
 
     copies = []
     for part in range(2):
-        tile = table_ref[count + DOCS - 1 + part]
+        tile = tiles_ref[place_ref[1] + part]
         base = tile * TILE
         begin = jnp.int32(0)
         row_pos = base + lane
@@ -80,7 +48,10 @@
         low = lax.div(begin, TILE)
         pairs = lax.div(tile - low + 2, 2)
 
-        q_t = q_ref[part]
+        q = q_ref[part * TILE:(part + 1) * TILE, :]
+        q_t = jnp.transpose(q.astype(jnp.float32) * (DH ** -0.5)).astype(jnp.bfloat16)
+        q_t = jnp.concatenate([q_t[h * DH:(h + 1) * DH] for h in range(HEADS)], axis=1)
+        q_t = jnp.concatenate([q_t, jnp.zeros_like(q_t)], axis=0)
 
         def score(pair, top):
             at = low + 2 * pair
@@ -132,26 +103,27 @@
         copy.wait()
 
 
-def attention(place, table, q_t, own, other, peers):
+def attention(place, tiles, docs, queries, own, other, peers):
     smem = pl.BlockSpec(memory_space=pltpu.SMEM)
     vmem = pl.BlockSpec(memory_space=pltpu.VMEM)
-    rows, columns = 2 * TILE, HEADS * DH
+    rows, columns = queries.shape
     return pl.pallas_call(
         attention_kernel,
         out_shape=(
             jax.ShapeDtypeStruct((rows, columns), jnp.float32),
             jax.ShapeDtypeStruct((peers, rows, columns), jnp.float32),
         ),
-        in_specs=[smem, smem, vmem, vmem, vmem],
+        in_specs=[smem, smem, vmem, vmem, vmem, vmem],
         out_specs=(pl.BlockSpec(memory_space=pl.ANY), pl.BlockSpec(memory_space=pl.ANY)),
         scratch_shapes=[
+            pltpu.SMEM((tiles.shape[0],), jnp.int32),
             pltpu.VMEM((SPAN * TILE, HEADS * TILE), jnp.float32),
             pltpu.VMEM((2, TILE, columns), jnp.float32),
             pltpu.SemaphoreType.DMA((2, 1 + peers)),
         ],
         cost_estimate=pl.CostEstimate(flops=1_200_000_000, bytes_accessed=4_000_000, transcendentals=2_200_000),
         compiler_params=pltpu.CompilerParams(vmem_limit_bytes=32 << 20),
-    )(place, table, q_t, own, other)
+    )(place, tiles, docs.reshape(-1, TILE), queries, own, other)
 
 
 def term_kernel(place_ref, g00_ref, g01_ref, g10_ref, g11_ref, a_ref, out_ref, own_ref, high_ref, low_ref, sum_ref):
@@ -160,13 +132,12 @@
     high = a.astype(jnp.bfloat16)
     high_ref[...] = high
     low_ref[...] = (a - high.astype(jnp.float32)).astype(jnp.bfloat16)
-    places = ([z ^ k for k in (0, 4, 2, 6)], [(z + k) & 7 for k in (1, 5, 7, 3)])
     for flip, sides in enumerate(((g00_ref, g01_ref), (g10_ref, g11_ref))):
         pair = (z & 1) ^ flip
         for side, g_ref in zip((core, 1 - core), sides, strict=True):
             term = None
-            for i, place in enumerate(places[flip]):
-                peer = lax.shift_right_logical(place, 1)
+            for i in range(g_ref.shape[0]):
+                peer = lax.shift_right_logical(z, 1) ^ (((i & 1) << 1) | (i >> 1))
                 for half_ref in (high_ref, low_ref):
                     part = jnp.dot(g_ref[i], half_ref[peer], preferred_element_type=jnp.float32)
                     term = part if term is None else term + part
@@ -220,20 +191,16 @@
     own = everyone(own, "x", nx).reshape(nx * ny, TILE, 2 * DH)
     other = lax.ppermute(own, "core", swap)
 
-    place = jnp.stack([core, 2 * ctx])
-    table, q_t = tables_of(place, tile_list, doc_ids, queries)
-
-    came = lax.ppermute(grads[None], "z", [(i, i ^ 4) for i in range(nz)])
-    g_pair = jnp.concatenate([grads[None], came], axis=0)
-    g_even = lax.ppermute(g_pair, "z", [(i, i ^ 2) for i in range(nz)])
-    g_up = lax.ppermute(g_pair, "z", [((i + 1) % nz, i) for i in range(nz)])
-    g_down = lax.ppermute(g_pair, "z", [(i, (i + 1) % nz) for i in range(nz)])
-    g_own = jnp.concatenate([g_pair, g_even], axis=0)
-    g_next = jnp.concatenate([g_up, g_down], axis=0)
+    g_own = grads[None]
+    for bit in (4, 2):
+        came = lax.ppermute(g_own, "z", [(i, i ^ bit) for i in range(nz)])
+        g_own = jnp.concatenate([g_own, came], axis=0)
+    g_next = lax.ppermute(g_own, "z", [(i, i ^ 1) for i in range(nz)])
     g_other = lax.ppermute(g_own, "core", swap)
     g_both = lax.ppermute(g_next, "core", swap)
 
-    attended, send = attention(place, table, q_t, own, other, nx)
+    place = jnp.stack([core, 2 * ctx])
+    attended, send = attention(place, tile_list, doc_ids, queries, own, other, nx)
     gathered = lax.all_to_all(send, "x", 0, 0)
     y = lax.axis_index("y")
     place = jnp.stack([core, lax.axis_index("z"), y])

time: 128 us -> 129 us (level)
  the two profiles are of different devices: /device:TPU:1 before, /device:TPU:64 now
where the time goes in v8:
time: 129 us; the launch traced here: 128 us
  starting transfers between devices  44.8 us (35%)
  waiting for transfers between devices  36.5 us (28%)
  blocking collectives  36.4 us (28%)
  Pallas kernels  7.32 us (6%)
    all_to_all x2, blocking collectives, everyone(): lax.all_to_all(jnp.broadcast_to(x[None], (size,) + x.shape), axes, 0, 0)  36.4 us
    ppermute x2, starting transfers between devices, on_device(): came = lax.ppermute(g_own, 'z', [(i, i ^ bit) for i in range(nz)])  25 us
    all_to_all x1, waiting for transfers between devices, on_device(): parts = lax.all_to_all(term.reshape(ny, PADDED, -1), 'y', 0, 0)  13.8 us
    ppermute x2, waiting for transfers between devices, on_device(): came = lax.ppermute(g_own, 'z', [(i, i ^ bit) for i in range(nz)])  12.1 us
    all_to_all x1, waiting for transfers between devices, on_device(): gathered = lax.all_to_all(send, 'x', 0, 0)  9.42 us
    ppermute x1, starting transfers between devices, on_device(): g_next = lax.ppermute(g_own, 'z', [(i, i ^ 1) for i in range(nz)])  5.84 us
    pallas_call x1, Pallas kernels, attention(): pl.pallas_call(attention_kernel, out_shape=(jax.ShapeDtypeStruct((rows, c...  4.76 us
    all_to_all x1, starting transfers between devices, on_device(): gathered = lax.all_to_all(send, 'x', 0, 0)  3.53 us
  transfers between devices with their start and end apart: 9, of which 5 were waited for; matrix products, arithmetic and copies ran while one was open for 0% of the time, Pallas kernels for 4%

profile of v8, /device:TPU:64, one launch (start us, length us, event | category | flops | bytes accessed | tf_op | source)
XLA Modules:
  0.0 128.0 jit_solution(9024041743215588182)
XLA Ops:
  0.6 0.0 dynamic-slice-start
  0.7 0.7 dynamic-slice-done
  1.4 18.8 %all_to_all.20 = bf16[8,128,128]{2,1,0:T(8,128)(2,1)S(1)} all-to-all(bf16[8,128,128]{2,1,0:T(8,128)(2,1)S(1)} %broadcast_in_dim.9), channel_id=1, replica_groups=mesh['x'=4,'y'=8,'z'=8,'core'=2] {'y'}, dimensions={0} | all-to-all | bytes 524288 | tf_op jit(solution)/shard_map/all_to_all | solution.py:173
  20.2 0.2 broadcast_in_dim.20
  20.5 0.0 copy-start.3
  20.5 17.7 %all_to_all.21 = bf16[4,8,128,128]{3,2,1,0:T(8,128)(2,1)S(1)} all-to-all(bf16[4,8,128,128]{3,2,1,0:T(8,128)(2,1)S(1)} %broadcast_in_dim.20), channel_id=1, replica_groups=mesh['x'=4,'y'=8,'z'=8,'core'=2] {'x'}, dimensions={0} | all-to-all | bytes 2097152 | tf_op jit(solution)/shard_map/all_to_all | solution.py:173
  38.1 1.9 %collective-permute-start = (bf16[32,128,128]{2,1,0:T(8,128)(2,1)S(1)}, bf16[32,128,128]{2,1,0:T(8,128)(2,1)S(1)}, u32[]{:S(2)}, u32[]{:S(2)}) collective-permute-start(bf16[32,128,128]{2,1,0:T(8,128)(2,1)S(1)} %bitcast.10), channel_id=1, source_target_pairs={{0,1},{1,0},{2,3},{3,2},{4,5},{5,4},{6,7},{7,6},{8,9},{9,8},{10,11... | collective-permute-start | bytes 3145736 | tf_op jit(solution)/shard_map/ppermute | solution.py:192
  40.0 0.0 copy-done.3
  40.1 0.7 collective-permute-start.1
  40.8 0.0 collective-permute-done.1
  40.8 22.7 %collective-permute-start.2 = (bf16[1,192,256]{2,1,0:T(8,128)(2,1)S(1)}, bf16[1,192,256]{2,1,0:T(8,128)(2,1)S(1)}, u32[]{:S(2)}, u32[]{:S(2)}) collective-permute-start(bf16[1,192,256]{2,1,0:T(8,128)(2,1)S(1)} %bitcast.13), channel_id=1, source_target_pairs={{0,8},{2,10},{4,12},{6,14},{8,0},{10,2},{12,4},{14,6},{1,9},{3,11}... | collective-permute-start | bytes 294920 | tf_op jit(solution)/shard_map/ppermute | solution.py:196
  63.5 4.8 %collective-permute-done.2 = bf16[1,192,256]{2,1,0:T(8,128)(2,1)S(1)} collective-permute-done((bf16[1,192,256]{2,1,0:T(8,128)(2,1)S(1)}, bf16[1,192,256]{2,1,0:T(8,128)(2,1)S(1)}, u32[]{:S(2)}, u32[]{:S(2)}) %collective-permute-start.2) | collective-permute-done | bytes 98336 | tf_op jit(solution)/shard_map/ppermute | solution.py:196
  68.3 2.3 %collective-permute-start.3 = (bf16[2,192,256]{2,1,0:T(8,128)(2,1)S(1)}, bf16[2,192,256]{2,1,0:T(8,128)(2,1)S(1)}, u32[]{:S(2)}, u32[]{:S(2)}) collective-permute-start(bf16[2,192,256]{2,1,0:T(8,128)(2,1)S(1)} %pad_maximum_fusion.1), channel_id=1, source_target_pairs={{0,4},{2,6},{4,0},{6,2},{8,12},{10,14},{12,8},{14,10},{1,5},{3,7},... | collective-permute-start | bytes 589832 | tf_op jit(solution)/shard_map/ppermute | solution.py:196
  70.6 0.1 pad_add_fusion.place_ref
  70.7 7.3 %collective-permute-done.3 = bf16[2,192,256]{2,1,0:T(8,128)(2,1)S(1)} collective-permute-done((bf16[2,192,256]{2,1,0:T(8,128)(2,1)S(1)}, bf16[2,192,256]{2,1,0:T(8,128)(2,1)S(1)}, u32[]{:S(2)}, u32[]{:S(2)}) %collective-permute-start.3) | collective-permute-done | bytes 196640 | tf_op jit(solution)/shard_map/ppermute | solution.py:196
  78.1 0.0 copy-start.2
  78.1 5.8 %collective-permute-start.5 = (bf16[4,192,256]{2,1,0:T(8,128)(2,1)S(1)}, bf16[4,192,256]{2,1,0:T(8,128)(2,1)S(1)}, u32[]{:S(2)}, u32[]{:S(2)}) collective-permute-start(bf16[4,192,256]{2,1,0:T(8,128)(2,1)S(1)} %pad_maximum_fusion.g00_ref), channel_id=1, source_target_pairs={{0,2},{2,0},{4,6},{6,4},{8,10},{10,8},{12,14},{14,12},{1,3},{3,1},... | collective-permute-start | bytes 1179656 | tf_op jit(solution)/shard_map/ppermute | solution.py:198
  83.9 0.0 collective-permute-done.other_ref
  84.0 4.8 %shard_map.68 = (f32[256,256]{1,0:T(8,128)}, f32[4,256,256]{2,1,0:T(8,128)}) custom-call(s32[2]{0:T(128)S(1)} %pad_add_fusion.place_ref, s32[64]{0:T(128)S(1)} %copy-done.2, s32[64,128]{1,0:T(8,128)S(1)} %bitcast.12, bf16[256,256]{1,0:T(8,128)(2,1)S(1)} %copy-done, bf16[32,128,128]{2,1,0:T(8,128)(2,1)S(1)} %bitcast.11, ...), custom_call_target="tpu_custom_call" | custom-call | flops 1200000000 | bytes 4000000 | tf_op jit(solution)/shard_map/pallas_call | solution.py:110
  88.7 3.5 %all-to-all-start.2 = ((f32[4,256,256]{2,1,0:T(8,128)}), f32[4,256,256]{2,1,0:T(8,128)S(1)}, u32[]{:S(2)}, u32[]{:S(2)}) async-start(f32[4,256,256]{2,1,0:T(8,128)} %get-tuple-element.7), calls=%async_computation.2 | async-start | bytes 2097152 | tf_op jit(solution)/shard_map/all_to_all | solution.py:204
  92.3 1.9 %collective-permute-start.4 = (bf16[4,192,256]{2,1,0:T(8,128)(2,1)S(1)}, bf16[4,192,256]{2,1,0:T(8,128)(2,1)S(1)}, u32[]{:S(2)}, u32[]{:S(2)}) collective-permute-start(bf16[4,192,256]{2,1,0:T(8,128)(2,1)S(1)} %pad_maximum_fusion.g00_ref), channel_id=1, source_target_pairs={{0,1},{1,0},{2,3},{3,2},{4,5},{5,4},{6,7},{7,6},{8,9},{9,8},{10,11... | collective-permute-start | bytes 1179656 | tf_op jit(solution)/shard_map/ppermute | solution.py:199
  94.2 0.0 collective-permute-done.5.g10_ref
  94.2 2.4 %collective-permute-start.6 = (bf16[4,192,256]{2,1,0:T(8,128)(2,1)S(1)}, bf16[4,192,256]{2,1,0:T(8,128)(2,1)S(1)}, u32[]{:S(2)}, u32[]{:S(2)}) collective-permute-start(bf16[4,192,256]{2,1,0:T(8,128)(2,1)S(1)} %collective-permute-done.5.g10_ref), channel_id=1, source_target_pairs={{0,1},{1,0},{2,3},{3,2},{4,5},{5,4},{6,7},{7,6},{8,9},{9,8},{10,11... | collective-permute-start | bytes 1179656 | tf_op jit(solution)/shard_map/ppermute | solution.py:200
  96.6 0.1 pad_add_fusion.1.place_ref
  96.7 0.0 collective-permute-done.4.g01_ref
  96.7 1.2 collective-permute-done.6.g11_ref
  98.0 9.4 %all-to-all-done.2.a_ref = f32[4,256,256]{2,1,0:T(8,128)S(1)} async-done(((f32[4,256,256]{2,1,0:T(8,128)}), f32[4,256,256]{2,1,0:T(8,128)S(1)}, u32[]{:S(2)}, u32[]{:S(2)}) %all-to-all-start.2) | async-done | bytes 1048608 | tf_op jit(solution)/shard_map/all_to_all | solution.py:204
  107.4 2.6 %shard_map.69 = (bf16[4,192,256]{2,1,0:T(8,128)(2,1)}, f32[96,256]{1,0:T(8,128)S(1)}) custom-call(s32[3]{0:T(128)S(1)} %pad_add_fusion.1.place_ref, bf16[4,192,256]{2,1,0:T(8,128)(2,1)S(1)} %pad_maximum_fusion.g00_ref, bf16[4,192,256]{2,1,0:T(8,128)(2,1)S(1)} %collective-permute-done.4.g01_ref, bf16[4,192,256]{2,1,0:T(8,128)(2,1)S(1)} %collective-permute-done.5.g10_ref, ...), custom_call_target="tpu_custom_call" | custom-call | flops 900000000 | bytes 3000000 | tf_op jit(solution)/shard_map/pallas_call | solution.py:154
  109.9 3.5 %all-to-all-start.3 = ((bf16[8,96,256]{2,1,0:T(8,128)(2,1)}), bf16[8,96,256]{2,1,0:T(8,128)(2,1)S(1)}, u32[]{:S(2)}, u32[]{:S(2)}) async-start(bf16[8,96,256]{2,1,0:T(8,128)(2,1)} %bitcast.9), calls=%async_computation.3 | async-start | bytes 786432 | tf_op jit(solution)/shard_map/all_to_all | solution.py:208
  113.4 13.8 %all-to-all-done.3 = bf16[8,96,256]{2,1,0:T(8,128)(2,1)S(1)} async-done(((bf16[8,96,256]{2,1,0:T(8,128)(2,1)}), bf16[8,96,256]{2,1,0:T(8,128)(2,1)S(1)}, u32[]{:S(2)}, u32[]{:S(2)}) %all-to-all-start.3) | async-done | bytes 393248 | tf_op jit(solution)/shard_map/all_to_all | solution.py:208
  127.2 0.1 select_reduce_fusion
  127.3 0.7 slice_add_fusion
  (11 shorter events, 0.1 us)
Async XLA Ops:
  0.6 0.8 dynamic-slice-start
  20.5 19.6 %copy-start.3 = (bf16[256,180]{0,1:T(8,128)(2,1)S(1)}, bf16[256,180]{0,1:T(8,128)(2,1)}, u32[]{:S(2)}) copy-start(bf16[256,180]{0,1:T(8,128)(2,1)} %param.7) | copy-start | bytes 276484
  38.1 45.8 %collective-permute-start = (bf16[32,128,128]{2,1,0:T(8,128)(2,1)S(1)}, bf16[32,128,128]{2,1,0:T(8,128)(2,1)S(1)}, u32[]{:S(2)}, u32[]{:S(2)}) collective-permute-start(bf16[32,128,128]{2,1,0:T(8,128)(2,1)S(1)} %bitcast.10), channel_id=1, source_target_pairs={{0,1},{1,0},{2,3},{3,2},{4,5},{5,4},{6,7},{7,6},{8,9},{9,8},{10,11... | collective-permute-start | bytes 3145736 | tf_op jit(solution)/shard_map/ppermute | solution.py:192
  40.1 0.7 collective-permute-start.1
  40.8 27.5 %collective-permute-start.2 = (bf16[1,192,256]{2,1,0:T(8,128)(2,1)S(1)}, bf16[1,192,256]{2,1,0:T(8,128)(2,1)S(1)}, u32[]{:S(2)}, u32[]{:S(2)}) collective-permute-start(bf16[1,192,256]{2,1,0:T(8,128)(2,1)S(1)} %bitcast.13), channel_id=1, source_target_pairs={{0,8},{2,10},{4,12},{6,14},{8,0},{10,2},{12,4},{14,6},{1,9},{3,11}... | collective-permute-start | bytes 294920 | tf_op jit(solution)/shard_map/ppermute | solution.py:196
  68.3 9.7 %collective-permute-start.3 = (bf16[2,192,256]{2,1,0:T(8,128)(2,1)S(1)}, bf16[2,192,256]{2,1,0:T(8,128)(2,1)S(1)}, u32[]{:S(2)}, u32[]{:S(2)}) collective-permute-start(bf16[2,192,256]{2,1,0:T(8,128)(2,1)S(1)} %pad_maximum_fusion.1), channel_id=1, source_target_pairs={{0,4},{2,6},{4,0},{6,2},{8,12},{10,14},{12,8},{14,10},{1,5},{3,7},... | collective-permute-start | bytes 589832 | tf_op jit(solution)/shard_map/ppermute | solution.py:196
  70.7 13.2 %copy-start = (bf16[256,256]{1,0:T(8,128)(2,1)S(1)}, bf16[256,256]{1,0:T(8,128)(2,1)}, u32[]{:S(2)}) copy-start(bf16[256,256]{1,0:T(8,128)(2,1)} %q_ref.1) | copy-start | bytes 393220
  70.7 13.2 %copy-start.1 = (s32[8192]{0:T(1024)S(1)}, s32[8192]{0:T(1024)}, u32[]{:S(2)}) copy-start(s32[8192]{0:T(1024)} %param.8) | copy-start | bytes 98308
  78.1 5.9 %copy-start.2 = (s32[64]{0:T(128)S(1)}, s32[64]{0:T(128)}, u32[]{:S(2)}) copy-start(s32[64]{0:T(128)} %tiles_ref.1) | copy-start | bytes 772
  78.1 16.1 %collective-permute-start.5 = (bf16[4,192,256]{2,1,0:T(8,128)(2,1)S(1)}, bf16[4,192,256]{2,1,0:T(8,128)(2,1)S(1)}, u32[]{:S(2)}, u32[]{:S(2)}) collective-permute-start(bf16[4,192,256]{2,1,0:T(8,128)(2,1)S(1)} %pad_maximum_fusion.g00_ref), channel_id=1, source_target_pairs={{0,2},{2,0},{4,6},{6,4},{8,10},{10,8},{12,14},{14,12},{1,3},{3,1},... | collective-permute-start | bytes 1179656 | tf_op jit(solution)/shard_map/ppermute | solution.py:198
  88.7 18.6 %all-to-all-start.2 = ((f32[4,256,256]{2,1,0:T(8,128)}), f32[4,256,256]{2,1,0:T(8,128)S(1)}, u32[]{:S(2)}, u32[]{:S(2)}) async-start(f32[4,256,256]{2,1,0:T(8,128)} %get-tuple-element.7), calls=%async_computation.2 | async-start | bytes 2097152 | tf_op jit(solution)/shard_map/all_to_all | solution.py:204
  92.3 4.4 %collective-permute-start.4 = (bf16[4,192,256]{2,1,0:T(8,128)(2,1)S(1)}, bf16[4,192,256]{2,1,0:T(8,128)(2,1)S(1)}, u32[]{:S(2)}, u32[]{:S(2)}) collective-permute-start(bf16[4,192,256]{2,1,0:T(8,128)(2,1)S(1)} %pad_maximum_fusion.g00_ref), channel_id=1, source_target_pairs={{0,1},{1,0},{2,3},{3,2},{4,5},{5,4},{6,7},{7,6},{8,9},{9,8},{10,11... | collective-permute-start | bytes 1179656 | tf_op jit(solution)/shard_map/ppermute | solution.py:199
  94.2 3.7 %collective-permute-start.6 = (bf16[4,192,256]{2,1,0:T(8,128)(2,1)S(1)}, bf16[4,192,256]{2,1,0:T(8,128)(2,1)S(1)}, u32[]{:S(2)}, u32[]{:S(2)}) collective-permute-start(bf16[4,192,256]{2,1,0:T(8,128)(2,1)S(1)} %collective-permute-done.5.g10_ref), channel_id=1, source_target_pairs={{0,1},{1,0},{2,3},{3,2},{4,5},{5,4},{6,7},{7,6},{8,9},{9,8},{10,11... | collective-permute-start | bytes 1179656 | tf_op jit(solution)/shard_map/ppermute | solution.py:200
  109.9 17.2 %all-to-all-start.3 = ((bf16[8,96,256]{2,1,0:T(8,128)(2,1)}), bf16[8,96,256]{2,1,0:T(8,128)(2,1)S(1)}, u32[]{:S(2)}, u32[]{:S(2)}) async-start(bf16[8,96,256]{2,1,0:T(8,128)(2,1)} %bitcast.9), calls=%async_computation.3 | async-start | bytes 786432 | tf_op jit(solution)/shard_map/all_to_all | solution.py:208

commit v9 on v8

--- a/solution.py
+++ b/solution.py
@@ -17,7 +17,7 @@
 
 
 def attention_kernel(
-    place_ref, tiles_ref, docs_ref, q_ref, own_ref, other_ref, out_ref, send_ref, slot_ref, s_ref, o_ref, sems
+    place_ref, tiles_ref, docs_ref, q_ref, own_ref, other_ref, out_ref, send_ref, slot_ref, s_ref, o_ref, b_ref, sems
 ):
     core = place_ref[0]
     width = HEADS * TILE
@@ -93,10 +93,11 @@
             )
             both = jnp.transpose(both)
             o_ref[part, :, h * DH:(h + 2) * DH] = both
+            b_ref[part, :, h * DH:(h + 2) * DH] = both.astype(b_ref.dtype)
         rows = pl.ds(part * TILE, TILE)
         copies.append(pltpu.make_async_copy(o_ref.at[part], out_ref.at[rows], sems.at[part, 0]))
         for peer in range(send_ref.shape[0]):
-            copies.append(pltpu.make_async_copy(o_ref.at[part], send_ref.at[peer, rows], sems.at[part, 1 + peer]))
+            copies.append(pltpu.make_async_copy(b_ref.at[part], send_ref.at[peer, rows], sems.at[part, 1 + peer]))
         for copy in copies[-1 - send_ref.shape[0]:]:
             copy.start()
     for copy in copies:
@@ -111,7 +112,7 @@
         attention_kernel,
         out_shape=(
             jax.ShapeDtypeStruct((rows, columns), jnp.float32),
-            jax.ShapeDtypeStruct((peers, rows, columns), jnp.float32),
+            jax.ShapeDtypeStruct((peers, rows, columns), jnp.bfloat16),
         ),
         in_specs=[smem, smem, vmem, vmem, vmem, vmem],
         out_specs=(pl.BlockSpec(memory_space=pl.ANY), pl.BlockSpec(memory_space=pl.ANY)),
@@ -119,6 +120,7 @@
             pltpu.SMEM((tiles.shape[0],), jnp.int32),
             pltpu.VMEM((SPAN * TILE, HEADS * TILE), jnp.float32),
             pltpu.VMEM((2, TILE, columns), jnp.float32),
+            pltpu.VMEM((2, TILE, columns), jnp.bfloat16),
             pltpu.SemaphoreType.DMA((2, 1 + peers)),
         ],
         cost_estimate=pl.CostEstimate(flops=1_200_000_000, bytes_accessed=4_000_000, transcendentals=2_200_000),
@@ -126,47 +128,35 @@
     )(place, tiles, docs.reshape(-1, TILE), queries, own, other)
 
 
-def term_kernel(place_ref, g00_ref, g01_ref, g10_ref, g11_ref, a_ref, out_ref, own_ref, high_ref, low_ref, sum_ref):
-    core, z, y = place_ref[0], place_ref[1], place_ref[2]
-    a = a_ref[...]
-    high = a.astype(jnp.bfloat16)
-    high_ref[...] = high
-    low_ref[...] = (a - high.astype(jnp.float32)).astype(jnp.bfloat16)
+def term_kernel(place_ref, g00_ref, g01_ref, g10_ref, g11_ref, a_ref, own_ref, out_ref):
+    core, z, x = place_ref[0], place_ref[1], place_ref[2]
+    zx = lax.shift_right_logical(z, 1)
+    apart = zx ^ x
+    at = ((apart & 1) << 1) | lax.shift_right_logical(apart, 1)
+    a = own_ref[...]
+    low = (a - a.astype(jnp.bfloat16).astype(jnp.float32)).astype(jnp.bfloat16)
     for flip, sides in enumerate(((g00_ref, g01_ref), (g10_ref, g11_ref))):
         pair = (z & 1) ^ flip
         for side, g_ref in zip((core, 1 - core), sides, strict=True):
-            term = None
+            term = jnp.dot(g_ref[at], low, preferred_element_type=jnp.float32)
             for i in range(g_ref.shape[0]):
-                peer = lax.shift_right_logical(z, 1) ^ (((i & 1) << 1) | (i >> 1))
-                for half_ref in (high_ref, low_ref):
-                    part = jnp.dot(g_ref[i], half_ref[peer], preferred_element_type=jnp.float32)
-                    term = part if term is None else term + part
-            sum_ref[2 * pair + side] = term
-            out_ref[2 * pair + side] = term.astype(out_ref.dtype)
-    own_ref[...] = sum_ref[lax.shift_right_logical(y, 1), pl.ds(pl.multiple_of((y & 1) * PADDED, PADDED), PADDED), :]
-
-
-def term_of(place, grads, gathered):
+                peer = zx ^ (((i & 1) << 1) | (i >> 1))
+                term = term + jnp.dot(g_ref[i], a_ref[peer], preferred_element_type=jnp.float32)
+            out_ref[2 * pair + side] = term
+
+
+def term_of(place, grads, gathered, attended):
     smem = pl.BlockSpec(memory_space=pltpu.SMEM)
     vmem = pl.BlockSpec(memory_space=pltpu.VMEM)
     blocks, rows = grads[0].shape[0], grads[0].shape[1]
-    columns = gathered.shape[2]
     return pl.pallas_call(
         term_kernel,
-        out_shape=(
-            jax.ShapeDtypeStruct((blocks, rows, columns), jnp.bfloat16),
-            jax.ShapeDtypeStruct((PADDED, columns), jnp.float32),
-        ),
-        in_specs=[smem] + [vmem] * 5,
-        out_specs=(vmem, vmem),
-        scratch_shapes=[
-            pltpu.VMEM(gathered.shape, jnp.bfloat16),
-            pltpu.VMEM(gathered.shape, jnp.bfloat16),
-            pltpu.VMEM((blocks, rows, columns), jnp.float32),
-        ],
-        cost_estimate=pl.CostEstimate(flops=900_000_000, bytes_accessed=3_000_000, transcendentals=0),
+        out_shape=jax.ShapeDtypeStruct((blocks, rows, attended.shape[1]), jnp.float32),
+        in_specs=[smem] + [vmem] * 6,
+        out_specs=vmem,
+        cost_estimate=pl.CostEstimate(flops=500_000_000, bytes_accessed=3_000_000, transcendentals=0),
         compiler_params=pltpu.CompilerParams(vmem_limit_bytes=32 << 20),
-    )(place, *grads, gathered)
+    )(place, *grads, gathered, attended)
 
 
 def everyone(x, axes, size):
@@ -184,17 +174,17 @@
     grads = jnp.pad(jnp.transpose(grad_rows).reshape(2, BLOCK, tokens), ((0, 0), (0, PADDED - BLOCK), (0, 0)))
     grads = grads.reshape(2 * PADDED, tokens)
     turn = [(a * nz + half * b + c, b * nz + half * a + c) for a in range(nx) for b in range(nx) for c in range(half)]
-    grads = lax.ppermute(grads, ("x", "z"), turn)
+    home = lax.ppermute(grads, ("x", "z"), turn)
+    far = lax.ppermute(grads, ("x", "z"), [(i, j ^ 4) for i, j in turn])
 
     mine = lax.dynamic_slice(keys_values, (core * TILE, lax.axis_index("z") * (2 * DH)), (TILE, 2 * DH))
     own = everyone(mine, "y", ny)
     own = everyone(own, "x", nx).reshape(nx * ny, TILE, 2 * DH)
     other = lax.ppermute(own, "core", swap)
 
-    g_own = grads[None]
-    for bit in (4, 2):
-        came = lax.ppermute(g_own, "z", [(i, i ^ bit) for i in range(nz)])
-        g_own = jnp.concatenate([g_own, came], axis=0)
+    g_own = jnp.stack([home, far])
+    came = lax.ppermute(g_own, "z", [(i, i ^ 2) for i in range(nz)])
+    g_own = jnp.concatenate([g_own, came], axis=0)
     g_next = lax.ppermute(g_own, "z", [(i, i ^ 1) for i in range(nz)])
     g_other = lax.ppermute(g_own, "core", swap)
     g_both = lax.ppermute(g_next, "core", swap)
@@ -202,12 +192,10 @@
     place = jnp.stack([core, 2 * ctx])
     attended, send = attention(place, tile_list, doc_ids, queries, own, other, nx)
     gathered = lax.all_to_all(send, "x", 0, 0)
-    y = lax.axis_index("y")
-    place = jnp.stack([core, lax.axis_index("z"), y])
-    term, mine = term_of(place, (g_own, g_other, g_next, g_both), gathered)
+    place = jnp.stack([core, lax.axis_index("z"), x])
+    term = term_of(place, (g_own, g_other, g_next, g_both), gathered, attended)
     parts = lax.all_to_all(term.reshape(ny, PADDED, -1), "y", 0, 0)
-    others = lax.broadcasted_iota(jnp.int32, parts.shape, 0) != y
-    weight_grad = (mine + jnp.sum(jnp.where(others, parts.astype(jnp.float32), 0.0), axis=0))[:BLOCK]
+    weight_grad = jnp.sum(parts, axis=0)[:BLOCK]
     return attended, weight_grad
 
 

time: 129 us -> 140 us (1.085)
  the two profiles are of different devices: /device:TPU:64 before, /device:TPU:2 now
where the time goes in v9:
time: 140 us
  blocking collectives  62.2 us (44%)
  starting transfers between devices  35 us (25%)
  waiting for transfers between devices  32.9 us (24%)
  Pallas kernels  6.57 us (5%)
    all_to_all x2, blocking collectives, everyone(): lax.all_to_all(jnp.broadcast_to(x[None], (size,) + x.shape), axes, 0, 0)  35.5 us
    all_to_all x1, blocking collectives, on_device(): parts = lax.all_to_all(term.reshape(ny, PADDED, -1), 'y', 0, 0)  26.7 us
    all_to_all x1, starting transfers between devices, on_device(): gathered = lax.all_to_all(send, 'x', 0, 0)  9.74 us
    ppermute x1, waiting for transfers between devices, on_device(): came = lax.ppermute(g_own, 'z', [(i, i ^ 2) for i in range(nz)])  9.71 us
    all_to_all x1, waiting for transfers between devices, on_device(): gathered = lax.all_to_all(send, 'x', 0, 0)  8.61 us
    ppermute x1, waiting for transfers between devices, on_device(): g_next = lax.ppermute(g_own, 'z', [(i, i ^ 1) for i in range(nz)])  7.67 us
    ppermute x1, starting transfers between devices, on_device(): home = lax.ppermute(grads, ('x', 'z'), turn)  6.99 us
    ppermute x1, waiting for transfers between devices, on_device(): far = lax.ppermute(grads, ('x', 'z'), [(i, j ^ 4) for i, j in turn])  6.93 us
  transfers between devices with their start and end apart: 8, of which 4 were waited for; matrix products, arithmetic and copies ran while one was open for 0% of the time, Pallas kernels for 4%

profile of v9, /device:TPU:2, one launch (start us, length us, event | category | flops | bytes accessed | tf_op | source)
XLA Modules:
  0.0 139.5 jit_solution(16773342223125134174)
XLA Ops:
  0.6 0.0 dynamic-slice-start
  0.7 0.7 dynamic-slice-done
  1.4 18.8 %all_to_all.20 = bf16[8,128,128]{2,1,0:T(8,128)(2,1)S(1)} all-to-all(bf16[8,128,128]{2,1,0:T(8,128)(2,1)S(1)} %broadcast_in_dim.4), channel_id=1, replica_groups=mesh['x'=4,'y'=8,'z'=8,'core'=2] {'y'}, dimensions={0} | all-to-all | bytes 524288 | tf_op jit(solution)/shard_map/all_to_all | solution.py:163
  20.2 0.2 broadcast_in_dim.5
  20.5 0.0 copy-start.4
  20.5 16.7 %all_to_all.21 = bf16[4,8,128,128]{3,2,1,0:T(8,128)(2,1)S(1)} all-to-all(bf16[4,8,128,128]{3,2,1,0:T(8,128)(2,1)S(1)} %broadcast_in_dim.5), channel_id=1, replica_groups=mesh['x'=4,'y'=8,'z'=8,'core'=2] {'x'}, dimensions={0} | all-to-all | bytes 2097152 | tf_op jit(solution)/shard_map/all_to_all | solution.py:163
  37.2 1.9 %collective-permute-start = (bf16[32,128,128]{2,1,0:T(8,128)(2,1)S(1)}, bf16[32,128,128]{2,1,0:T(8,128)(2,1)}, u32[]{:S(2)}, u32[]{:S(2)}) collective-permute-start(bf16[32,128,128]{2,1,0:T(8,128)(2,1)S(1)} %bitcast.13), channel_id=1, source_target_pairs={{0,1},{1,0},{2,3},{3,2},{4,5},{5,4},{6,7},{7,6},{8,9},{9,8},{10,11... | collective-permute-start | bytes 3145736 | tf_op jit(solution)/shard_map/ppermute | solution.py:183
  39.2 7.0 %collective-permute-start.1 = (bf16[192,256]{1,0:T(8,128)(2,1)S(1)}, bf16[192,256]{1,0:T(8,128)(2,1)S(1)}, u32[]{:S(2)}, u32[]{:S(2)}) collective-permute-start(bf16[192,256]{1,0:T(8,128)(2,1)S(1)} %bitcast.21), channel_id=1, source_target_pairs={{0,0},{2,2},{4,128},{6,130},{8,256},{10,258},{12,384},{14,386},{12... | collective-permute-start | bytes 294920 | tf_op jit(solution)/shard_map/ppermute | solution.py:177
  46.2 6.8 %collective-permute-start.2 = (bf16[192,256]{1,0:T(8,128)(2,1)S(1)}, bf16[192,256]{1,0:T(8,128)(2,1)S(1)}, u32[]{:S(2)}, u32[]{:S(2)}) collective-permute-start(bf16[192,256]{1,0:T(8,128)(2,1)S(1)} %bitcast.22), channel_id=1, source_target_pairs={{0,8},{2,10},{4,136},{6,138},{8,264},{10,266},{12,392},{14,394},{1... | collective-permute-start | bytes 294920 | tf_op jit(solution)/shard_map/ppermute | solution.py:178
  52.9 0.0 collective-permute-done.1
  53.0 6.9 %collective-permute-done.2 = bf16[192,256]{1,0:T(8,128)(2,1)S(1)} collective-permute-done((bf16[192,256]{1,0:T(8,128)(2,1)S(1)}, bf16[192,256]{1,0:T(8,128)(2,1)S(1)}, u32[]{:S(2)}, u32[]{:S(2)}) %collective-permute-start.2) | collective-permute-done | bytes 98336 | tf_op jit(solution)/shard_map/ppermute | solution.py:178
  59.9 0.0 copy-start.1
  59.9 0.0 copy-start.2
  59.9 3.7 %collective-permute-start.3 = (bf16[2,192,256]{2,1,0:T(8,128)(2,1)S(1)}, bf16[2,192,256]{2,1,0:T(8,128)(2,1)S(1)}, u32[]{:S(2)}, u32[]{:S(2)}) collective-permute-start(bf16[2,192,256]{2,1,0:T(8,128)(2,1)S(1)} %pad_maximum_fusion.1), channel_id=1, source_target_pairs={{0,4},{2,6},{4,0},{6,2},{8,12},{10,14},{12,8},{14,10},{1,5},{3,7},... | collective-permute-start | bytes 589832 | tf_op jit(solution)/shard_map/ppermute | solution.py:186
  63.6 9.7 %collective-permute-done.3 = bf16[2,192,256]{2,1,0:T(8,128)(2,1)S(1)} collective-permute-done((bf16[2,192,256]{2,1,0:T(8,128)(2,1)S(1)}, bf16[2,192,256]{2,1,0:T(8,128)(2,1)S(1)}, u32[]{:S(2)}, u32[]{:S(2)}) %collective-permute-start.3) | collective-permute-done | bytes 196640 | tf_op jit(solution)/shard_map/ppermute | solution.py:186
  73.4 1.9 %collective-permute-start.5 = (bf16[4,192,256]{2,1,0:T(8,128)(2,1)S(1)}, bf16[4,192,256]{2,1,0:T(8,128)(2,1)S(1)}, u32[]{:S(2)}, u32[]{:S(2)}) collective-permute-start(bf16[4,192,256]{2,1,0:T(8,128)(2,1)S(1)} %pad_maximum_fusion.g00_ref), channel_id=1, source_target_pairs={{0,2},{2,0},{4,6},{6,4},{8,10},{10,8},{12,14},{14,12},{1,3},{3,1},... | collective-permute-start | bytes 1179656 | tf_op jit(solution)/shard_map/ppermute | solution.py:188
  75.3 0.1 pad_add_fusion.place_ref
  75.4 2.0 %collective-permute-start.4 = (bf16[4,192,256]{2,1,0:T(8,128)(2,1)S(1)}, bf16[4,192,256]{2,1,0:T(8,128)(2,1)S(1)}, u32[]{:S(2)}, u32[]{:S(2)}) collective-permute-start(bf16[4,192,256]{2,1,0:T(8,128)(2,1)S(1)} %pad_maximum_fusion.g00_ref), channel_id=1, source_target_pairs={{0,1},{1,0},{2,3},{3,2},{4,5},{5,4},{6,7},{7,6},{8,9},{9,8},{10,11... | collective-permute-start | bytes 1179656 | tf_op jit(solution)/shard_map/ppermute | solution.py:189
  77.5 7.7 %collective-permute-done.5.g10_ref = bf16[4,192,256]{2,1,0:T(8,128)(2,1)S(1)} collective-permute-done((bf16[4,192,256]{2,1,0:T(8,128)(2,1)S(1)}, bf16[4,192,256]{2,1,0:T(8,128)(2,1)S(1)}, u32[]{:S(2)}, u32[]{:S(2)}) %collective-permute-start.5) | collective-permute-done | bytes 393248 | tf_op jit(solution)/shard_map/ppermute | solution.py:188
  85.1 1.9 %collective-permute-start.6 = (bf16[4,192,256]{2,1,0:T(8,128)(2,1)S(1)}, bf16[4,192,256]{2,1,0:T(8,128)(2,1)S(1)}, u32[]{:S(2)}, u32[]{:S(2)}) collective-permute-start(bf16[4,192,256]{2,1,0:T(8,128)(2,1)S(1)} %collective-permute-done.5.g10_ref), channel_id=1, source_target_pairs={{0,1},{1,0},{2,3},{3,2},{4,5},{5,4},{6,7},{7,6},{8,9},{9,8},{10,11... | collective-permute-start | bytes 1179656 | tf_op jit(solution)/shard_map/ppermute | solution.py:190
  87.0 0.0 collective-permute-done.other_ref
  87.0 0.0 copy-done.1
  87.1 5.3 %shard_map.68 = (f32[256,256]{1,0:T(8,128)}, bf16[4,256,256]{2,1,0:T(8,128)(2,1)}) custom-call(s32[2]{0:T(128)S(1)} %pad_add_fusion.place_ref, s32[64]{0:T(128)S(1)} %copy-done.3, s32[64,128]{1,0:T(8,128)S(1)} %bitcast.15, bf16[256,256]{1,0:T(8,128)(2,1)S(1)} %copy-done.1, bf16[32,128,128]{2,1,0:T(8,128)(2,1)S(1)} %bitcast.14, ...), custom_call_target="tpu_custom_call" | custom-call | flops 1200000000 | bytes 4000000 | tf_op jit(solution)/shard_map/pallas_call | solution.py:111
  92.4 0.0 copy-start
  92.4 9.7 %all-to-all-start.2 = ((bf16[4,256,256]{2,1,0:T(8,128)(2,1)}), bf16[4,256,256]{2,1,0:T(8,128)(2,1)S(1)}, u32[]{:S(2)}, u32[]{:S(2)}) async-start(bf16[4,256,256]{2,1,0:T(8,128)(2,1)} %get-tuple-element.5), calls=%async_computation.2 | async-start | bytes 1048576 | tf_op jit(solution)/shard_map/all_to_all | solution.py:194
  102.2 0.1 pad_add_fusion.1.place_ref
  102.3 0.0 collective-permute-done.4.g01_ref
  102.3 0.0 collective-permute-done.6.g11_ref
  102.3 8.6 %all-to-all-done.2.a_ref = bf16[4,256,256]{2,1,0:T(8,128)(2,1)S(1)} async-done(((bf16[4,256,256]{2,1,0:T(8,128)(2,1)}), bf16[4,256,256]{2,1,0:T(8,128)(2,1)S(1)}, u32[]{:S(2)}, u32[]{:S(2)}) %all-to-all-start.2) | async-done | bytes 524320 | tf_op jit(solution)/shard_map/all_to_all | solution.py:194
  110.9 1.2 shard_map.69
  112.1 26.7 %all_to_all.22 = f32[8,96,256]{2,1,0:T(8,128)S(1)} all-to-all(f32[8,96,256]{2,1,0:T(8,128)S(1)} %bitcast.12), channel_id=1, replica_groups=mesh['x'=4,'y'=8,'z'=8,'core'=2] {'y'}, dimensions={0} | all-to-all | bytes 1572864 | tf_op jit(solution)/shard_map/all_to_all | solution.py:197
  138.8 0.7 reduce_sum.9
  (10 shorter events, 0.1 us)
Async XLA Ops:
  0.6 0.8 dynamic-slice-start
  20.5 18.7 %copy-start.4 = (bf16[256,180]{0,1:T(8,128)(2,1)S(1)}, bf16[256,180]{0,1:T(8,128)(2,1)}, u32[]{:S(2)}) copy-start(bf16[256,180]{0,1:T(8,128)(2,1)} %param.7) | copy-start | bytes 276484
  37.2 49.8 %collective-permute-start = (bf16[32,128,128]{2,1,0:T(8,128)(2,1)S(1)}, bf16[32,128,128]{2,1,0:T(8,128)(2,1)}, u32[]{:S(2)}, u32[]{:S(2)}) collective-permute-start(bf16[32,128,128]{2,1,0:T(8,128)(2,1)S(1)} %bitcast.13), channel_id=1, source_target_pairs={{0,1},{1,0},{2,3},{3,2},{4,5},{5,4},{6,7},{7,6},{8,9},{9,8},{10,11... | collective-permute-start | bytes 3145736 | tf_op jit(solution)/shard_map/ppermute | solution.py:183
  39.2 13.8 %collective-permute-start.1 = (bf16[192,256]{1,0:T(8,128)(2,1)S(1)}, bf16[192,256]{1,0:T(8,128)(2,1)S(1)}, u32[]{:S(2)}, u32[]{:S(2)}) collective-permute-start(bf16[192,256]{1,0:T(8,128)(2,1)S(1)} %bitcast.21), channel_id=1, source_target_pairs={{0,0},{2,2},{4,128},{6,130},{8,256},{10,258},{12,384},{14,386},{12... | collective-permute-start | bytes 294920 | tf_op jit(solution)/shard_map/ppermute | solution.py:177
  46.2 13.7 %collective-permute-start.2 = (bf16[192,256]{1,0:T(8,128)(2,1)S(1)}, bf16[192,256]{1,0:T(8,128)(2,1)S(1)}, u32[]{:S(2)}, u32[]{:S(2)}) collective-permute-start(bf16[192,256]{1,0:T(8,128)(2,1)S(1)} %bitcast.22), channel_id=1, source_target_pairs={{0,8},{2,10},{4,136},{6,138},{8,264},{10,266},{12,392},{14,394},{1... | collective-permute-start | bytes 294920 | tf_op jit(solution)/shard_map/ppermute | solution.py:178
  59.9 27.1 %copy-start.1 = (bf16[256,256]{1,0:T(8,128)(2,1)S(1)}, bf16[256,256]{1,0:T(8,128)(2,1)}, u32[]{:S(2)}) copy-start(bf16[256,256]{1,0:T(8,128)(2,1)} %q_ref.1) | copy-start | bytes 393220
  59.9 27.1 %copy-start.2 = (s32[8192]{0:T(1024)S(1)}, s32[8192]{0:T(1024)}, u32[]{:S(2)}) copy-start(s32[8192]{0:T(1024)} %param.8) | copy-start | bytes 98308
  59.9 13.4 %collective-permute-start.3 = (bf16[2,192,256]{2,1,0:T(8,128)(2,1)S(1)}, bf16[2,192,256]{2,1,0:T(8,128)(2,1)S(1)}, u32[]{:S(2)}, u32[]{:S(2)}) collective-permute-start(bf16[2,192,256]{2,1,0:T(8,128)(2,1)S(1)} %pad_maximum_fusion.1), channel_id=1, source_target_pairs={{0,4},{2,6},{4,0},{6,2},{8,12},{10,14},{12,8},{14,10},{1,5},{3,7},... | collective-permute-start | bytes 589832 | tf_op jit(solution)/shard_map/ppermute | solution.py:186
  73.4 11.7 %collective-permute-start.5 = (bf16[4,192,256]{2,1,0:T(8,128)(2,1)S(1)}, bf16[4,192,256]{2,1,0:T(8,128)(2,1)S(1)}, u32[]{:S(2)}, u32[]{:S(2)}) collective-permute-start(bf16[4,192,256]{2,1,0:T(8,128)(2,1)S(1)} %pad_maximum_fusion.g00_ref), channel_id=1, source_target_pairs={{0,2},{2,0},{4,6},{6,4},{8,10},{10,8},{12,14},{14,12},{1,3},{3,1},... | collective-permute-start | bytes 1179656 | tf_op jit(solution)/shard_map/ppermute | solution.py:188
  75.4 11.7 %copy-start.3 = (s32[64]{0:T(128)S(1)}, s32[64]{0:T(128)}, u32[]{:S(2)}) copy-start(s32[64]{0:T(128)} %tiles_ref.1) | copy-start | bytes 772
  75.4 26.9 %collective-permute-start.4 = (bf16[4,192,256]{2,1,0:T(8,128)(2,1)S(1)}, bf16[4,192,256]{2,1,0:T(8,128)(2,1)S(1)}, u32[]{:S(2)}, u32[]{:S(2)}) collective-permute-start(bf16[4,192,256]{2,1,0:T(8,128)(2,1)S(1)} %pad_maximum_fusion.g00_ref), channel_id=1, source_target_pairs={{0,1},{1,0},{2,3},{3,2},{4,5},{5,4},{6,7},{7,6},{8,9},{9,8},{10,11... | collective-permute-start | bytes 1179656 | tf_op jit(solution)/shard_map/ppermute | solution.py:189
  85.1 17.1 %collective-permute-start.6 = (bf16[4,192,256]{2,1,0:T(8,128)(2,1)S(1)}, bf16[4,192,256]{2,1,0:T(8,128)(2,1)S(1)}, u32[]{:S(2)}, u32[]{:S(2)}) collective-permute-start(bf16[4,192,256]{2,1,0:T(8,128)(2,1)S(1)} %collective-permute-done.5.g10_ref), channel_id=1, source_target_pairs={{0,1},{1,0},{2,3},{3,2},{4,5},{5,4},{6,7},{7,6},{8,9},{9,8},{10,11... | collective-permute-start | bytes 1179656 | tf_op jit(solution)/shard_map/ppermute | solution.py:190
  92.4 18.5 %copy-start = (f32[256,256]{1,0:T(8,128)S(1)}, f32[256,256]{1,0:T(8,128)}, u32[]{:S(2)}) copy-start(f32[256,256]{1,0:T(8,128)} %get-tuple-element.2.own_ref) | copy-start | bytes 786436
  92.4 18.4 %all-to-all-start.2 = ((bf16[4,256,256]{2,1,0:T(8,128)(2,1)}), bf16[4,256,256]{2,1,0:T(8,128)(2,1)S(1)}, u32[]{:S(2)}, u32[]{:S(2)}) async-start(bf16[4,256,256]{2,1,0:T(8,128)(2,1)} %get-tuple-element.5), calls=%async_computation.2 | async-start | bytes 1048576 | tf_op jit(solution)/shard_map/all_to_all | solution.py:194

commit v10 on v8

--- a/solution.py
+++ b/solution.py
@@ -184,17 +184,17 @@
     grads = jnp.pad(jnp.transpose(grad_rows).reshape(2, BLOCK, tokens), ((0, 0), (0, PADDED - BLOCK), (0, 0)))
     grads = grads.reshape(2 * PADDED, tokens)
     turn = [(a * nz + half * b + c, b * nz + half * a + c) for a in range(nx) for b in range(nx) for c in range(half)]
-    grads = lax.ppermute(grads, ("x", "z"), turn)
+    home = lax.ppermute(grads, ("x", "z"), turn)
+    far = lax.ppermute(grads, ("x", "z"), [(i, j ^ 4) for i, j in turn])
 
     mine = lax.dynamic_slice(keys_values, (core * TILE, lax.axis_index("z") * (2 * DH)), (TILE, 2 * DH))
     own = everyone(mine, "y", ny)
     own = everyone(own, "x", nx).reshape(nx * ny, TILE, 2 * DH)
     other = lax.ppermute(own, "core", swap)
 
-    g_own = grads[None]
-    for bit in (4, 2):
-        came = lax.ppermute(g_own, "z", [(i, i ^ bit) for i in range(nz)])
-        g_own = jnp.concatenate([g_own, came], axis=0)
+    g_own = jnp.stack([home, far])
+    came = lax.ppermute(g_own, "z", [(i, i ^ 2) for i in range(nz)])
+    g_own = jnp.concatenate([g_own, came], axis=0)
     g_next = lax.ppermute(g_own, "z", [(i, i ^ 1) for i in range(nz)])
     g_other = lax.ppermute(g_own, "core", swap)
     g_both = lax.ppermute(g_next, "core", swap)

time: 129 us -> 124 us (0.961)
  starting transfers between devices: 44.8 us -> 40.8 us
    ppermute x3, starting transfers between devices: 25.7 us -> 18 us  [the longest x1 11.3 us: on_device(): far = lax.ppermute(grads, ('x', 'z'), [(i, j ^ 4) for i, j in turn])]
    all_to_all x1, starting transfers between devices: 3.53 us -> 8.49 us  [on_device(): gathered = lax.all_to_all(send, 'x', 0, 0)]
    ppermute x1, starting transfers between devices: 5.84 us -> 3.75 us  [on_device(): g_next = lax.ppermute(g_own, 'z', [(i, i ^ 1) for i in range(nz)])]
where the time goes in v10:
time: 124 us
  starting transfers between devices  40.8 us (33%)
  blocking collectives  36.4 us (29%)
  waiting for transfers between devices  36.1 us (29%)
  Pallas kernels  7.33 us (6%)
    all_to_all x2, blocking collectives, everyone(): lax.all_to_all(jnp.broadcast_to(x[None], (size,) + x.shape), axes, 0, 0)  36.4 us
    all_to_all x1, waiting for transfers between devices, on_device(): parts = lax.all_to_all(term.reshape(ny, PADDED, -1), 'y', 0, 0)  13.5 us
    ppermute x1, starting transfers between devices, on_device(): far = lax.ppermute(grads, ('x', 'z'), [(i, j ^ 4) for i, j in turn])  11.3 us
    all_to_all x1, waiting for transfers between devices, on_device(): gathered = lax.all_to_all(send, 'x', 0, 0)  9.33 us
    all_to_all x1, starting transfers between devices, on_device(): gathered = lax.all_to_all(send, 'x', 0, 0)  8.49 us
    ppermute x1, waiting for transfers between devices, on_device(): far = lax.ppermute(grads, ('x', 'z'), [(i, j ^ 4) for i, j in turn])  6.11 us
    ppermute x1, starting transfers between devices, on_device(): came = lax.ppermute(g_own, 'z', [(i, i ^ 2) for i in range(nz)])  6.09 us
    ppermute x1, waiting for transfers between devices, on_device(): came = lax.ppermute(g_own, 'z', [(i, i ^ 2) for i in range(nz)])  5.97 us
  transfers between devices with their start and end apart: 9, of which 5 were waited for; matrix products, arithmetic and copies ran while one was open for 0% of the time, Pallas kernels for 4%

profile of v10, /device:TPU:64, one launch (start us, length us, event | category | flops | bytes accessed | tf_op | source)
XLA Modules:
  0.0 123.6 jit_solution(13773137524402291059)
XLA Ops:
  0.6 0.0 dynamic-slice-start
  0.7 0.7 dynamic-slice-done
  1.4 18.8 %all_to_all.20 = bf16[8,128,128]{2,1,0:T(8,128)(2,1)S(1)} all-to-all(bf16[8,128,128]{2,1,0:T(8,128)(2,1)S(1)} %broadcast_in_dim.7), channel_id=1, replica_groups=mesh['x'=4,'y'=8,'z'=8,'core'=2] {'y'}, dimensions={0} | all-to-all | bytes 524288 | tf_op jit(solution)/shard_map/all_to_all | solution.py:173
  20.2 0.2 broadcast_in_dim.8
  20.5 0.0 copy-start.3
  20.5 17.7 %all_to_all.21 = bf16[4,8,128,128]{3,2,1,0:T(8,128)(2,1)S(1)} all-to-all(bf16[4,8,128,128]{3,2,1,0:T(8,128)(2,1)S(1)} %broadcast_in_dim.8), channel_id=1, replica_groups=mesh['x'=4,'y'=8,'z'=8,'core'=2] {'x'}, dimensions={0} | all-to-all | bytes 2097152 | tf_op jit(solution)/shard_map/all_to_all | solution.py:173
  38.1 1.9 %collective-permute-start = (bf16[32,128,128]{2,1,0:T(8,128)(2,1)S(1)}, bf16[32,128,128]{2,1,0:T(8,128)(2,1)S(1)}, u32[]{:S(2)}, u32[]{:S(2)}) collective-permute-start(bf16[32,128,128]{2,1,0:T(8,128)(2,1)S(1)} %bitcast.11), channel_id=1, source_target_pairs={{0,1},{1,0},{2,3},{3,2},{4,5},{5,4},{6,7},{7,6},{8,9},{9,8},{10,11... | collective-permute-start | bytes 3145736 | tf_op jit(solution)/shard_map/ppermute | solution.py:193
  40.0 0.0 copy-done.3
  40.1 0.7 collective-permute-start.1
  40.8 11.3 %collective-permute-start.2 = (bf16[192,256]{1,0:T(8,128)(2,1)S(1)}, bf16[192,256]{1,0:T(8,128)(2,1)S(1)}, u32[]{:S(2)}, u32[]{:S(2)}) collective-permute-start(bf16[192,256]{1,0:T(8,128)(2,1)S(1)} %bitcast.19), channel_id=1, source_target_pairs={{0,8},{2,10},{4,136},{6,138},{8,264},{10,266},{12,392},{14,394},{1... | collective-permute-start | bytes 294920 | tf_op jit(solution)/shard_map/ppermute | solution.py:188
  52.1 0.0 collective-permute-done.1
  52.1 6.1 %collective-permute-done.2 = bf16[192,256]{1,0:T(8,128)(2,1)S(1)} collective-permute-done((bf16[192,256]{1,0:T(8,128)(2,1)S(1)}, bf16[192,256]{1,0:T(8,128)(2,1)S(1)}, u32[]{:S(2)}, u32[]{:S(2)}) %collective-permute-start.2) | collective-permute-done | bytes 98336 | tf_op jit(solution)/shard_map/ppermute | solution.py:188
  58.2 6.1 %collective-permute-start.3 = (bf16[2,192,256]{2,1,0:T(8,128)(2,1)S(1)}, bf16[2,192,256]{2,1,0:T(8,128)(2,1)S(1)}, u32[]{:S(2)}, u32[]{:S(2)}) collective-permute-start(bf16[2,192,256]{2,1,0:T(8,128)(2,1)S(1)} %pad_maximum_fusion.1), channel_id=1, source_target_pairs={{0,4},{2,6},{4,0},{6,2},{8,12},{10,14},{12,8},{14,10},{1,5},{3,7},... | collective-permute-start | bytes 589832 | tf_op jit(solution)/shard_map/ppermute | solution.py:196
  64.3 0.1 pad_add_fusion.place_ref
  64.4 6.0 %collective-permute-done.3 = bf16[2,192,256]{2,1,0:T(8,128)(2,1)S(1)} collective-permute-done((bf16[2,192,256]{2,1,0:T(8,128)(2,1)S(1)}, bf16[2,192,256]{2,1,0:T(8,128)(2,1)S(1)}, u32[]{:S(2)}, u32[]{:S(2)}) %collective-permute-start.3) | collective-permute-done | bytes 196640 | tf_op jit(solution)/shard_map/ppermute | solution.py:196
  70.4 0.0 copy-start.2
  70.4 3.7 %collective-permute-start.5 = (bf16[4,192,256]{2,1,0:T(8,128)(2,1)S(1)}, bf16[4,192,256]{2,1,0:T(8,128)(2,1)S(1)}, u32[]{:S(2)}, u32[]{:S(2)}) collective-permute-start(bf16[4,192,256]{2,1,0:T(8,128)(2,1)S(1)} %pad_maximum_fusion.g00_ref), channel_id=1, source_target_pairs={{0,2},{2,0},{4,6},{6,4},{8,10},{10,8},{12,14},{14,12},{1,3},{3,1},... | collective-permute-start | bytes 1179656 | tf_op jit(solution)/shard_map/ppermute | solution.py:198
  74.2 0.0 collective-permute-done.other_ref
  74.2 4.8 %shard_map.68 = (f32[256,256]{1,0:T(8,128)}, f32[4,256,256]{2,1,0:T(8,128)}) custom-call(s32[2]{0:T(128)S(1)} %pad_add_fusion.place_ref, s32[64]{0:T(128)S(1)} %copy-done.2, s32[64,128]{1,0:T(8,128)S(1)} %bitcast.13, bf16[256,256]{1,0:T(8,128)(2,1)S(1)} %copy-done, bf16[32,128,128]{2,1,0:T(8,128)(2,1)S(1)} %bitcast.12, ...), custom_call_target="tpu_custom_call" | custom-call | flops 1200000000 | bytes 4000000 | tf_op jit(solution)/shard_map/pallas_call | solution.py:110
  79.0 8.5 %all-to-all-start.2 = ((f32[4,256,256]{2,1,0:T(8,128)}), f32[4,256,256]{2,1,0:T(8,128)S(1)}, u32[]{:S(2)}, u32[]{:S(2)}) async-start(f32[4,256,256]{2,1,0:T(8,128)} %get-tuple-element.7), calls=%async_computation.2 | async-start | bytes 2097152 | tf_op jit(solution)/shard_map/all_to_all | solution.py:204
  87.5 1.9 %collective-permute-start.4 = (bf16[4,192,256]{2,1,0:T(8,128)(2,1)S(1)}, bf16[4,192,256]{2,1,0:T(8,128)(2,1)S(1)}, u32[]{:S(2)}, u32[]{:S(2)}) collective-permute-start(bf16[4,192,256]{2,1,0:T(8,128)(2,1)S(1)} %pad_maximum_fusion.g00_ref), channel_id=1, source_target_pairs={{0,1},{1,0},{2,3},{3,2},{4,5},{5,4},{6,7},{7,6},{8,9},{9,8},{10,11... | collective-permute-start | bytes 1179656 | tf_op jit(solution)/shard_map/ppermute | solution.py:199
  89.4 0.0 collective-permute-done.5.g10_ref
  89.4 2.4 %collective-permute-start.6 = (bf16[4,192,256]{2,1,0:T(8,128)(2,1)S(1)}, bf16[4,192,256]{2,1,0:T(8,128)(2,1)S(1)}, u32[]{:S(2)}, u32[]{:S(2)}) collective-permute-start(bf16[4,192,256]{2,1,0:T(8,128)(2,1)S(1)} %collective-permute-done.5.g10_ref), channel_id=1, source_target_pairs={{0,1},{1,0},{2,3},{3,2},{4,5},{5,4},{6,7},{7,6},{8,9},{9,8},{10,11... | collective-permute-start | bytes 1179656 | tf_op jit(solution)/shard_map/ppermute | solution.py:200
  91.8 0.1 pad_add_fusion.1.place_ref
  91.9 0.0 collective-permute-done.4.g01_ref
  91.9 1.2 %collective-permute-done.6.g11_ref = bf16[4,192,256]{2,1,0:T(8,128)(2,1)S(1)} collective-permute-done((bf16[4,192,256]{2,1,0:T(8,128)(2,1)S(1)}, bf16[4,192,256]{2,1,0:T(8,128)(2,1)S(1)}, u32[]{:S(2)}, u32[]{:S(2)}) %collective-permute-start.6) | collective-permute-done | bytes 393248 | tf_op jit(solution)/shard_map/ppermute | solution.py:200
  93.1 9.3 %all-to-all-done.2.a_ref = f32[4,256,256]{2,1,0:T(8,128)S(1)} async-done(((f32[4,256,256]{2,1,0:T(8,128)}), f32[4,256,256]{2,1,0:T(8,128)S(1)}, u32[]{:S(2)}, u32[]{:S(2)}) %all-to-all-start.2) | async-done | bytes 1048608 | tf_op jit(solution)/shard_map/all_to_all | solution.py:204
  102.5 2.6 %shard_map.69 = (bf16[4,192,256]{2,1,0:T(8,128)(2,1)}, f32[96,256]{1,0:T(8,128)S(1)}) custom-call(s32[3]{0:T(128)S(1)} %pad_add_fusion.1.place_ref, bf16[4,192,256]{2,1,0:T(8,128)(2,1)S(1)} %pad_maximum_fusion.g00_ref, bf16[4,192,256]{2,1,0:T(8,128)(2,1)S(1)} %collective-permute-done.4.g01_ref, bf16[4,192,256]{2,1,0:T(8,128)(2,1)S(1)} %collective-permute-done.5.g10_ref, ...), custom_call_target="tpu_custom_call" | custom-call | flops 900000000 | bytes 3000000 | tf_op jit(solution)/shard_map/pallas_call | solution.py:154
  105.0 4.3 %all-to-all-start.3 = ((bf16[8,96,256]{2,1,0:T(8,128)(2,1)}), bf16[8,96,256]{2,1,0:T(8,128)(2,1)S(1)}, u32[]{:S(2)}, u32[]{:S(2)}) async-start(bf16[8,96,256]{2,1,0:T(8,128)(2,1)} %bitcast.10), calls=%async_computation.3 | async-start | bytes 786432 | tf_op jit(solution)/shard_map/all_to_all | solution.py:208
  109.3 13.5 %all-to-all-done.3 = bf16[8,96,256]{2,1,0:T(8,128)(2,1)S(1)} async-done(((bf16[8,96,256]{2,1,0:T(8,128)(2,1)}), bf16[8,96,256]{2,1,0:T(8,128)(2,1)S(1)}, u32[]{:S(2)}, u32[]{:S(2)}) %all-to-all-start.3) | async-done | bytes 393248 | tf_op jit(solution)/shard_map/all_to_all | solution.py:208
  122.8 0.1 select_reduce_fusion
  122.9 0.7 slice_add_fusion
  (11 shorter events, 0.1 us)
Async XLA Ops:
  0.6 0.8 dynamic-slice-start
  20.5 19.6 %copy-start.3 = (bf16[256,180]{0,1:T(8,128)(2,1)S(1)}, bf16[256,180]{0,1:T(8,128)(2,1)}, u32[]{:S(2)}) copy-start(bf16[256,180]{0,1:T(8,128)(2,1)} %param.7) | copy-start | bytes 276484
  38.1 36.0 %collective-permute-start = (bf16[32,128,128]{2,1,0:T(8,128)(2,1)S(1)}, bf16[32,128,128]{2,1,0:T(8,128)(2,1)S(1)}, u32[]{:S(2)}, u32[]{:S(2)}) collective-permute-start(bf16[32,128,128]{2,1,0:T(8,128)(2,1)S(1)} %bitcast.11), channel_id=1, source_target_pairs={{0,1},{1,0},{2,3},{3,2},{4,5},{5,4},{6,7},{7,6},{8,9},{9,8},{10,11... | collective-permute-start | bytes 3145736 | tf_op jit(solution)/shard_map/ppermute | solution.py:193
  40.1 12.0 %collective-permute-start.1 = (bf16[192,256]{1,0:T(8,128)(2,1)S(1)}, bf16[192,256]{1,0:T(8,128)(2,1)S(1)}, u32[]{:S(2)}, u32[]{:S(2)}) collective-permute-start(bf16[192,256]{1,0:T(8,128)(2,1)S(1)} %bitcast.18), channel_id=1, source_target_pairs={{0,0},{2,2},{4,128},{6,130},{8,256},{10,258},{12,384},{14,386},{12... | collective-permute-start | bytes 294920 | tf_op jit(solution)/shard_map/ppermute | solution.py:187
  40.8 17.4 %collective-permute-start.2 = (bf16[192,256]{1,0:T(8,128)(2,1)S(1)}, bf16[192,256]{1,0:T(8,128)(2,1)S(1)}, u32[]{:S(2)}, u32[]{:S(2)}) collective-permute-start(bf16[192,256]{1,0:T(8,128)(2,1)S(1)} %bitcast.19), channel_id=1, source_target_pairs={{0,8},{2,10},{4,136},{6,138},{8,264},{10,266},{12,392},{14,394},{1... | collective-permute-start | bytes 294920 | tf_op jit(solution)/shard_map/ppermute | solution.py:188
  58.2 12.2 %collective-permute-start.3 = (bf16[2,192,256]{2,1,0:T(8,128)(2,1)S(1)}, bf16[2,192,256]{2,1,0:T(8,128)(2,1)S(1)}, u32[]{:S(2)}, u32[]{:S(2)}) collective-permute-start(bf16[2,192,256]{2,1,0:T(8,128)(2,1)S(1)} %pad_maximum_fusion.1), channel_id=1, source_target_pairs={{0,4},{2,6},{4,0},{6,2},{8,12},{10,14},{12,8},{14,10},{1,5},{3,7},... | collective-permute-start | bytes 589832 | tf_op jit(solution)/shard_map/ppermute | solution.py:196
  64.4 9.8 %copy-start = (bf16[256,256]{1,0:T(8,128)(2,1)S(1)}, bf16[256,256]{1,0:T(8,128)(2,1)}, u32[]{:S(2)}) copy-start(bf16[256,256]{1,0:T(8,128)(2,1)} %q_ref.1) | copy-start | bytes 393220
  64.4 9.8 %copy-start.1 = (s32[8192]{0:T(1024)S(1)}, s32[8192]{0:T(1024)}, u32[]{:S(2)}) copy-start(s32[8192]{0:T(1024)} %param.8) | copy-start | bytes 98308
  70.4 3.8 %copy-start.2 = (s32[64]{0:T(128)S(1)}, s32[64]{0:T(128)}, u32[]{:S(2)}) copy-start(s32[64]{0:T(128)} %tiles_ref.1) | copy-start | bytes 772
  70.4 19.0 %collective-permute-start.5 = (bf16[4,192,256]{2,1,0:T(8,128)(2,1)S(1)}, bf16[4,192,256]{2,1,0:T(8,128)(2,1)S(1)}, u32[]{:S(2)}, u32[]{:S(2)}) collective-permute-start(bf16[4,192,256]{2,1,0:T(8,128)(2,1)S(1)} %pad_maximum_fusion.g00_ref), channel_id=1, source_target_pairs={{0,2},{2,0},{4,6},{6,4},{8,10},{10,8},{12,14},{14,12},{1,3},{3,1},... | collective-permute-start | bytes 1179656 | tf_op jit(solution)/shard_map/ppermute | solution.py:198
  79.0 23.5 %all-to-all-start.2 = ((f32[4,256,256]{2,1,0:T(8,128)}), f32[4,256,256]{2,1,0:T(8,128)S(1)}, u32[]{:S(2)}, u32[]{:S(2)}) async-start(f32[4,256,256]{2,1,0:T(8,128)} %get-tuple-element.7), calls=%async_computation.2 | async-start | bytes 2097152 | tf_op jit(solution)/shard_map/all_to_all | solution.py:204
  87.5 4.4 %collective-permute-start.4 = (bf16[4,192,256]{2,1,0:T(8,128)(2,1)S(1)}, bf16[4,192,256]{2,1,0:T(8,128)(2,1)S(1)}, u32[]{:S(2)}, u32[]{:S(2)}) collective-permute-start(bf16[4,192,256]{2,1,0:T(8,128)(2,1)S(1)} %pad_maximum_fusion.g00_ref), channel_id=1, source_target_pairs={{0,1},{1,0},{2,3},{3,2},{4,5},{5,4},{6,7},{7,6},{8,9},{9,8},{10,11... | collective-permute-start | bytes 1179656 | tf_op jit(solution)/shard_map/ppermute | solution.py:199
  89.4 3.7 %collective-permute-start.6 = (bf16[4,192,256]{2,1,0:T(8,128)(2,1)S(1)}, bf16[4,192,256]{2,1,0:T(8,128)(2,1)S(1)}, u32[]{:S(2)}, u32[]{:S(2)}) collective-permute-start(bf16[4,192,256]{2,1,0:T(8,128)(2,1)S(1)} %collective-permute-done.5.g10_ref), channel_id=1, source_target_pairs={{0,1},{1,0},{2,3},{3,2},{4,5},{5,4},{6,7},{7,6},{8,9},{9,8},{10,11... | collective-permute-start | bytes 1179656 | tf_op jit(solution)/shard_map/ppermute | solution.py:200
  105.0 17.7 %all-to-all-start.3 = ((bf16[8,96,256]{2,1,0:T(8,128)(2,1)}), bf16[8,96,256]{2,1,0:T(8,128)(2,1)S(1)}, u32[]{:S(2)}, u32[]{:S(2)}) async-start(bf16[8,96,256]{2,1,0:T(8,128)(2,1)} %bitcast.10), calls=%async_computation.3 | async-start | bytes 786432 | tf_op jit(solution)/shard_map/all_to_all | solution.py:208

commit v11 on v10

--- a/solution.py
+++ b/solution.py
@@ -57,8 +57,7 @@
             at = low + 2 * pair
             kv = jnp.concatenate([pick(at), pick(jnp.minimum(at + 1, tile))], axis=0)
             scores = jnp.dot(kv, q_t, preferred_element_type=jnp.float32)
-            key_pos = at * TILE + sub
-            allowed = (key_pos >= row_begin) & (key_pos <= row_pos)
+            allowed = (sub >= row_begin - at * TILE) & (sub <= row_pos - at * TILE)
             start = pl.multiple_of(pair * (2 * TILE), 2 * TILE)
             tops = []
             for h in range(HEADS):
@@ -206,8 +205,9 @@
     place = jnp.stack([core, lax.axis_index("z"), y])
     term, mine = term_of(place, (g_own, g_other, g_next, g_both), gathered)
     parts = lax.all_to_all(term.reshape(ny, PADDED, -1), "y", 0, 0)
+    parts = parts[:, :BLOCK]
     others = lax.broadcasted_iota(jnp.int32, parts.shape, 0) != y
-    weight_grad = (mine + jnp.sum(jnp.where(others, parts.astype(jnp.float32), 0.0), axis=0))[:BLOCK]
+    weight_grad = mine[:BLOCK] + jnp.sum(jnp.where(others, parts.astype(jnp.float32), 0.0), axis=0)
     return attended, weight_grad
 
 

time: 124 us -> 124 us (level)
  no operation moved by 1% of the time
where the time goes in v11:
time: 124 us
  starting transfers between devices  40.8 us (33%)
  blocking collectives  36.4 us (29%)
  waiting for transfers between devices  36.1 us (29%)
  Pallas kernels  7.32 us (6%)
    all_to_all x2, blocking collectives, everyone(): lax.all_to_all(jnp.broadcast_to(x[None], (size,) + x.shape), axes, 0, 0)  36.4 us
    all_to_all x1, waiting for transfers between devices, on_device(): parts = lax.all_to_all(term.reshape(ny, PADDED, -1), 'y', 0, 0)  13.5 us
    ppermute x1, starting transfers between devices, on_device(): far = lax.ppermute(grads, ('x', 'z'), [(i, j ^ 4) for i, j in turn])  11.3 us
    all_to_all x1, waiting for transfers between devices, on_device(): gathered = lax.all_to_all(send, 'x', 0, 0)  9.34 us
    all_to_all x1, starting transfers between devices, on_device(): gathered = lax.all_to_all(send, 'x', 0, 0)  8.49 us
    ppermute x1, waiting for transfers between devices, on_device(): far = lax.ppermute(grads, ('x', 'z'), [(i, j ^ 4) for i, j in turn])  6.11 us
    ppermute x1, starting transfers between devices, on_device(): came = lax.ppermute(g_own, 'z', [(i, i ^ 2) for i in range(nz)])  6.09 us
    ppermute x1, waiting for transfers between devices, on_device(): came = lax.ppermute(g_own, 'z', [(i, i ^ 2) for i in range(nz)])  5.97 us
  transfers between devices with their start and end apart: 9, of which 5 were waited for; matrix products, arithmetic and copies ran while one was open for 0% of the time, Pallas kernels for 4%

profile of v11, /device:TPU:64, one launch (start us, length us, event | category | flops | bytes accessed | tf_op | source)
XLA Modules:
  0.0 123.6 jit_solution(2922515559522808827)
XLA Ops:
  0.6 0.0 dynamic-slice-start
  0.7 0.7 dynamic-slice-done
  1.4 18.8 %all_to_all.20 = bf16[8,128,128]{2,1,0:T(8,128)(2,1)S(1)} all-to-all(bf16[8,128,128]{2,1,0:T(8,128)(2,1)S(1)} %broadcast_in_dim.7), channel_id=1, replica_groups=mesh['x'=4,'y'=8,'z'=8,'core'=2] {'y'}, dimensions={0} | all-to-all | bytes 524288 | tf_op jit(solution)/shard_map/all_to_all | solution.py:172
  20.2 0.2 broadcast_in_dim.8
  20.5 0.0 copy-start.3
  20.5 17.7 %all_to_all.21 = bf16[4,8,128,128]{3,2,1,0:T(8,128)(2,1)S(1)} all-to-all(bf16[4,8,128,128]{3,2,1,0:T(8,128)(2,1)S(1)} %broadcast_in_dim.8), channel_id=1, replica_groups=mesh['x'=4,'y'=8,'z'=8,'core'=2] {'x'}, dimensions={0} | all-to-all | bytes 2097152 | tf_op jit(solution)/shard_map/all_to_all | solution.py:172
  38.1 1.9 %collective-permute-start = (bf16[32,128,128]{2,1,0:T(8,128)(2,1)S(1)}, bf16[32,128,128]{2,1,0:T(8,128)(2,1)S(1)}, u32[]{:S(2)}, u32[]{:S(2)}) collective-permute-start(bf16[32,128,128]{2,1,0:T(8,128)(2,1)S(1)} %bitcast.11), channel_id=1, source_target_pairs={{0,1},{1,0},{2,3},{3,2},{4,5},{5,4},{6,7},{7,6},{8,9},{9,8},{10,11... | collective-permute-start | bytes 3145736 | tf_op jit(solution)/shard_map/ppermute | solution.py:192
  40.0 0.0 copy-done.3
  40.1 0.7 collective-permute-start.1
  40.8 11.3 %collective-permute-start.2 = (bf16[192,256]{1,0:T(8,128)(2,1)S(1)}, bf16[192,256]{1,0:T(8,128)(2,1)S(1)}, u32[]{:S(2)}, u32[]{:S(2)}) collective-permute-start(bf16[192,256]{1,0:T(8,128)(2,1)S(1)} %bitcast.19), channel_id=1, source_target_pairs={{0,8},{2,10},{4,136},{6,138},{8,264},{10,266},{12,392},{14,394},{1... | collective-permute-start | bytes 294920 | tf_op jit(solution)/shard_map/ppermute | solution.py:187
  52.1 0.0 collective-permute-done.1
  52.1 6.1 %collective-permute-done.2 = bf16[192,256]{1,0:T(8,128)(2,1)S(1)} collective-permute-done((bf16[192,256]{1,0:T(8,128)(2,1)S(1)}, bf16[192,256]{1,0:T(8,128)(2,1)S(1)}, u32[]{:S(2)}, u32[]{:S(2)}) %collective-permute-start.2) | collective-permute-done | bytes 98336 | tf_op jit(solution)/shard_map/ppermute | solution.py:187
  58.2 6.1 %collective-permute-start.3 = (bf16[2,192,256]{2,1,0:T(8,128)(2,1)S(1)}, bf16[2,192,256]{2,1,0:T(8,128)(2,1)S(1)}, u32[]{:S(2)}, u32[]{:S(2)}) collective-permute-start(bf16[2,192,256]{2,1,0:T(8,128)(2,1)S(1)} %pad_maximum_fusion.1), channel_id=1, source_target_pairs={{0,4},{2,6},{4,0},{6,2},{8,12},{10,14},{12,8},{14,10},{1,5},{3,7},... | collective-permute-start | bytes 589832 | tf_op jit(solution)/shard_map/ppermute | solution.py:195
  64.3 0.1 pad_add_fusion.place_ref
  64.4 6.0 %collective-permute-done.3 = bf16[2,192,256]{2,1,0:T(8,128)(2,1)S(1)} collective-permute-done((bf16[2,192,256]{2,1,0:T(8,128)(2,1)S(1)}, bf16[2,192,256]{2,1,0:T(8,128)(2,1)S(1)}, u32[]{:S(2)}, u32[]{:S(2)}) %collective-permute-start.3) | collective-permute-done | bytes 196640 | tf_op jit(solution)/shard_map/ppermute | solution.py:195
  70.4 0.0 copy-start.2
  70.4 3.7 %collective-permute-start.5 = (bf16[4,192,256]{2,1,0:T(8,128)(2,1)S(1)}, bf16[4,192,256]{2,1,0:T(8,128)(2,1)S(1)}, u32[]{:S(2)}, u32[]{:S(2)}) collective-permute-start(bf16[4,192,256]{2,1,0:T(8,128)(2,1)S(1)} %pad_maximum_fusion.g00_ref), channel_id=1, source_target_pairs={{0,2},{2,0},{4,6},{6,4},{8,10},{10,8},{12,14},{14,12},{1,3},{3,1},... | collective-permute-start | bytes 1179656 | tf_op jit(solution)/shard_map/ppermute | solution.py:197
  74.2 0.0 collective-permute-done.other_ref
  74.2 4.8 %shard_map.68 = (f32[256,256]{1,0:T(8,128)}, f32[4,256,256]{2,1,0:T(8,128)}) custom-call(s32[2]{0:T(128)S(1)} %pad_add_fusion.place_ref, s32[64]{0:T(128)S(1)} %copy-done.2, s32[64,128]{1,0:T(8,128)S(1)} %bitcast.13, bf16[256,256]{1,0:T(8,128)(2,1)S(1)} %copy-done, bf16[32,128,128]{2,1,0:T(8,128)(2,1)S(1)} %bitcast.12, ...), custom_call_target="tpu_custom_call" | custom-call | flops 1200000000 | bytes 4000000 | tf_op jit(solution)/shard_map/pallas_call | solution.py:109
  79.0 8.5 %all-to-all-start.2 = ((f32[4,256,256]{2,1,0:T(8,128)}), f32[4,256,256]{2,1,0:T(8,128)S(1)}, u32[]{:S(2)}, u32[]{:S(2)}) async-start(f32[4,256,256]{2,1,0:T(8,128)} %get-tuple-element.7), calls=%async_computation.2 | async-start | bytes 2097152 | tf_op jit(solution)/shard_map/all_to_all | solution.py:203
  87.5 1.9 %collective-permute-start.4 = (bf16[4,192,256]{2,1,0:T(8,128)(2,1)S(1)}, bf16[4,192,256]{2,1,0:T(8,128)(2,1)S(1)}, u32[]{:S(2)}, u32[]{:S(2)}) collective-permute-start(bf16[4,192,256]{2,1,0:T(8,128)(2,1)S(1)} %pad_maximum_fusion.g00_ref), channel_id=1, source_target_pairs={{0,1},{1,0},{2,3},{3,2},{4,5},{5,4},{6,7},{7,6},{8,9},{9,8},{10,11... | collective-permute-start | bytes 1179656 | tf_op jit(solution)/shard_map/ppermute | solution.py:198
  89.4 0.0 collective-permute-done.5.g10_ref
  89.4 2.4 %collective-permute-start.6 = (bf16[4,192,256]{2,1,0:T(8,128)(2,1)S(1)}, bf16[4,192,256]{2,1,0:T(8,128)(2,1)S(1)}, u32[]{:S(2)}, u32[]{:S(2)}) collective-permute-start(bf16[4,192,256]{2,1,0:T(8,128)(2,1)S(1)} %collective-permute-done.5.g10_ref), channel_id=1, source_target_pairs={{0,1},{1,0},{2,3},{3,2},{4,5},{5,4},{6,7},{7,6},{8,9},{9,8},{10,11... | collective-permute-start | bytes 1179656 | tf_op jit(solution)/shard_map/ppermute | solution.py:199
  91.8 0.1 pad_add_fusion.1.place_ref
  91.9 0.0 collective-permute-done.4.g01_ref
  91.9 1.2 %collective-permute-done.6.g11_ref = bf16[4,192,256]{2,1,0:T(8,128)(2,1)S(1)} collective-permute-done((bf16[4,192,256]{2,1,0:T(8,128)(2,1)S(1)}, bf16[4,192,256]{2,1,0:T(8,128)(2,1)S(1)}, u32[]{:S(2)}, u32[]{:S(2)}) %collective-permute-start.6) | collective-permute-done | bytes 393248 | tf_op jit(solution)/shard_map/ppermute | solution.py:199
  93.1 9.3 %all-to-all-done.2.a_ref = f32[4,256,256]{2,1,0:T(8,128)S(1)} async-done(((f32[4,256,256]{2,1,0:T(8,128)}), f32[4,256,256]{2,1,0:T(8,128)S(1)}, u32[]{:S(2)}, u32[]{:S(2)}) %all-to-all-start.2) | async-done | bytes 1048608 | tf_op jit(solution)/shard_map/all_to_all | solution.py:203
  102.5 2.6 %shard_map.69 = (bf16[4,192,256]{2,1,0:T(8,128)(2,1)}, f32[96,256]{1,0:T(8,128)S(1)}) custom-call(s32[3]{0:T(128)S(1)} %pad_add_fusion.1.place_ref, bf16[4,192,256]{2,1,0:T(8,128)(2,1)S(1)} %pad_maximum_fusion.g00_ref, bf16[4,192,256]{2,1,0:T(8,128)(2,1)S(1)} %collective-permute-done.4.g01_ref, bf16[4,192,256]{2,1,0:T(8,128)(2,1)S(1)} %collective-permute-done.5.g10_ref, ...), custom_call_target="tpu_custom_call" | custom-call | flops 900000000 | bytes 3000000 | tf_op jit(solution)/shard_map/pallas_call | solution.py:153
  105.0 4.3 %all-to-all-start.3 = ((bf16[8,96,256]{2,1,0:T(8,128)(2,1)}), bf16[8,96,256]{2,1,0:T(8,128)(2,1)S(1)}, u32[]{:S(2)}, u32[]{:S(2)}) async-start(bf16[8,96,256]{2,1,0:T(8,128)(2,1)} %bitcast.10), calls=%async_computation.3 | async-start | bytes 786432 | tf_op jit(solution)/shard_map/all_to_all | solution.py:207
  109.3 13.5 %all-to-all-done.3 = bf16[8,96,256]{2,1,0:T(8,128)(2,1)S(1)} async-done(((bf16[8,96,256]{2,1,0:T(8,128)(2,1)}), bf16[8,96,256]{2,1,0:T(8,128)(2,1)S(1)}, u32[]{:S(2)}, u32[]{:S(2)}) %all-to-all-start.3) | async-done | bytes 393248 | tf_op jit(solution)/shard_map/all_to_all | solution.py:207
  122.8 0.1 select_reduce_fusion
  123.0 0.7 slice_add_fusion
  (11 shorter events, 0.1 us)
Async XLA Ops:
  0.6 0.8 dynamic-slice-start
  20.5 19.6 %copy-start.3 = (bf16[256,180]{0,1:T(8,128)(2,1)S(1)}, bf16[256,180]{0,1:T(8,128)(2,1)}, u32[]{:S(2)}) copy-start(bf16[256,180]{0,1:T(8,128)(2,1)} %param.7) | copy-start | bytes 276484
  38.1 36.0 %collective-permute-start = (bf16[32,128,128]{2,1,0:T(8,128)(2,1)S(1)}, bf16[32,128,128]{2,1,0:T(8,128)(2,1)S(1)}, u32[]{:S(2)}, u32[]{:S(2)}) collective-permute-start(bf16[32,128,128]{2,1,0:T(8,128)(2,1)S(1)} %bitcast.11), channel_id=1, source_target_pairs={{0,1},{1,0},{2,3},{3,2},{4,5},{5,4},{6,7},{7,6},{8,9},{9,8},{10,11... | collective-permute-start | bytes 3145736 | tf_op jit(solution)/shard_map/ppermute | solution.py:192
  40.1 12.0 %collective-permute-start.1 = (bf16[192,256]{1,0:T(8,128)(2,1)S(1)}, bf16[192,256]{1,0:T(8,128)(2,1)S(1)}, u32[]{:S(2)}, u32[]{:S(2)}) collective-permute-start(bf16[192,256]{1,0:T(8,128)(2,1)S(1)} %bitcast.18), channel_id=1, source_target_pairs={{0,0},{2,2},{4,128},{6,130},{8,256},{10,258},{12,384},{14,386},{12... | collective-permute-start | bytes 294920 | tf_op jit(solution)/shard_map/ppermute | solution.py:186
  40.8 17.4 %collective-permute-start.2 = (bf16[192,256]{1,0:T(8,128)(2,1)S(1)}, bf16[192,256]{1,0:T(8,128)(2,1)S(1)}, u32[]{:S(2)}, u32[]{:S(2)}) collective-permute-start(bf16[192,256]{1,0:T(8,128)(2,1)S(1)} %bitcast.19), channel_id=1, source_target_pairs={{0,8},{2,10},{4,136},{6,138},{8,264},{10,266},{12,392},{14,394},{1... | collective-permute-start | bytes 294920 | tf_op jit(solution)/shard_map/ppermute | solution.py:187
  58.2 12.2 %collective-permute-start.3 = (bf16[2,192,256]{2,1,0:T(8,128)(2,1)S(1)}, bf16[2,192,256]{2,1,0:T(8,128)(2,1)S(1)}, u32[]{:S(2)}, u32[]{:S(2)}) collective-permute-start(bf16[2,192,256]{2,1,0:T(8,128)(2,1)S(1)} %pad_maximum_fusion.1), channel_id=1, source_target_pairs={{0,4},{2,6},{4,0},{6,2},{8,12},{10,14},{12,8},{14,10},{1,5},{3,7},... | collective-permute-start | bytes 589832 | tf_op jit(solution)/shard_map/ppermute | solution.py:195
  64.4 9.8 %copy-start = (bf16[256,256]{1,0:T(8,128)(2,1)S(1)}, bf16[256,256]{1,0:T(8,128)(2,1)}, u32[]{:S(2)}) copy-start(bf16[256,256]{1,0:T(8,128)(2,1)} %q_ref.1) | copy-start | bytes 393220
  64.4 9.8 %copy-start.1 = (s32[8192]{0:T(1024)S(1)}, s32[8192]{0:T(1024)}, u32[]{:S(2)}) copy-start(s32[8192]{0:T(1024)} %param.8) | copy-start | bytes 98308
  70.4 3.8 %copy-start.2 = (s32[64]{0:T(128)S(1)}, s32[64]{0:T(128)}, u32[]{:S(2)}) copy-start(s32[64]{0:T(128)} %tiles_ref.1) | copy-start | bytes 772
  70.4 19.0 %collective-permute-start.5 = (bf16[4,192,256]{2,1,0:T(8,128)(2,1)S(1)}, bf16[4,192,256]{2,1,0:T(8,128)(2,1)S(1)}, u32[]{:S(2)}, u32[]{:S(2)}) collective-permute-start(bf16[4,192,256]{2,1,0:T(8,128)(2,1)S(1)} %pad_maximum_fusion.g00_ref), channel_id=1, source_target_pairs={{0,2},{2,0},{4,6},{6,4},{8,10},{10,8},{12,14},{14,12},{1,3},{3,1},... | collective-permute-start | bytes 1179656 | tf_op jit(solution)/shard_map/ppermute | solution.py:197
  79.0 23.5 %all-to-all-start.2 = ((f32[4,256,256]{2,1,0:T(8,128)}), f32[4,256,256]{2,1,0:T(8,128)S(1)}, u32[]{:S(2)}, u32[]{:S(2)}) async-start(f32[4,256,256]{2,1,0:T(8,128)} %get-tuple-element.7), calls=%async_computation.2 | async-start | bytes 2097152 | tf_op jit(solution)/shard_map/all_to_all | solution.py:203
  87.5 4.4 %collective-permute-start.4 = (bf16[4,192,256]{2,1,0:T(8,128)(2,1)S(1)}, bf16[4,192,256]{2,1,0:T(8,128)(2,1)S(1)}, u32[]{:S(2)}, u32[]{:S(2)}) collective-permute-start(bf16[4,192,256]{2,1,0:T(8,128)(2,1)S(1)} %pad_maximum_fusion.g00_ref), channel_id=1, source_target_pairs={{0,1},{1,0},{2,3},{3,2},{4,5},{5,4},{6,7},{7,6},{8,9},{9,8},{10,11... | collective-permute-start | bytes 1179656 | tf_op jit(solution)/shard_map/ppermute | solution.py:198
  89.4 3.7 %collective-permute-start.6 = (bf16[4,192,256]{2,1,0:T(8,128)(2,1)S(1)}, bf16[4,192,256]{2,1,0:T(8,128)(2,1)S(1)}, u32[]{:S(2)}, u32[]{:S(2)}) collective-permute-start(bf16[4,192,256]{2,1,0:T(8,128)(2,1)S(1)} %collective-permute-done.5.g10_ref), channel_id=1, source_target_pairs={{0,1},{1,0},{2,3},{3,2},{4,5},{5,4},{6,7},{7,6},{8,9},{9,8},{10,11... | collective-permute-start | bytes 1179656 | tf_op jit(solution)/shard_map/ppermute | solution.py:199
  105.0 17.8 %all-to-all-start.3 = ((bf16[8,96,256]{2,1,0:T(8,128)(2,1)}), bf16[8,96,256]{2,1,0:T(8,128)(2,1)S(1)}, u32[]{:S(2)}, u32[]{:S(2)}) async-start(bf16[8,96,256]{2,1,0:T(8,128)(2,1)} %bitcast.10), calls=%async_computation.3 | async-start | bytes 786432 | tf_op jit(solution)/shard_map/all_to_all | solution.py:207
